TPU v7x, 32 devices: a whole 2x2x4 slice. The times are simulated.
32 devices in a mesh: shot: 8 (over z, y), xy: 4 (over x, core).
Axes of the slice: x: 2, y: 2, z: 4, core: 2. Of those that a mesh axis runs over, the one named last changes fastest.
Arguments:
- fwd_prev: float32 [8, 32, 512, 128], P('shot', 'xy'), may hold values from -6 to 6
- fwd_cur: float32 [8, 32, 512, 128], P('shot', 'xy'), may hold values from -6 to 6
- bwd_next: float32 [8, 32, 512, 128], P('shot', 'xy'), may hold values from -6 to 6
- bwd_cur: float32 [8, 32, 512, 128], P('shot', 'xy'), may hold values from -6 to 6
- receiver_data: float32 [8, 7, 32, 512], P('shot', None, 'xy'), may hold values from -12 to 12
- velocity_term: float32 [32, 512, 128], P('xy'), may hold values from 0.05 to 0.25
- anisotropy: float32 [32, 512, 128], P('xy'), may hold values from 0 to 0.3
- wavelet: float32 [8, 7], replicated, may hold values from -16 to 16
- shot_x: int32 [8], replicated, may hold values from 0 to 31
- shot_y: int32 [8], replicated, may hold values from 0 to 511
- aperture: int32 [8, 2], replicated, may hold values from 0 to 3, all different within a row
- snap_steps: int32 [4], replicated, may hold values from 1 to 8, as said below
Outputs:
- image: float32 [32, 512, 128], P('xy', 'shot')
Inputs may be any that keep to these rules, and one draw needn't show every extreme that they name: `snap_steps`: 4 distinct increasing times; the last is 8. `aperture`: each row names 2 distinct tiles.
All inputs are finite; a program needn't handle non-finite values.
Results may differ from a plain program's by a relative error of at most 0.0021.
Values may be sent and summed in bfloat16 or wider, within the bound.
No kernel may reach another device: no remote copies, remote signals or barrier semaphores. Data moves between devices by JAX's collectives and lax.ppermute only.
A program may use at most 128 MiB of HBM per device.

v0:
```python
import jax
import jax.numpy as jnp
from jax import lax
from jax.sharding import PartitionSpec as P


def padded_2(x, sides, width):
    for axis, dim in sides:
        devices, length = (lax.axis_size(axis), x.shape[dim])
        up = [(i, (i + 1) % devices) for i in range(devices - 1)]
        down = [(j, i) for i, j in up]
        last = lax.slice_in_dim(x, length - width, length, axis=dim)
        initial = lax.slice_in_dim(x, 0, width, axis=dim)
        before = lax.ppermute(last, axis, up)
        after = lax.ppermute(initial, axis, down)
        x = jnp.concatenate([before, x, after], axis=dim)
    return x


def passed_along(block, axis, distance):
    devices = range(lax.axis_size(axis))
    route = [((i - distance) % len(devices), i) for i in devices]
    return lax.ppermute(block, axis, route)


def laplace(field, horizontal):
    padded = padded_2(field, (("xy", 0),), 1)
    lateral = padded[2:] + padded[:-2] - 4.0 * field
    side = jnp.pad(field, ((0, 0), (1, 1), (0, 0)))
    lateral = lateral + side[:, 2:] + side[:, :-2]
    deeper = jnp.pad(field, ((0, 0), (0, 0), (1, 1)))
    vertical = deeper[:, :, 2:] + deeper[:, :, :-2] - 2.0 * field
    return horizontal * lateral + vertical


def on_device(
    fwd_prev,
    fwd_cur,
    bwd_next,
    bwd_cur,
    receiver_data,
    velocity_term,
    anisotropy,
    wavelet,
    shot_x,
    shot_y,
    aperture,
    snap_steps,
):
    shot_count = lax.axis_size("shot")
    my_shot = lax.axis_index("shot")
    tile_index = lax.axis_index("xy")
    width = fwd_prev.shape[1]
    depth_cells = fwd_prev.shape[3]
    lateral_cells = fwd_prev.shape[2]
    snap_count = snap_steps.shape[0]
    step_count = wavelet.shape[1] + 1
    half = shot_count // 2
    horizontal = 1.0 + 2.0 * anisotropy
    surface = velocity_term[:, :, 0]
    slots = jnp.arange(snap_count, dtype=jnp.int32)
    shot_ids = jnp.arange(shot_count, dtype=jnp.int32)
    lateral_ids = jnp.arange(lateral_cells, dtype=jnp.int32)

    def record(snaps, field, time):
        is_hit = snap_steps == time
        found = jnp.any(is_hit)
        slot = jnp.sum(jnp.where(is_hit, slots, 0))
        older = lax.dynamic_slice_in_dim(snaps, slot, 1, 0)
        newer = jnp.where(found, field.astype(jnp.bfloat16)[None], older)
        return lax.dynamic_update_slice_in_dim(snaps, newer, slot, 0)

    selected = shot_ids == my_shot
    source_x = jnp.sum(jnp.where(selected, shot_x, 0))
    source_y = jnp.sum(jnp.where(selected, shot_y, 0))
    amplitudes = jnp.sum(jnp.where(selected[:, None], wavelet, 0.0), axis=0)
    cell_x = tile_index * width + jnp.arange(width, dtype=jnp.int32)
    plane = ((cell_x == source_x)[:, None] & (lateral_ids == source_y)[None, :]).astype(jnp.float32)
    source_plane = surface * plane

    def march(before, current, state, visit, source_at):

        def one_step(index, carry):
            before, current, state = carry
            state = visit(state, current, index)
            after = 2.0 * current - before + velocity_term * laplace(current, horizontal)
            after = after.at[:, :, 0].add(source_at(index, False))
            return (current, after, state)

        return lax.fori_loop(0, step_count - 1, one_step, (before, current, state))

    def forward_visit(snaps, field, index):
        return record(snaps, field, index + 1)

    def forward_source(index, widened):
        return source_plane * amplitudes[index]

    empty_snaps = jnp.zeros((snap_count, width, lateral_cells, depth_cells), jnp.bfloat16)
    before, current, snaps = march(
        fwd_prev[0], fwd_cur[0], empty_snaps, forward_visit, forward_source
    )
    snaps = record(snaps, current, step_count)
    later, wave, records = passed_along((bwd_next, bwd_cur, receiver_data), "shot", half)
    later, wave, records = (later[0], wave[0], records[0])

    def correlate(partial_value, field, time):
        is_hit = snap_steps == time
        found = jnp.any(is_hit)
        slot = jnp.sum(jnp.where(is_hit, slots, 0))
        taken = lax.dynamic_index_in_dim(snaps, slot, 0, keepdims=False).astype(jnp.float32)
        return partial_value + jnp.where(found, taken * field, 0.0)

    def backward_visit(partial_value, field, index):
        return correlate(partial_value, field, step_count - index)

    def backward_source(index, widened):
        time = step_count - index
        trace = lax.dynamic_index_in_dim(records, time - 2, 0, keepdims=False)
        return surface * trace

    partial_value = jnp.zeros((width, lateral_cells, depth_cells), jnp.float32)
    later, wave, partial_value = march(later, wave, partial_value, backward_visit, backward_source)
    partial_value = correlate(partial_value, wave, 1)
    image_row = jnp.sum(jnp.where((shot_ids == my_shot)[:, None], aperture, 0), axis=0)
    inside = jnp.any(image_row == tile_index).astype(jnp.float32)
    return lax.psum_scatter(partial_value * inside, "shot", scatter_dimension=1, tiled=True)


def solution(mesh):
    in_specs = (
        P("shot", "xy", None, None),
        P("shot", "xy", None, None),
        P("shot", "xy", None, None),
        P("shot", "xy", None, None),
        P("shot", None, "xy", None),
        P("xy", None, None),
        P("xy", None, None),
        P(),
        P(),
        P(),
        P(),
        P(),
    )
    out_specs = P("xy", "shot", None)
    return jax.shard_map(
        on_device, mesh=mesh, in_specs=in_specs, out_specs=out_specs, check_vma=False
    )
```

profile of v0, /device:TPU:0, one launch (start us, length us, event | category | flops | bytes accessed | tf_op | source)
XLA Modules:
  0.0 548.0 jit_solution(11190581827711602722)
XLA Ops:
  6.5 3.2 copy.14
  9.8 4.1 collective-permute-start.4
  22.0 3.2 copy.24
  40.1 175.9 %while.44 = (s32[]{:T(128)}, f32[8,512,128]{1,0,2:T(8,128)}, f32[8,512,128]{1,0,2:T(8,128)S(1)}, bf16[4,8,512,128]{3,2,1,0:T(8,128)(2,1)}, f32[8,512,128]{1,0,2:...) while((s32[]{:T(128)}, f32[8,512,128]{1,0,2:T(8,128)}, ...), condition=%wide.region_6.7_spmd.clone, body=%wide.region_3.6_spmd.clone.sunk | while | flops 8921111 | bytes 43565388 | solution.py:90
  56.5 4.0 fusion.43
  63.7 4.7 collective-permute-start
  82.5 4.0 fusion.43
  89.7 4.3 collective-permute-start
  108.0 4.0 fusion.43
  115.2 4.3 collective-permute-start
  133.4 4.0 fusion.43
  140.6 4.3 collective-permute-start
  158.9 4.0 fusion.43
  166.2 4.3 collective-permute-start
  184.4 4.0 fusion.43
  191.6 4.3 collective-permute-start
  209.9 4.0 fusion.43
  220.3 3.1 fusion.29
  223.5 237.7 %while.45 = (s32[]{:T(128)}, f32[8,512,128]{1,0,2:T(8,128)}, f32[8,512,128]{1,0,2:T(8,128)}, f32[8,512,128]{1,0,2:T(8,128)}, f32[8,512,128]{1,0,2:T(8,128)}, /*i...) while((s32[]{:T(128)}, f32[8,512,128]{1,0,2:T(8,128)}, ...), condition=%wide.region_12.13_spmd.clone, body=%wide.region_9.12_spmd.clone.sunk | while | flops 10493981 | bytes 32047488 | solution.py:90
  223.5 3.6 fusion.47
  227.0 4.3 collective-permute-start.2
  240.0 12.6 %fusion.48 = (f32[8,512,128]{1,0,2:T(8,128)}, f32[8,512,128]{1,0,2:T(8,128)S(1)}) fusion(f32[8,512,128]{1,0,2:T(8,128)} %get-tuple-element.950, f32[8,512,128]{1,0,2:T(8,128)} %get-tuple-element.951, bf16[1,8,512,128]{2,1,3,0:T(8,128)(2,1)S(1)} %copy.37, pred[]{:T(512)S(6)} %compare.41, pred[]{:T(512)} %compare_reduce_fusion.8, ...), kind=kLoop, calls=%fused_computation.36.clone.1 | loop fusion | flops 10485760 | bytes 16252930 | tf_op jit(solution)/shard_map/while/body/eval_jaxpr/add | solution.py:111
  252.6 3.1 copy.63
  257.2 3.6 fusion.47
  260.7 4.3 collective-permute-start.2
  273.7 13.0 %fusion.48 = (f32[8,512,128]{1,0,2:T(8,128)}, f32[8,512,128]{1,0,2:T(8,128)S(1)}) fusion(f32[8,512,128]{1,0,2:T(8,128)} %get-tuple-element.950, f32[8,512,128]{1,0,2:T(8,128)} %get-tuple-element.951, bf16[1,8,512,128]{2,1,3,0:T(8,128)(2,1)S(1)} %copy.37, pred[]{:T(512)S(6)} %compare.41, pred[]{:T(512)} %compare_reduce_fusion.8, ...), kind=kLoop, calls=%fused_computation.36.clone.1 | loop fusion | flops 10485760 | bytes 16252930 | tf_op jit(solution)/shard_map/while/body/eval_jaxpr/add | solution.py:111
  286.6 3.1 copy.63
  291.2 3.6 fusion.47
  294.7 4.3 collective-permute-start.2
  307.7 13.0 %fusion.48 = (f32[8,512,128]{1,0,2:T(8,128)}, f32[8,512,128]{1,0,2:T(8,128)S(1)}) fusion(f32[8,512,128]{1,0,2:T(8,128)} %get-tuple-element.950, f32[8,512,128]{1,0,2:T(8,128)} %get-tuple-element.951, bf16[1,8,512,128]{2,1,3,0:T(8,128)(2,1)S(1)} %copy.37, pred[]{:T(512)S(6)} %compare.41, pred[]{:T(512)} %compare_reduce_fusion.8, ...), kind=kLoop, calls=%fused_computation.36.clone.1 | loop fusion | flops 10485760 | bytes 16252930 | tf_op jit(solution)/shard_map/while/body/eval_jaxpr/add | solution.py:111
  320.7 3.1 copy.63
  325.2 3.6 fusion.47
  328.7 4.3 collective-permute-start.2
  341.7 13.0 %fusion.48 = (f32[8,512,128]{1,0,2:T(8,128)}, f32[8,512,128]{1,0,2:T(8,128)S(1)}) fusion(f32[8,512,128]{1,0,2:T(8,128)} %get-tuple-element.950, f32[8,512,128]{1,0,2:T(8,128)} %get-tuple-element.951, bf16[1,8,512,128]{2,1,3,0:T(8,128)(2,1)S(1)} %copy.37, pred[]{:T(512)S(6)} %compare.41, pred[]{:T(512)} %compare_reduce_fusion.8, ...), kind=kLoop, calls=%fused_computation.36.clone.1 | loop fusion | flops 10485760 | bytes 16252930 | tf_op jit(solution)/shard_map/while/body/eval_jaxpr/add | solution.py:111
  354.7 3.1 copy.63
  359.2 3.6 fusion.47
  362.7 4.3 collective-permute-start.2
  375.7 13.0 %fusion.48 = (f32[8,512,128]{1,0,2:T(8,128)}, f32[8,512,128]{1,0,2:T(8,128)S(1)}) fusion(f32[8,512,128]{1,0,2:T(8,128)} %get-tuple-element.950, f32[8,512,128]{1,0,2:T(8,128)} %get-tuple-element.951, bf16[1,8,512,128]{2,1,3,0:T(8,128)(2,1)S(1)} %copy.37, pred[]{:T(512)S(6)} %compare.41, pred[]{:T(512)} %compare_reduce_fusion.8, ...), kind=kLoop, calls=%fused_computation.36.clone.1 | loop fusion | flops 10485760 | bytes 16252930 | tf_op jit(solution)/shard_map/while/body/eval_jaxpr/add | solution.py:111
  388.7 3.1 copy.63
  393.2 3.6 fusion.47
  396.7 4.3 collective-permute-start.2
  409.7 13.0 %fusion.48 = (f32[8,512,128]{1,0,2:T(8,128)}, f32[8,512,128]{1,0,2:T(8,128)S(1)}) fusion(f32[8,512,128]{1,0,2:T(8,128)} %get-tuple-element.950, f32[8,512,128]{1,0,2:T(8,128)} %get-tuple-element.951, bf16[1,8,512,128]{2,1,3,0:T(8,128)(2,1)S(1)} %copy.37, pred[]{:T(512)S(6)} %compare.41, pred[]{:T(512)} %compare_reduce_fusion.8, ...), kind=kLoop, calls=%fused_computation.36.clone.1 | loop fusion | flops 10485760 | bytes 16252930 | tf_op jit(solution)/shard_map/while/body/eval_jaxpr/add | solution.py:111
  427.2 3.6 fusion.47
  430.7 4.3 collective-permute-start.2
  443.7 13.0 %fusion.48 = (f32[8,512,128]{1,0,2:T(8,128)}, f32[8,512,128]{1,0,2:T(8,128)S(1)}) fusion(f32[8,512,128]{1,0,2:T(8,128)} %get-tuple-element.950, f32[8,512,128]{1,0,2:T(8,128)} %get-tuple-element.951, bf16[1,8,512,128]{2,1,3,0:T(8,128)(2,1)S(1)} %copy.37, pred[]{:T(512)S(6)} %compare.41, pred[]{:T(512)} %compare_reduce_fusion.8, ...), kind=kLoop, calls=%fused_computation.36.clone.1 | loop fusion | flops 10485760 | bytes 16252930 | tf_op jit(solution)/shard_map/while/body/eval_jaxpr/add | solution.py:111
  461.2 3.1 copy.26
  466.2 4.8 fusion.28
  471.0 70.2 %reduce-scatter.2.cloned.1.call-done = f32[8,64,128]{2,1,0:T(8,128)} async-done(((f32[8,512,128]{2,1,0:T(8,128)}), f32[8,64,128]{2,1,0:T(8,128)}) %reduce-scatter.2.cloned.1.call-update) | async-done | bytes 262160 | tf_op jit(solution)/shard_map/reduce_scatter | solution.py:126
  (228 shorter events, 197.3 us)
Async XLA Ops:
  6.5 7.3 %copy-start.3 = (f32[1,8,512,128]{3,2,1,0:T(8,128)S(1)}, f32[1,8,512,128]{3,2,1,0:T(8,128)}, u32[]{:S(2)}) copy-start(f32[1,8,512,128]{3,2,1,0:T(8,128)} %param.23) | copy-start | bytes 6291460
  6.5 534.6 %reduce-scatter.2.cloned.1.call-start = ((), (), s32[]{:S(2)}) async-start(), calls=%async_computation.1 | async-start | bytes 2359296 | tf_op jit(solution)/shard_map/reduce_scatter | solution.py:126
  9.8 9.0 %copy-start.8 = (s32[4]{0:T(128)S(1)}, s32[4]{0:T(128)}, u32[]{:S(2)}) copy-start(s32[4]{0:T(128)} %param.31) | copy-start | bytes 52
  9.8 213.7 %collective-permute-start.4 = (f32[1,8,512,128]{2,1,3,0:T(8,128)}, f32[1,8,512,128]{2,1,3,0:T(8,128)}, u32[]{:S(2)}, u32[]{:S(2)}) collective-permute-start(f32[1,8,512,128]{2,1,3,0:T(8,128)} %copy.14), channel_id=1, source_target_pairs={{16,0},{20,4},{24,8},{28,12},{0,16},{4,20},{8,24},{12,28},{17,1},{... | collective-permute-start | bytes 6291464 | tf_op jit(solution)/shard_map/ppermute | solution.py:23
  15.8 207.6 %collective-permute-start.5 = (f32[1,8,512,128]{2,1,3,0:T(8,128)}, f32[1,8,512,128]{2,1,3,0:T(8,128)}, u32[]{:S(2)}, u32[]{:S(2)}) collective-permute-start(f32[1,8,512,128]{2,1,3,0:T(8,128)} %copy.15), channel_id=1, source_target_pairs={{16,0},{20,4},{24,8},{28,12},{0,16},{4,20},{8,24},{12,28},{17,1},{... | collective-permute-start | bytes 6291464 | tf_op jit(solution)/shard_map/ppermute | solution.py:23
  15.8 207.6 %collective-permute-start.6 = (f32[1,7,8,512]{3,2,1,0:T(8,128)}, f32[1,7,8,512]{3,2,1,0:T(8,128)S(1)}, u32[]{:S(2)}, u32[]{:S(2)}) collective-permute-start(f32[1,7,8,512]{3,2,1,0:T(8,128)} %param.24), channel_id=1, source_target_pairs={{16,0},{20,4},{24,8},{28,12},{0,16},{4,20},{8,24},{12,28},{17,1},{... | collective-permute-start | bytes 344072 | tf_op jit(solution)/shard_map/ppermute | solution.py:23
  22.0 3.2 copy-start.6
  22.0 3.2 copy-start.7
  33.5 2.9 copy-start.4
  41.2 15.3 %collective-permute-start = (f32[1,512,128]{1,0,2:T(1,128)}, f32[1,512,128]{1,0,2:T(1,128)S(1)}, u32[]{:S(2)}, u32[]{:S(2)}) collective-permute-start(f32[1,512,128]{1,0,2:T(1,128)} %get-tuple-element.880), channel_id=1, source_target_pairs={{0,1},{1,2},{2,3},{4,5},{5,6},{6,7},{8,9},{9,10},{10,11},{12,13},{... | collective-permute-start | bytes 786440 | tf_op jit(solution)/shard_map/while/body/eval_jaxpr/ppermute | solution.py:14
  42.5 14.0 %collective-permute-start.1 = (f32[1,512,128]{1,0,2:T(1,128)}, f32[1,512,128]{1,0,2:T(1,128)}, u32[]{:S(2)}, u32[]{:S(2)}) collective-permute-start(f32[1,512,128]{1,0,2:T(1,128)} %get-tuple-element.881), channel_id=1, source_target_pairs={{1,0},{2,1},{3,2},{5,4},{6,5},{7,6},{9,8},{10,9},{11,10},{13,12},{... | collective-permute-start | bytes 786440 | tf_op jit(solution)/shard_map/while/body/eval_jaxpr/ppermute | solution.py:15
  54.8 1.7 copy-start
  63.7 18.7 %collective-permute-start = (f32[1,512,128]{1,0,2:T(1,128)}, f32[1,512,128]{1,0,2:T(1,128)S(1)}, u32[]{:S(2)}, u32[]{:S(2)}) collective-permute-start(f32[1,512,128]{1,0,2:T(1,128)} %get-tuple-element.880), channel_id=1, source_target_pairs={{0,1},{1,2},{2,3},{4,5},{5,6},{6,7},{8,9},{9,10},{10,11},{12,13},{... | collective-permute-start | bytes 786440 | tf_op jit(solution)/shard_map/while/body/eval_jaxpr/ppermute | solution.py:14
  68.5 14.0 %collective-permute-start.1 = (f32[1,512,128]{1,0,2:T(1,128)}, f32[1,512,128]{1,0,2:T(1,128)}, u32[]{:S(2)}, u32[]{:S(2)}) collective-permute-start(f32[1,512,128]{1,0,2:T(1,128)} %get-tuple-element.881), channel_id=1, source_target_pairs={{1,0},{2,1},{3,2},{5,4},{6,5},{7,6},{9,8},{10,9},{11,10},{13,12},{... | collective-permute-start | bytes 786440 | tf_op jit(solution)/shard_map/while/body/eval_jaxpr/ppermute | solution.py:15
  80.8 1.7 copy-start
  89.7 18.3 %collective-permute-start = (f32[1,512,128]{1,0,2:T(1,128)}, f32[1,512,128]{1,0,2:T(1,128)S(1)}, u32[]{:S(2)}, u32[]{:S(2)}) collective-permute-start(f32[1,512,128]{1,0,2:T(1,128)} %get-tuple-element.880), channel_id=1, source_target_pairs={{0,1},{1,2},{2,3},{4,5},{5,6},{6,7},{8,9},{9,10},{10,11},{12,13},{... | collective-permute-start | bytes 786440 | tf_op jit(solution)/shard_map/while/body/eval_jaxpr/ppermute | solution.py:14
  94.0 14.0 %collective-permute-start.1 = (f32[1,512,128]{1,0,2:T(1,128)}, f32[1,512,128]{1,0,2:T(1,128)}, u32[]{:S(2)}, u32[]{:S(2)}) collective-permute-start(f32[1,512,128]{1,0,2:T(1,128)} %get-tuple-element.881), channel_id=1, source_target_pairs={{1,0},{2,1},{3,2},{5,4},{6,5},{7,6},{9,8},{10,9},{11,10},{13,12},{... | collective-permute-start | bytes 786440 | tf_op jit(solution)/shard_map/while/body/eval_jaxpr/ppermute | solution.py:15
  106.2 1.7 copy-start
  115.2 18.3 %collective-permute-start = (f32[1,512,128]{1,0,2:T(1,128)}, f32[1,512,128]{1,0,2:T(1,128)S(1)}, u32[]{:S(2)}, u32[]{:S(2)}) collective-permute-start(f32[1,512,128]{1,0,2:T(1,128)} %get-tuple-element.880), channel_id=1, source_target_pairs={{0,1},{1,2},{2,3},{4,5},{5,6},{6,7},{8,9},{9,10},{10,11},{12,13},{... | collective-permute-start | bytes 786440 | tf_op jit(solution)/shard_map/while/body/eval_jaxpr/ppermute | solution.py:14
  119.4 14.0 %collective-permute-start.1 = (f32[1,512,128]{1,0,2:T(1,128)}, f32[1,512,128]{1,0,2:T(1,128)}, u32[]{:S(2)}, u32[]{:S(2)}) collective-permute-start(f32[1,512,128]{1,0,2:T(1,128)} %get-tuple-element.881), channel_id=1, source_target_pairs={{1,0},{2,1},{3,2},{5,4},{6,5},{7,6},{9,8},{10,9},{11,10},{13,12},{... | collective-permute-start | bytes 786440 | tf_op jit(solution)/shard_map/while/body/eval_jaxpr/ppermute | solution.py:15
  131.7 1.7 copy-start
  140.6 18.3 %collective-permute-start = (f32[1,512,128]{1,0,2:T(1,128)}, f32[1,512,128]{1,0,2:T(1,128)S(1)}, u32[]{:S(2)}, u32[]{:S(2)}) collective-permute-start(f32[1,512,128]{1,0,2:T(1,128)} %get-tuple-element.880), channel_id=1, source_target_pairs={{0,1},{1,2},{2,3},{4,5},{5,6},{6,7},{8,9},{9,10},{10,11},{12,13},{... | collective-permute-start | bytes 786440 | tf_op jit(solution)/shard_map/while/body/eval_jaxpr/ppermute | solution.py:14
  144.9 14.0 %collective-permute-start.1 = (f32[1,512,128]{1,0,2:T(1,128)}, f32[1,512,128]{1,0,2:T(1,128)}, u32[]{:S(2)}, u32[]{:S(2)}) collective-permute-start(f32[1,512,128]{1,0,2:T(1,128)} %get-tuple-element.881), channel_id=1, source_target_pairs={{1,0},{2,1},{3,2},{5,4},{6,5},{7,6},{9,8},{10,9},{11,10},{13,12},{... | collective-permute-start | bytes 786440 | tf_op jit(solution)/shard_map/while/body/eval_jaxpr/ppermute | solution.py:15
  157.2 1.8 copy-start
  166.2 18.2 %collective-permute-start = (f32[1,512,128]{1,0,2:T(1,128)}, f32[1,512,128]{1,0,2:T(1,128)S(1)}, u32[]{:S(2)}, u32[]{:S(2)}) collective-permute-start(f32[1,512,128]{1,0,2:T(1,128)} %get-tuple-element.880), channel_id=1, source_target_pairs={{0,1},{1,2},{2,3},{4,5},{5,6},{6,7},{8,9},{9,10},{10,11},{12,13},{... | collective-permute-start | bytes 786440 | tf_op jit(solution)/shard_map/while/body/eval_jaxpr/ppermute | solution.py:14
  170.4 14.0 %collective-permute-start.1 = (f32[1,512,128]{1,0,2:T(1,128)}, f32[1,512,128]{1,0,2:T(1,128)}, u32[]{:S(2)}, u32[]{:S(2)}) collective-permute-start(f32[1,512,128]{1,0,2:T(1,128)} %get-tuple-element.881), channel_id=1, source_target_pairs={{1,0},{2,1},{3,2},{5,4},{6,5},{7,6},{9,8},{10,9},{11,10},{13,12},{... | collective-permute-start | bytes 786440 | tf_op jit(solution)/shard_map/while/body/eval_jaxpr/ppermute | solution.py:15
  182.7 1.7 copy-start
  191.6 18.3 %collective-permute-start = (f32[1,512,128]{1,0,2:T(1,128)}, f32[1,512,128]{1,0,2:T(1,128)S(1)}, u32[]{:S(2)}, u32[]{:S(2)}) collective-permute-start(f32[1,512,128]{1,0,2:T(1,128)} %get-tuple-element.880), channel_id=1, source_target_pairs={{0,1},{1,2},{2,3},{4,5},{5,6},{6,7},{8,9},{9,10},{10,11},{12,13},{... | collective-permute-start | bytes 786440 | tf_op jit(solution)/shard_map/while/body/eval_jaxpr/ppermute | solution.py:14
  195.9 14.0 %collective-permute-start.1 = (f32[1,512,128]{1,0,2:T(1,128)}, f32[1,512,128]{1,0,2:T(1,128)}, u32[]{:S(2)}, u32[]{:S(2)}) collective-permute-start(f32[1,512,128]{1,0,2:T(1,128)} %get-tuple-element.881), channel_id=1, source_target_pairs={{1,0},{2,1},{3,2},{5,4},{6,5},{7,6},{9,8},{10,9},{11,10},{13,12},{... | collective-permute-start | bytes 786440 | tf_op jit(solution)/shard_map/while/body/eval_jaxpr/ppermute | solution.py:15
  208.2 1.7 copy-start
  216.0 1.0 copy-start.5
  217.0 6.5 %copy-start.1 = (f32[8,512,128]{1,0,2:T(8,128)S(1)}, f32[8,512,128]{1,0,2:T(8,128)}, u32[]{:S(2)}) copy-start(f32[8,512,128]{1,0,2:T(8,128)} %get-tuple-element.981) | copy-start | bytes 6291460
  227.0 13.0 %collective-permute-start.2 = (f32[1,512,128]{1,0,2:T(1,128)}, f32[1,512,128]{1,0,2:T(1,128)S(1)}, u32[]{:S(2)}, u32[]{:S(2)}) collective-permute-start(f32[1,512,128]{1,0,2:T(1,128)} %get-tuple-element.892), channel_id=1, source_target_pairs={{0,1},{1,2},{2,3},{4,5},{5,6},{6,7},{8,9},{9,10},{10,11},{12,13},{... | collective-permute-start | bytes 786440 | tf_op jit(solution)/shard_map/while/body/eval_jaxpr/ppermute | solution.py:14
  231.3 8.7 %collective-permute-start.3 = (f32[1,512,128]{1,0,2:T(1,128)}, f32[1,512,128]{1,0,2:T(1,128)}, u32[]{:S(2)}, u32[]{:S(2)}) collective-permute-start(f32[1,512,128]{1,0,2:T(1,128)} %get-tuple-element.893), channel_id=1, source_target_pairs={{1,0},{2,1},{3,2},{5,4},{6,5},{7,6},{9,8},{10,9},{11,10},{13,12},{... | collective-permute-start | bytes 786440 | tf_op jit(solution)/shard_map/while/body/eval_jaxpr/ppermute | solution.py:15
  260.7 13.0 %collective-permute-start.2 = (f32[1,512,128]{1,0,2:T(1,128)}, f32[1,512,128]{1,0,2:T(1,128)S(1)}, u32[]{:S(2)}, u32[]{:S(2)}) collective-permute-start(f32[1,512,128]{1,0,2:T(1,128)} %get-tuple-element.892), channel_id=1, source_target_pairs={{0,1},{1,2},{2,3},{4,5},{5,6},{6,7},{8,9},{9,10},{10,11},{12,13},{... | collective-permute-start | bytes 786440 | tf_op jit(solution)/shard_map/while/body/eval_jaxpr/ppermute | solution.py:14
  265.0 8.7 %collective-permute-start.3 = (f32[1,512,128]{1,0,2:T(1,128)}, f32[1,512,128]{1,0,2:T(1,128)}, u32[]{:S(2)}, u32[]{:S(2)}) collective-permute-start(f32[1,512,128]{1,0,2:T(1,128)} %get-tuple-element.893), channel_id=1, source_target_pairs={{1,0},{2,1},{3,2},{5,4},{6,5},{7,6},{9,8},{10,9},{11,10},{13,12},{... | collective-permute-start | bytes 786440 | tf_op jit(solution)/shard_map/while/body/eval_jaxpr/ppermute | solution.py:15
  294.7 13.0 %collective-permute-start.2 = (f32[1,512,128]{1,0,2:T(1,128)}, f32[1,512,128]{1,0,2:T(1,128)S(1)}, u32[]{:S(2)}, u32[]{:S(2)}) collective-permute-start(f32[1,512,128]{1,0,2:T(1,128)} %get-tuple-element.892), channel_id=1, source_target_pairs={{0,1},{1,2},{2,3},{4,5},{5,6},{6,7},{8,9},{9,10},{10,11},{12,13},{... | collective-permute-start | bytes 786440 | tf_op jit(solution)/shard_map/while/body/eval_jaxpr/ppermute | solution.py:14
  299.0 8.7 %collective-permute-start.3 = (f32[1,512,128]{1,0,2:T(1,128)}, f32[1,512,128]{1,0,2:T(1,128)}, u32[]{:S(2)}, u32[]{:S(2)}) collective-permute-start(f32[1,512,128]{1,0,2:T(1,128)} %get-tuple-element.893), channel_id=1, source_target_pairs={{1,0},{2,1},{3,2},{5,4},{6,5},{7,6},{9,8},{10,9},{11,10},{13,12},{... | collective-permute-start | bytes 786440 | tf_op jit(solution)/shard_map/while/body/eval_jaxpr/ppermute | solution.py:15
  328.7 13.0 %collective-permute-start.2 = (f32[1,512,128]{1,0,2:T(1,128)}, f32[1,512,128]{1,0,2:T(1,128)S(1)}, u32[]{:S(2)}, u32[]{:S(2)}) collective-permute-start(f32[1,512,128]{1,0,2:T(1,128)} %get-tuple-element.892), channel_id=1, source_target_pairs={{0,1},{1,2},{2,3},{4,5},{5,6},{6,7},{8,9},{9,10},{10,11},{12,13},{... | collective-permute-start | bytes 786440 | tf_op jit(solution)/shard_map/while/body/eval_jaxpr/ppermute | solution.py:14
  333.0 8.7 %collective-permute-start.3 = (f32[1,512,128]{1,0,2:T(1,128)}, f32[1,512,128]{1,0,2:T(1,128)}, u32[]{:S(2)}, u32[]{:S(2)}) collective-permute-start(f32[1,512,128]{1,0,2:T(1,128)} %get-tuple-element.893), channel_id=1, source_target_pairs={{1,0},{2,1},{3,2},{5,4},{6,5},{7,6},{9,8},{10,9},{11,10},{13,12},{... | collective-permute-start | bytes 786440 | tf_op jit(solution)/shard_map/while/body/eval_jaxpr/ppermute | solution.py:15
  362.7 13.0 %collective-permute-start.2 = (f32[1,512,128]{1,0,2:T(1,128)}, f32[1,512,128]{1,0,2:T(1,128)S(1)}, u32[]{:S(2)}, u32[]{:S(2)}) collective-permute-start(f32[1,512,128]{1,0,2:T(1,128)} %get-tuple-element.892), channel_id=1, source_target_pairs={{0,1},{1,2},{2,3},{4,5},{5,6},{6,7},{8,9},{9,10},{10,11},{12,13},{... | collective-permute-start | bytes 786440 | tf_op jit(solution)/shard_map/while/body/eval_jaxpr/ppermute | solution.py:14
  367.0 8.7 %collective-permute-start.3 = (f32[1,512,128]{1,0,2:T(1,128)}, f32[1,512,128]{1,0,2:T(1,128)}, u32[]{:S(2)}, u32[]{:S(2)}) collective-permute-start(f32[1,512,128]{1,0,2:T(1,128)} %get-tuple-element.893), channel_id=1, source_target_pairs={{1,0},{2,1},{3,2},{5,4},{6,5},{7,6},{9,8},{10,9},{11,10},{13,12},{... | collective-permute-start | bytes 786440 | tf_op jit(solution)/shard_map/while/body/eval_jaxpr/ppermute | solution.py:15
  396.7 13.0 %collective-permute-start.2 = (f32[1,512,128]{1,0,2:T(1,128)}, f32[1,512,128]{1,0,2:T(1,128)S(1)}, u32[]{:S(2)}, u32[]{:S(2)}) collective-permute-start(f32[1,512,128]{1,0,2:T(1,128)} %get-tuple-element.892), channel_id=1, source_target_pairs={{0,1},{1,2},{2,3},{4,5},{5,6},{6,7},{8,9},{9,10},{10,11},{12,13},{... | collective-permute-start | bytes 786440 | tf_op jit(solution)/shard_map/while/body/eval_jaxpr/ppermute | solution.py:14
  401.0 8.7 %collective-permute-start.3 = (f32[1,512,128]{1,0,2:T(1,128)}, f32[1,512,128]{1,0,2:T(1,128)}, u32[]{:S(2)}, u32[]{:S(2)}) collective-permute-start(f32[1,512,128]{1,0,2:T(1,128)} %get-tuple-element.893), channel_id=1, source_target_pairs={{1,0},{2,1},{3,2},{5,4},{6,5},{7,6},{9,8},{10,9},{11,10},{13,12},{... | collective-permute-start | bytes 786440 | tf_op jit(solution)/shard_map/while/body/eval_jaxpr/ppermute | solution.py:15
  430.7 13.0 %collective-permute-start.2 = (f32[1,512,128]{1,0,2:T(1,128)}, f32[1,512,128]{1,0,2:T(1,128)S(1)}, u32[]{:S(2)}, u32[]{:S(2)}) collective-permute-start(f32[1,512,128]{1,0,2:T(1,128)} %get-tuple-element.892), channel_id=1, source_target_pairs={{0,1},{1,2},{2,3},{4,5},{5,6},{6,7},{8,9},{9,10},{10,11},{12,13},{... | collective-permute-start | bytes 786440 | tf_op jit(solution)/shard_map/while/body/eval_jaxpr/ppermute | solution.py:14
  435.0 8.7 %collective-permute-start.3 = (f32[1,512,128]{1,0,2:T(1,128)}, f32[1,512,128]{1,0,2:T(1,128)}, u32[]{:S(2)}, u32[]{:S(2)}) collective-permute-start(f32[1,512,128]{1,0,2:T(1,128)} %get-tuple-element.893), channel_id=1, source_target_pairs={{1,0},{2,1},{3,2},{5,4},{6,5},{7,6},{9,8},{10,9},{11,10},{13,12},{... | collective-permute-start | bytes 786440 | tf_op jit(solution)/shard_map/while/body/eval_jaxpr/ppermute | solution.py:15
  461.2 3.1 copy-start.2
Sparse Core Ops, SparseCore 0:
  471.1 69.9 reduce-scatter.1
where the time goes:
time: 551 us; the launch traced here: 548 us
  local copies, waits for them, and re-layouts  183 us (33%)
  other arithmetic  168 us (30%)
  starting transfers between devices  82.2 us (15%)
  waiting for transfers between devices  70.3 us (13%)
  loops' own time  26.5 us (5%)
  between operations  18 us (3%)
    add x7, other arithmetic, correlate(): return partial_value + jnp.where(found, taken * field, 0.0)  90.5 us
    reduce_scatter x1, waiting for transfers between devices, on_device(): lax.psum_scatter(partial_value * inside, 'shot', scatter_dimension=1, til...  70.2 us
    ppermute x14, starting transfers between devices, padded_2(): before = lax.ppermute(last, axis, up)  57.2 us
    while x42, local copies, waits for them, and re-layouts  41.8 us
    slice x14, local copies, waits for them, and re-layouts, padded_2(): initial = lax.slice_in_dim(x, 0, width, axis=dim)  32.8 us
    dynamic_slice x14, local copies, waits for them, and re-layouts, correlate(): lax.dynamic_index_in_dim(snaps, slot, 0, keepdims=False).astype(jnp.float32)  29.6 us
    dynamic_slice x14, local copies, waits for them, and re-layouts, record(): older = lax.dynamic_slice_in_dim(snaps, slot, 1, 0)  29 us
    add x7, other arithmetic, one_step(): 2.0 * current - before + velocity_term * laplace(current, horizontal)  27.8 us
  transfers between devices with their start and end apart: 32, of which 1 were waited for; matrix products, arithmetic and copies ran while one was open for 35% of the time, Pallas kernels for 0%

commit v1 on v0

v1 whole, which is shorter than its diff:
```python
import jax
import jax.numpy as jnp
from jax import lax
from jax.experimental import pallas as pl
from jax.experimental.pallas import tpu as pltpu
from jax.sharding import PartitionSpec as P


PAD = 8
EDGE = 16
LANES = 128
WIRE = jnp.int16
STEPS_OF_SCALE = (32, 16, 8, 4, 2, 1)
FIXED = 65536.0


def spans(rows, chunk):
    return [(r0, min(chunk, rows - r0)) for r0 in range(0, rows, chunk)]


def neighbour_matrix():
    row = lax.broadcasted_iota(jnp.int32, (2 * LANES, LANES), 0)
    column = lax.broadcasted_iota(jnp.int32, (2 * LANES, LANES), 1)
    row = jnp.where(row >= LANES, row - LANES, row)
    beside = (row - column == 1) | (column - row == 1)
    return jnp.where(beside, 1.0, 0.0).astype(jnp.bfloat16)


def stencil_step(src, dst, coefs, lo, hi, rows, beside, sums, surface=None):
    centre, hor, vel = coefs

    def body(i, carry):
        x = lo + 2 * i
        for j in range(2):
            for r0, size in spans(rows, 144):
                c = src[x + j, pl.ds(PAD + r0, size), :]
                high = c.astype(jnp.bfloat16)
                low = (c - high.astype(jnp.float32)).astype(jnp.bfloat16)
                sums[j, pl.ds(r0, size), :] = jnp.dot(
                    jnp.concatenate([high, low], axis=1), beside[...],
                    preferred_element_type=jnp.float32,
                )
        shifts = [None, None] if surface is None else [surface[1](x), surface[1](x + 1)]
        for r0, size in spans(rows, 32):
            at = pl.ds(PAD + r0, size)
            here = pl.ds(r0, size)
            c = [src[x - 1 + j, at, :] for j in range(4)]
            for j in range(2):
                mid = c[j + 1]
                lateral = c[j] + c[j + 2]
                lateral = lateral + src[x + j, pl.ds(PAD + r0 - 1, size), :]
                lateral = lateral + src[x + j, pl.ds(PAD + r0 + 1, size), :]
                vertical = sums[j, here, :]
                if surface is not None:
                    lane = lax.broadcasted_iota(jnp.int32, (size, LANES), 1)
                    plane, shift = shifts[j]
                    data = pltpu.roll(surface[0][plane, here, :], shift, 1)
                    vertical = vertical + jnp.where(lane == 0, data, 0.0)
                new = centre[x + j, here, :] * mid - dst[x + j, at, :]
                new = new + hor[x + j, here, :] * lateral
                new = new + vel[x + j, here, :] * vertical
                dst[x + j, at, :] = new
        return carry

    lax.fori_loop(0, (hi - lo) // 2, body, 0)


def header_rows(first, half_rows):
    return jnp.where(first == 0, half_rows + 8, 0)


def encode_scale(top):
    up, down, exponent = jnp.ones_like(top), jnp.ones_like(top), jnp.zeros_like(top)
    for j in STEPS_OF_SCALE:
        more = top * 2.0**j
        fits = more < 15.9
        top = jnp.where(fits, more, top)
        up = jnp.where(fits, up * 2.0**j, up)
        down = jnp.where(fits, down * 2.0**-j, down)
        exponent = jnp.where(fits, exponent + j, exponent)
    return up * 2048.0, down / 2048.0, exponent


def decode_scale(stage, layer, first, half_rows):
    base = pl.multiple_of(jnp.where(first == 0, half_rows, 0), 16)
    block = stage[layer, pl.ds(base, 16), :].astype(jnp.int32).astype(jnp.float32)
    row = lax.broadcasted_iota(jnp.int32, (16, LANES), 0)
    skip = jnp.where(first == 0, 8, 0)
    held = (row >= skip) & (row < skip + 8)
    exponent = jnp.max(jnp.where(held, block, 0.0), axis=(0, 1), keepdims=True)
    scale = jnp.full_like(exponent, 1.0 / 2048.0)
    for j in STEPS_OF_SCALE:
        holds = exponent >= j
        scale = jnp.where(holds, scale * 2.0**-j, scale)
        exponent = jnp.where(holds, exponent - j, exponent)
    return scale


def slot_of(steps, time):
    slot = jnp.int32(0)
    found = jnp.int32(0)
    for k, step in enumerate(steps):
        hit = (step == time).astype(jnp.int32)
        slot = slot + hit * k
        found = found + hit
    return slot, found > 0


def wave_pass(kind, field, field_at, vel, ani, left, right, halo_at, ints, amps, half_rows, reach,
              n_snaps, blocks=1, others=(), data=None):
    width, all_rows, depth_cells = vel.shape
    rows = half_rows + EDGE
    layers = width + 2 * reach
    near = reach - 1
    backward = kind in ("waves", "image")
    packed = not isinstance(field, tuple)
    fields = [field] if packed else list(field) + ([data] if backward else [])
    depths = (reach, near, near, near) + ((1,) if backward else ())
    n_side = len(left)

    def kernel(*refs):
        ints_ref, amps_ref = refs[0], refs[1]
        pos = 2
        field_refs = refs[pos : pos + len(fields)]
        pos += len(fields)
        vel_ref, ani_ref = refs[pos : pos + 2]
        pos += 2
        left_refs = refs[pos : pos + n_side]
        pos += n_side
        right_refs = refs[pos : pos + n_side]
        pos += n_side
        other_hbm = refs[pos : pos + len(others)]
        pos += len(others)
        n_out = blocks if kind == "blocks" else 1
        outs = refs[pos : pos + n_out]
        pos += n_out
        buf_a, buf_b, v_buf, h_buf, c_buf, stage_l, stage_r, stage_t, top, beside, sums, sem = refs[
            pos : pos + 12
        ]

        steps = [ints_ref[k] for k in range(n_snaps)]
        first_row, skip, inside, source_x, source_y, place = [
            ints_ref[n_snaps + k] for k in range(6)
        ]
        window = pl.ds(pl.multiple_of(first_row, 8), rows)
        inner = pl.ds(PAD, rows)

        tile_copies = [
            pltpu.make_async_copy(
                vel_ref.at[:, window], v_buf.at[pl.ds(reach, width)], sem.at[0]
            ),
            pltpu.make_async_copy(
                ani_ref.at[:, window], h_buf.at[pl.ds(reach, width)], sem.at[1]
            ),
        ]
        side_copies = []
        where = 0
        offsets = []
        for depth, (pack, layer) in zip(depths, halo_at):
            n = len(side_copies)
            side_copies.append(
                pltpu.make_async_copy(
                    left_refs[pack].at[pl.ds(layer, depth)],
                    stage_l.at[pl.ds(where, depth)],
                    sem.at[2 + n],
                )
            )
            side_copies.append(
                pltpu.make_async_copy(
                    right_refs[pack].at[pl.ds(layer, depth)],
                    stage_r.at[pl.ds(where, depth)],
                    sem.at[3 + n],
                )
            )
            offsets.append(where)
            where += depth
        if packed:
            field_copies = [pltpu.make_async_copy(field_refs[0], stage_t, sem.at[12])]
        else:
            field_copies = [
                pltpu.make_async_copy(
                    field_refs[0].at[:, window], buf_a.at[pl.ds(reach, width), inner], sem.at[12]
                ),
                pltpu.make_async_copy(
                    field_refs[1].at[:, window], buf_b.at[pl.ds(reach, width), inner], sem.at[13]
                ),
            ]
            if backward:
                n_data = data.shape[0]
                flat = refs[-2]
                field_copies.append(
                    pltpu.make_async_copy(field_refs[2], flat.at[pl.ds(0, n_data)], sem.at[14])
                )
                flat[n_data:, :] = jnp.zeros((LANES - n_data, all_rows), jnp.float32)
        other_refs = refs[pos + 12 : pos + 12 + len(others)]
        other_copies = [
            pltpu.make_async_copy(source, target, sem.at[15 + n])
            for n, (source, target) in enumerate(zip(other_hbm, other_refs))
        ]
        for copy in tile_copies + side_copies + field_copies + other_copies:
            copy.start()
        beside[...] = neighbour_matrix()
        zeros = jnp.zeros((layers, PAD, LANES), jnp.float32)
        for buf in (buf_a, buf_b):
            buf[:, 0:PAD, :] = zeros
            buf[:, PAD + rows : PAD + rows + PAD, :] = zeros
        for copy in side_copies:
            copy.wait()

        def widen(stage, at, dst, first, count, row0, scale):
            def body(x, carry):
                for r0, size in spans(rows, 64):
                    code = stage[at + x, pl.ds(r0, size), :].astype(jnp.int32)
                    dst[first + x, pl.ds(row0 + r0, size), :] = code.astype(jnp.float32) * scale
                return carry

            lax.fori_loop(0, count, body, 0)

        side_scales = []
        for stage, starts in ((stage_l, (0, 1, 1, 1)), (stage_r, (reach + width,) * 4)):
            scale = decode_scale(stage, offsets[0], first_row, half_rows)
            side_scales.append(scale)
            for dst, at, start, depth, row0, unit in zip(
                (buf_a, buf_b, v_buf, h_buf), offsets, starts, depths, (PAD, PAD, 0, 0),
                (scale, scale, 1.0 / FIXED, 1.0 / FIXED),
            ):
                widen(stage, at, dst, start, depth, row0, unit)
        for copy in tile_copies:
            copy.wait()

        def coefficients(x, carry):
            for r0, size in spans(rows, 64):
                at = pl.ds(r0, size)
                v = v_buf[x, at, :]
                h = v * (1.0 + 2.0 * h_buf[x, at, :])
                h_buf[x, at, :] = h
                c_buf[x, at, :] = 2.0 - (4.0 * h + 2.0 * v)
            return carry

        lax.fori_loop(1, layers - 1, coefficients, 0)
        for copy in field_copies:
            copy.wait()
        if packed:
            scale = decode_scale(stage_t, field_at[0], first_row, half_rows)
            widen(stage_t, field_at[0], buf_a, reach, width, PAD, scale)
            widen(stage_t, field_at[1], buf_b, reach, width, PAD, scale)
        surface = None
        if backward:
            widen(stage_l, offsets[4], top, 0, 1, 0, side_scales[0])
            if packed:
                widen(stage_t, field_at[2], top, 1, 1, 0, scale)
            else:
                turned = refs[-1]
                turned[...] = flat[...].T
                top[1] = turned[window, :]
            widen(stage_r, offsets[4], top, 2, 1, 0, side_scales[1])

        if kind in ("image", "blocks"):
            image = outs[0] if kind == "image" else refs[-1]
            image[...] = jnp.zeros_like(image)

        def record(buf, time):
            slot, found = slot_of(steps, time)
            if kind in ("image", "blocks"):
                found = found & (inside > 0)

            @pl.when(found)
            def _():
                def body(x, carry):
                    for r0, size in spans(half_rows, 64):
                        base = pl.multiple_of(PAD + skip + r0, 8)
                        at = pl.ds(r0, size)
                        value = buf[reach + x, pl.ds(base, size), :]
                        if kind in ("snaps", "waves"):
                            outs[0][slot, x, at, :] = value.astype(outs[0].dtype)
                        elif kind == "image":
                            u = other_refs[0][slot, x, at, :].astype(jnp.float32)
                            image[x, at, :] = image[x, at, :] + u * value
                        else:
                            u = value.astype(jnp.bfloat16).astype(jnp.float32)
                            image[x, at, :] = image[x, at, :] + u * other_refs[1][slot, x, at, :]
                    return carry

                lax.fori_loop(0, width, body, 0)

        src, dst = buf_a, buf_b
        coefs = (c_buf, h_buf, v_buf)
        for copy in other_copies:
            copy.wait()
        record(src, reach + 1 if backward else 1)
        for step in range(1, reach + 1):
            lo, hi = step, layers - step
            if backward:

                def shift(x, step=step):
                    past = x - reach + width
                    plane = past // width
                    lane = (reach - step) * width + past - plane * width
                    return plane, lax.rem(LANES - lane, LANES)

                surface = (top, shift)
            stencil_step(src, dst, coefs, lo, hi, rows, beside, sums, surface)
            if not backward:
                row8 = lax.broadcasted_iota(jnp.int32, (8, LANES), 0)
                lane8 = lax.broadcasted_iota(jnp.int32, (8, LANES), 1)

                @pl.when((source_x >= lo) & (source_x < hi) & (source_y >= 0) & (source_y < rows))
                def _(dst=dst, step=step):
                    base = pl.multiple_of((source_y // 8) * 8, 8)
                    at = pl.ds(pl.multiple_of(base + PAD, 8), 8)
                    mask = (row8 == source_y - base) & (lane8 == 0)
                    add = v_buf[source_x, pl.ds(base, 8), :] * amps_ref[step - 1]
                    dst[source_x, at, :] = dst[source_x, at, :] + jnp.where(mask, add, 0.0)

            src, dst = dst, src
            record(src, reach + 1 - step if backward else step + 1)

        if kind == "blocks":
            block = half_rows // blocks
            for d, out in enumerate(outs):
                base = pl.multiple_of(lax.rem(place + d, blocks) * block, 8)

                def cut(x, carry, out=out, base=base):
                    at = pl.ds(base, block)
                    out[x] = other_refs[0][x, at, :] + image[x, at, :]
                    return carry

                lax.fori_loop(0, width, cut, 0)

    any_spec = pl.BlockSpec(memory_space=pl.ANY)
    smem = pl.BlockSpec(memory_space=pltpu.SMEM)
    vmem = pl.BlockSpec(memory_space=pltpu.VMEM)
    shape = (width, half_rows, depth_cells)
    if kind == "blocks":
        out_shape = (jax.ShapeDtypeStruct((width, half_rows // blocks, depth_cells), jnp.float32),) * blocks
    elif kind == "image":
        out_shape = (jax.ShapeDtypeStruct(shape, jnp.float32),)
    else:
        dtype = jnp.bfloat16 if kind == "snaps" else jnp.float32
        out_shape = (jax.ShapeDtypeStruct((n_snaps,) + shape, dtype),)
    cells = layers * rows * depth_cells
    grid_buf = pltpu.VMEM((layers, rows, depth_cells), jnp.float32)
    field_buf = pltpu.VMEM((layers, rows + 2 * PAD, depth_cells), jnp.float32)
    stage_layers = field.shape[0] if packed else 1
    side = pltpu.VMEM((sum(depths), rows, depth_cells), WIRE)
    return pl.pallas_call(
        kernel,
        out_shape=out_shape,
        in_specs=[smem, smem] + [any_spec] * (len(fields) + 2 + 2 * n_side + len(others)),
        out_specs=(vmem,) * len(out_shape),
        scratch_shapes=[
            field_buf, field_buf, grid_buf, grid_buf, grid_buf, side, side,
            pltpu.VMEM((stage_layers, rows, depth_cells), WIRE),
            pltpu.VMEM((3, rows, depth_cells), jnp.float32),
            pltpu.VMEM((2 * LANES, LANES), jnp.bfloat16),
            pltpu.VMEM((2, rows, depth_cells), jnp.float32),
            pltpu.SemaphoreType.DMA((18,)),
        ]
        + [pltpu.VMEM(other.shape, other.dtype) for other in others]
        + ([pltpu.VMEM(shape, jnp.float32)] if kind == "blocks" else [])
        + (
            [pltpu.VMEM((LANES, all_rows), jnp.float32), pltpu.VMEM((all_rows, LANES), jnp.float32)]
            if kind == "waves"
            else []
        ),
        cost_estimate=pl.CostEstimate(
            flops=15 * cells * reach, bytes_accessed=20 * cells, transcendentals=0
        ),
    )(ints, amps, *fields, vel, ani, *left, *right, *others)


def any_specs(n):
    return [pl.BlockSpec(memory_space=pl.ANY)] * n


def pack_rows(first, fields, ranges, groups, data):
    width, all_rows, depth_cells = fields[0].shape
    half_rows = all_rows // 2
    rows = half_rows + EDGE
    tail = 0 if data is None else 1
    sizes = [sum(hi - lo for _, lo, hi in r) + tail for r in ranges]
    n = len(fields)
    loose = [i for i in range(n) if not any(i in group for group in groups)]

    def kernel(first_ref, *refs):
        field_refs = refs[:n]
        outs = refs[n + tail : n + tail + len(ranges)]
        rest = refs[n + tail + len(ranges) :]
        wide, narrow, sem, out_sem = rest[:4]
        window = pl.ds(pl.multiple_of(first_ref[0], 16), rows)
        spare = pl.ds(pl.multiple_of(header_rows(first_ref[0], half_rows), 8), 8)
        copies = [
            pltpu.make_async_copy(ref.at[:, window], wide.at[i], sem.at[i])
            for i, ref in enumerate(field_refs)
        ]
        for copy in copies:
            copy.start()
        started = []

        def go(source, target):
            copy = pltpu.make_async_copy(source, target, out_sem.at[len(started)])
            copy.start()
            started.append(copy)

        def code(values, scale):
            return jnp.floor(values * scale + 0.5).astype(jnp.int32).astype(WIRE)

        def put(i, scale):
            def body(x, carry):
                for r0, size in spans(rows, 64):
                    at = pl.ds(r0, size)
                    narrow[i, x, at, :] = code(wide[i, x, at, :], scale)
                return carry

            lax.fori_loop(0, width, body, 0)
            for out, pieces in zip(outs, ranges):
                where = 0
                for field, lo, hi in pieces:
                    if field == i:
                        go(narrow.at[i, pl.ds(lo, hi - lo)], out.at[pl.ds(where, hi - lo)])
                    where += hi - lo

        for number, group in enumerate(groups):
            with_data = tail and number == len(groups) - 1
            if with_data:
                flat, turned = rest[4:6]
                load = pltpu.make_async_copy(refs[n], flat.at[pl.ds(0, data.shape[0])], sem.at[n])
                load.start()
                load.wait()
                flat[data.shape[0] :, :] = jnp.zeros((LANES - data.shape[0], all_rows), jnp.float32)
                turned[...] = flat[...].T
            top = jnp.zeros((8, LANES), jnp.float32)
            for i in group:
                copies[i].wait()

                def largest(x, top, i=i):
                    for r0, size in spans(rows, 64):
                        block = jnp.abs(wide[i, x, pl.ds(r0, size), :])
                        top = jnp.maximum(top, jnp.max(block.reshape(-1, 8, LANES), axis=0))
                    return top

                top = lax.fori_loop(0, width, largest, top)
            if with_data:
                block = jnp.abs(turned[window, :])
                top = jnp.maximum(top, jnp.max(block.reshape(-1, 8, LANES), axis=0))
            top = jnp.max(top, axis=(0, 1), keepdims=True)
            scale, unit, exponent = encode_scale(top)
            header = jnp.broadcast_to(exponent * unit, (8, LANES))
            for x in range(width):
                wide[group[0], x, spare, :] = header
            for i in group:
                put(i, scale)
            if with_data:
                narrow[n, 0] = code(turned[window, :], scale)
                for out, size in zip(outs, sizes):
                    go(narrow.at[n, pl.ds(0, 1)], out.at[pl.ds(size - 1, 1)])
        for i in loose:
            copies[i].wait()
            put(i, FIXED)
        for copy in started:
            copy.wait()

    n_out = sum(len(r) for r in ranges) + tail * len(ranges)
    scratch = [
        pltpu.VMEM((n, width, rows, depth_cells), jnp.float32),
        pltpu.VMEM((n + tail, width, rows, depth_cells), WIRE),
        pltpu.SemaphoreType.DMA((n + 1,)),
        pltpu.SemaphoreType.DMA((n_out,)),
    ]
    if tail:
        scratch += [
            pltpu.VMEM((LANES, all_rows), jnp.float32),
            pltpu.VMEM((all_rows, LANES), jnp.float32),
        ]
    cells = n * width * rows * depth_cells
    return pl.pallas_call(
        kernel,
        out_shape=tuple(jax.ShapeDtypeStruct((m, rows, depth_cells), WIRE) for m in sizes),
        in_specs=[pl.BlockSpec(memory_space=pltpu.SMEM)] + any_specs(n + tail),
        out_specs=tuple(any_specs(len(sizes))),
        scratch_shapes=scratch,
        cost_estimate=pl.CostEstimate(flops=cells, bytes_accessed=8 * cells, transcendentals=0),
        name="pack_rows",
    )(first, *fields, *([] if data is None else [data]))


def repack(packed, ranges):
    sizes = [sum(hi - lo for lo, hi in r) for r in ranges]
    n_out = sum(len(r) for r in ranges)

    def kernel(packed_ref, *refs):
        outs = refs[: len(ranges)]
        stage, sem, out_sem = refs[len(ranges) :]
        load = pltpu.make_async_copy(packed_ref, stage, sem.at[0])
        load.start()
        load.wait()
        started = []
        for out, pieces in zip(outs, ranges):
            where = 0
            for lo, hi in pieces:
                copy = pltpu.make_async_copy(
                    stage.at[pl.ds(lo, hi - lo)],
                    out.at[pl.ds(where, hi - lo)],
                    out_sem.at[len(started)],
                )
                copy.start()
                started.append(copy)
                where += hi - lo
        for copy in started:
            copy.wait()

    return pl.pallas_call(
        kernel,
        out_shape=tuple(jax.ShapeDtypeStruct((m,) + packed.shape[1:], packed.dtype) for m in sizes),
        in_specs=any_specs(1),
        out_specs=tuple(any_specs(len(sizes))),
        scratch_shapes=[
            pltpu.VMEM(packed.shape, packed.dtype),
            pltpu.SemaphoreType.DMA((1,)),
            pltpu.SemaphoreType.DMA((n_out,)),
        ],
        cost_estimate=pl.CostEstimate(
            flops=0, bytes_accessed=6 * packed.size, transcendentals=0
        ),
        name="repack",
    )(packed)


def on_device(
    fwd_prev,
    fwd_cur,
    bwd_next,
    bwd_cur,
    receiver_data,
    velocity_term,
    anisotropy,
    wavelet,
    shot_x,
    shot_y,
    aperture,
    snap_steps,
):
    shots = lax.axis_size("shot")
    tiles = lax.axis_size("xy")
    me = lax.axis_index("shot")
    tile = lax.axis_index("xy")
    half = shots // 2
    side = me // half
    partner = (me + half) % shots
    width, rows = fwd_prev.shape[1], fwd_prev.shape[2]
    reach = wavelet.shape[1]
    near = reach - 1
    n_snaps = snap_steps.shape[0]
    half_rows = rows // 2
    my_first = side * (half_rows - EDGE)
    their_first = (1 - side) * (half_rows - EDGE)
    across = [(i, (i + half) % shots) for i in range(shots)]
    up = [(i, i + 1) for i in range(tiles - 1)]
    down = [(i + 1, i) for i in range(tiles - 1)]
    u0, u1, w9, w8 = fwd_prev[0], fwd_cur[0], bwd_next[0], bwd_cur[0]

    data = receiver_data[0].reshape(reach * width, rows)

    def at(first):
        return jnp.reshape(first, (1,)).astype(jnp.int32)

    whole = ((0, 0, width), (1, 0, width))
    (send_w,) = pack_rows(at(their_first), (w8, w9), (whole,), ((0, 1),), data)
    import_w = lax.ppermute(send_w, "shot", across)
    (send_u,) = pack_rows(at(their_first), (u1, u0), (whole,), ((0, 1),), None)
    import_u = lax.ppermute(send_u, "shot", across)

    local = (u1, u0, velocity_term, anisotropy, w8, w9)
    depths = (reach, near, near, near, reach, near)
    up_m, down_m = pack_rows(
        at(my_first), local,
        (
            [(i, width - d, width) for i, d in enumerate(depths)],
            [(i, 0, d) for i, d in enumerate(depths)],
        ),
        ((0, 1), (4, 5)), data,
    )
    left = lax.ppermute(up_m, "xy", up)
    right = lax.ppermute(down_m, "xy", down)

    def numbers(shot):
        chosen = (jnp.arange(shots, dtype=jnp.int32) == shot).astype(jnp.int32)
        source_x = jnp.sum(chosen * shot_x) - tile * width + reach
        source_y = jnp.sum(chosen * shot_y) - my_first
        inside = jnp.any((chosen[:, None] > 0) & (aperture == tile)).astype(jnp.int32)
        amps = jnp.sum(jnp.where(chosen[:, None] > 0, wavelet, 0.0), axis=0)
        parts = jnp.stack([my_first, side * EDGE, inside, source_x, source_y, me % half])
        return jnp.concatenate([snap_steps, parts]).astype(jnp.int32), amps

    ints_me, amps_me = numbers(me)
    ints_partner, amps_partner = numbers(partner)
    common = dict(half_rows=half_rows, reach=reach, n_snaps=n_snaps)
    at_v, at_a = (0, reach + near), (0, reach + 2 * near)
    at_w = reach + 3 * near
    (snaps,) = wave_pass(
        "snaps", (u1, u0), None, velocity_term, anisotropy, [left], [right],
        ((0, 0), (0, reach), at_v, at_a), ints_me, amps_me, **common,
    )

    def from_sides(packed, tail):
        ends = [(2 * width, 2 * width + 1)] if tail else []
        send_up, send_down = repack(
            packed,
            (
                [(width - reach, width), (2 * width - near, 2 * width)] + ends,
                [(0, reach), (width, width + near)] + ends,
            ),
        )
        from_left = lax.ppermute(send_up, "xy", up)
        from_right = lax.ppermute(send_down, "xy", down)
        return from_left, from_right

    (waves,) = wave_pass(
        "waves", (w8, w9), None, velocity_term, anisotropy, [left], [right],
        ((0, at_w), (0, at_w + reach), at_v, at_a, (0, at_w + reach + near)),
        ints_partner, amps_partner, data=data, **common,
    )
    left_w, right_w = from_sides(import_w, True)
    (image,) = wave_pass(
        "image", import_w, (0, width, 2 * width), velocity_term, anisotropy,
        [left, left_w], [right, right_w],
        ((1, 0), (1, reach), at_v, at_a, (1, reach + near)),
        ints_me, amps_me, others=(snaps,), **common,
    )
    left_u, right_u = from_sides(import_u, False)
    blocks = wave_pass(
        "blocks", import_u, (0, width), velocity_term, anisotropy,
        [left, left_u], [right, right_u], ((1, 0), (1, reach), at_v, at_a),
        ints_partner, amps_partner, blocks=half, others=(image, waves), **common,
    )
    total = blocks[0]
    for d in range(1, half):
        route = [(i, (i // half) * half + (i % half + d) % half) for i in range(shots)]
        arrived = lax.ppermute(blocks[d], "shot", route)
        total = total + arrived
    return total


def solution(mesh):
    in_specs = (
        P("shot", "xy", None, None),
        P("shot", "xy", None, None),
        P("shot", "xy", None, None),
        P("shot", "xy", None, None),
        P("shot", None, "xy", None),
        P("xy", None, None),
        P("xy", None, None),
        P(),
        P(),
        P(),
        P(),
        P(),
    )
    out_specs = P("xy", "shot", None)

    return jax.shard_map(
        on_device, mesh=mesh, in_specs=in_specs, out_specs=out_specs, check_vma=False
    )
```

time: 551 us -> 228 us (0.41)
  local copies, waits for them, and re-layouts: 183 us -> 1.27 us
  other arithmetic: 168 us -> 3.83 us
  Pallas kernels: 0 us -> 94.6 us
  starting transfers between devices: 82.2 us -> 24.3 us
  waiting for transfers between devices: 70.3 us -> 97.4 us
  loops' own time: 26.5 us -> 0 us
  between operations: 18 us -> 3.95 us
    add x15 -> x1, other arithmetic: 120 us -> 1.72 us  [on_device(): total = total + arrived]
    ppermute x31 -> x11, waiting for transfers between devices: 0.08 us -> 97.4 us  [the longest x1 71.6 us: on_device(): import_w = lax.ppermute(send_w, 'shot', across)]
    pallas_call x0 -> x9, Pallas kernels: none -> 94.6 us  [the longest x4 76.4 us: wave_pass(): pl.pallas_call(kernel, out_shape=out_shape, in_specs=[smem, smem] + [any_...]
    reduce_scatter x1 -> x0, waiting for transfers between devices: 70.2 us -> none  [on_device(): lax.psum_scatter(partial_value * inside, 'shot', scatter_dimension=1, til...]
    dynamic_slice x35 -> x0, local copies, waits for them, and re-layouts: 62.9 us -> none  [the longest x14 29.6 us: correlate(): lax.dynamic_index_in_dim(snaps, slot, 0, keepdims=False).astype(jnp.float32)]
    ppermute x31 -> x11, starting transfers between devices: 82.2 us -> 24.3 us  [the longest x2 10 us: from_sides(): from_left = lax.ppermute(send_up, 'xy', up)]
    while x45 -> x0, local copies, waits for them, and re-layouts: 47.8 us -> none
    slice x14 -> x0, local copies, waits for them, and re-layouts: 32.8 us -> none  [padded_2(): initial = lax.slice_in_dim(x, 0, width, axis=dim)]
  transfers between devices with their start and end apart: 32 -> 11, of which waited for: 1 -> 5; matrix products, arithmetic and copies ran while one was open for 35% -> 1% of each run, Pallas kernels for 0% -> 31%
where the time goes in v1:
time: 228 us; the launch traced here: 225 us
  waiting for transfers between devices  97.4 us (43%)
  Pallas kernels  94.6 us (41%)
  starting transfers between devices  24.3 us (11%)
  between operations  3.95 us (2%)
  other arithmetic  3.83 us (2%)
    pallas_call x4, Pallas kernels, wave_pass(): pl.pallas_call(kernel, out_shape=out_shape, in_specs=[smem, smem] + [any_...  76.4 us
    ppermute x1, waiting for transfers between devices, on_device(): import_w = lax.ppermute(send_w, 'shot', across)  71.6 us
    ppermute x1, waiting for transfers between devices, on_device(): import_u = lax.ppermute(send_u, 'shot', across)  14.1 us
    pallas_call x3, Pallas kernels, pack_rows(): pl.pallas_call(kernel, out_shape=tuple((jax.ShapeDtypeStruct((m, rows, de...  13 us
    ppermute x3, waiting for transfers between devices, on_device(): arrived = lax.ppermute(blocks[d], 'shot', route)  11.6 us
    ppermute x2, starting transfers between devices, from_sides(): from_left = lax.ppermute(send_up, 'xy', up)  10 us
    pallas_call x2, Pallas kernels, repack(): pl.pallas_call(kernel, out_shape=tuple((jax.ShapeDtypeStruct((m,) + packe...  5.12 us
  transfers between devices with their start and end apart: 11, of which 5 were waited for; matrix products, arithmetic and copies ran while one was open for 1% of the time, Pallas kernels for 31%

profile of v1, /device:TPU:0, one launch (start us, length us, event | category | flops | bytes accessed | tf_op | source)
XLA Modules:
  0.0 225.2 jit_solution(11689668537908174315)
XLA Ops:
  0.0 6.3 %pack_rows.4 = (s16[39,272,128]{2,1,0:T(8,128)(2,1)}, s16[39,272,128]{2,1,0:T(8,128)(2,1)}) custom-call(s32[1]{0:T(128)} %bitcast.first_ref, f32[8,512,128]{2,1,0:T(8,128)} %bitcast.15, f32[8,512,128]{2,1,0:T(8,128)} %bitcast.18, f32[8,512,128]{2,1,0:T(8,128)} %refs_3_.5, f32[8,512,128]{2,1,0:T(8,128)} %refs_4_.5, f32[8,512,128]{2,1,0:T(8,128)} %bitcast.21, ...), custom_call_target="tpu_custom_call" | custom-call | flops 1671168 | bytes 13369344 | tf_op jit(solution)/shard_map/pack_rows/pallas_call | solution.py:476
  6.3 2.6 %collective-permute-start.1 = (s16[39,272,128]{2,1,0:T(8,128)(2,1)}, s16[39,272,128]{2,1,0:T(8,128)(2,1)S(1)}, u32[]{:S(2)}, u32[]{:S(2)}) collective-permute-start(s16[39,272,128]{2,1,0:T(8,128)(2,1)} %get-tuple-element.15), channel_id=1, source_target_pairs={{0,1},{1,2},{2,3},{4,5},{5,6},{6,7},{8,9},{9,10},{10,11},{12,13},{... | collective-permute-start | bytes 8146952 | tf_op jit(solution)/shard_map/ppermute | solution.py:583
  8.9 1.3 collective-permute-start.3
  10.2 3.5 %pack_rows.5 = s16[17,272,128]{2,1,0:T(8,128)(2,1)} custom-call(s32[1]{0:T(128)} %bitcast.6.first_ref, f32[8,512,128]{2,1,0:T(8,128)} %bitcast.22, f32[8,512,128]{2,1,0:T(8,128)} %bitcast.25, f32[56,512]{1,0:T(8,128)} %bitcast.28), custom_call_target="tpu_custom_call" | custom-call | flops 557056 | bytes 4456448 | tf_op jit(solution)/shard_map/pack_rows/pallas_call | solution.py:476
  13.7 3.5 %collective-permute-start.5 = (s16[17,272,128]{2,1,0:T(8,128)(2,1)}, s16[17,272,128]{2,1,0:T(8,128)(2,1)}, u32[]{:S(2)}, u32[]{:S(2)}) collective-permute-start(s16[17,272,128]{2,1,0:T(8,128)(2,1)} %pack_rows.5), channel_id=1, source_target_pairs={{0,16},{4,20},{8,24},{12,28},{16,0},{20,4},{24,8},{28,12},{1,17},{... | collective-permute-start | bytes 3551240 | tf_op jit(solution)/shard_map/ppermute | solution.py:569
  17.1 3.2 %pack_rows.3 = s16[16,272,128]{2,1,0:T(8,128)(2,1)} custom-call(s32[1]{0:T(128)} %bitcast.6.first_ref, f32[8,512,128]{2,1,0:T(8,128)} %bitcast.16, f32[8,512,128]{2,1,0:T(8,128)} %bitcast.19), custom_call_target="tpu_custom_call" | custom-call | flops 557056 | bytes 4456448 | tf_op jit(solution)/shard_map/pack_rows/pallas_call | solution.py:476
  20.4 0.0 copy-start.3
  20.4 0.0 copy-start.4
  20.4 0.0 copy-start.5
  20.4 0.0 copy-start.2
  20.4 0.0 copy-start.1
  20.5 0.1 collective-permute-start
  20.5 71.6 %collective-permute-done.5.packed_ref.refs_2_ = s16[17,272,128]{2,1,0:T(8,128)(2,1)} collective-permute-done((s16[17,272,128]{2,1,0:T(8,128)(2,1)}, s16[17,272,128]{2,1,0:T(8,128)(2,1)}, u32[]{:S(2)}, u32[]{:S(2)}) %collective-permute-start.5) | collective-permute-done | bytes 1183776 | tf_op jit(solution)/shard_map/ppermute | solution.py:569
  92.2 2.6 %repack.3 = (s16[14,272,128]{2,1,0:T(8,128)(2,1)}, s16[14,272,128]{2,1,0:T(8,128)(2,1)}) custom-call(s16[17,272,128]{2,1,0:T(8,128)(2,1)} %collective-permute-done.5.packed_ref.refs_2_), custom_call_target="tpu_custom_call" | custom-call | bytes 3551232 | tf_op jit(solution)/shard_map/repack/pallas_call | solution.py:512
  94.8 5.9 %collective-permute-start.6 = (s16[14,272,128]{2,1,0:T(8,128)(2,1)}, s16[14,272,128]{2,1,0:T(8,128)(2,1)}, u32[]{:S(2)}, u32[]{:S(2)}) collective-permute-start(s16[14,272,128]{2,1,0:T(8,128)(2,1)} %get-tuple-element.19), channel_id=1, source_target_pairs={{0,1},{1,2},{2,3},{4,5},{5,6},{6,7},{8,9},{9,10},{10,11},{12,13},{... | collective-permute-start | bytes 2924552 | tf_op jit(solution)/shard_map/ppermute | solution.py:614
  100.6 1.3 collective-permute-start.7
  101.9 14.1 %collective-permute-done.packed_ref.refs_2_ = s16[16,272,128]{2,1,0:T(8,128)(2,1)} collective-permute-done((s16[16,272,128]{2,1,0:T(8,128)(2,1)}, s16[16,272,128]{2,1,0:T(8,128)(2,1)}, u32[]{:S(2)}, u32[]{:S(2)}) %collective-permute-start) | collective-permute-done | bytes 1114144 | tf_op jit(solution)/shard_map/ppermute | solution.py:571
  116.0 2.5 %repack.2 = (s16[13,272,128]{2,1,0:T(8,128)(2,1)}, s16[13,272,128]{2,1,0:T(8,128)(2,1)}) custom-call(s16[16,272,128]{2,1,0:T(8,128)(2,1)} %collective-permute-done.packed_ref.refs_2_), custom_call_target="tpu_custom_call" | custom-call | bytes 3342336 | tf_op jit(solution)/shard_map/repack/pallas_call | solution.py:512
  118.6 4.1 %collective-permute-start.2 = (s16[13,272,128]{2,1,0:T(8,128)(2,1)}, s16[13,272,128]{2,1,0:T(8,128)(2,1)}, u32[]{:S(2)}, u32[]{:S(2)}) collective-permute-start(s16[13,272,128]{2,1,0:T(8,128)(2,1)} %get-tuple-element.16), channel_id=1, source_target_pairs={{0,1},{1,2},{2,3},{4,5},{5,6},{6,7},{8,9},{9,10},{10,11},{12,13},{... | collective-permute-start | bytes 2715656 | tf_op jit(solution)/shard_map/ppermute | solution.py:614
  122.7 0.0 collective-permute-done.1.refs_6_.refs_5_.refs_7_
  122.7 1.3 collective-permute-start.4
  124.1 0.0 copy-done.3
  124.1 0.7 and_reduce_fusion
  126.0 0.0 copy-done.4
  126.0 0.0 copy-done.5
  126.0 0.8 select_reduce_fusion.2
  129.2 0.0 copy-done.2
  129.3 0.6 concatenate.7.refs_0_
  129.9 0.6 concatenate.6.refs_0_
  130.5 0.0 copy-done.1
  130.5 0.7 select_reduce_fusion
  131.1 0.0 collective-permute-done.3.refs_7_.refs_8_
  131.1 0.0 copy-done
  131.1 18.3 %shard_map.118.refs_9_ = bf16[4,8,256,128]{3,2,1,0:T(8,128)(2,1)} custom-call(s32[10]{0:T(128)} %concatenate.7.refs_0_, f32[7]{0:T(128)} %get-tuple-element.25.refs_1_, f32[8,512,128]{2,1,0:T(8,128)} %bitcast.17, f32[8,512,128]{2,1,0:T(8,128)} %bitcast.20, f32[8,512,128]{2,1,0:T(8,128)} %refs_3_.5, f32[8,512,128]{2,1,0:T(8,128)} %refs_4_.5, ...), custom_call_target="tpu_custom_call" | custom-call | flops 80424960 | bytes 15319040 | tf_op jit(solution)/shard_map/pallas_call | solution.py:346
  149.5 19.7 %shard_map.120.refs_10_ = f32[4,8,256,128]{3,2,1,0:T(8,128)} custom-call(s32[10]{0:T(128)} %concatenate.6.refs_0_, f32[7]{0:T(128)} %get-tuple-element.26.refs_1_, f32[8,512,128]{2,1,0:T(8,128)} %bitcast.23, f32[8,512,128]{2,1,0:T(8,128)} %bitcast.26, f32[56,512]{1,0:T(8,128)} %bitcast.29, f32[8,512,128]{2,1,0:T(8,128)} %refs_3_.5, f32[8,512,128]{2,1,0:T(8,128)} %refs_4_.5, ...), custom_call_target="tpu_custom_call" | custom-call | flops 80424960 | bytes 15319040 | tf_op jit(solution)/shard_map/pallas_call | solution.py:346
  169.2 0.0 collective-permute-done.6.refs_6_
  169.2 0.0 collective-permute-done.7.refs_8_
  169.2 18.9 %shard_map.119.refs_9_ = f32[8,256,128]{2,1,0:T(8,128)} custom-call(s32[10]{0:T(128)} %concatenate.7.refs_0_, f32[7]{0:T(128)} %get-tuple-element.25.refs_1_, s16[17,272,128]{2,1,0:T(8,128)(2,1)} %collective-permute-done.5.packed_ref.refs_2_, f32[8,512,128]{2,1,0:T(8,128)} %refs_3_.5, f32[8,512,128]{2,1,0:T(8,128)} %refs_4_.5, s16[39,272,128]{2,1,0:T(8,128)(2,1)} %copy-done, ...), custom_call_target="tpu_custom_call" | custom-call | flops 80424960 | bytes 15319040 | tf_op jit(solution)/shard_map/pallas_call | solution.py:346
  188.2 0.0 collective-permute-done.2.refs_6_
  188.2 0.0 collective-permute-done.4.refs_8_
  188.2 19.5 %shard_map.121 = (f32[8,64,128]{2,1,0:T(8,128)}, f32[8,64,128]{2,1,0:T(8,128)}, f32[8,64,128]{2,1,0:T(8,128)}, f32[8,64,128]{2,1,0:T(8,128)}) custom-call(s32[10]{0:T(128)} %concatenate.6.refs_0_, f32[7]{0:T(128)} %get-tuple-element.26.refs_1_, s16[16,272,128]{2,1,0:T(8,128)(2,1)} %collective-permute-done.packed_ref.refs_2_, f32[8,512,128]{2,1,0:T(8,128)} %refs_3_.5, ...), custom_call_target="tpu_custom_call" | custom-call | flops 80424960 | bytes 15319040 | tf_op jit(solution)/shard_map/pallas_call | solution.py:346
  207.6 2.7 %collective-permute-start.8 = (f32[8,64,128]{2,1,0:T(8,128)}, f32[8,64,128]{2,1,0:T(8,128)S(1)}, u32[]{:S(2)}, u32[]{:S(2)}) collective-permute-start(f32[8,64,128]{2,1,0:T(8,128)} %get-tuple-element.22), channel_id=1, source_target_pairs={{0,4},{4,8},{8,12},{12,0},{16,20},{20,24},{24,28},{28,16},{1,5},{5... | collective-permute-start | bytes 786440 | tf_op jit(solution)/shard_map/ppermute | solution.py:639
  210.4 0.0 collective-permute-start.9
  210.4 1.5 collective-permute-start.10
  211.9 4.0 %collective-permute-done.8 = f32[8,64,128]{2,1,0:T(8,128)S(1)} collective-permute-done((f32[8,64,128]{2,1,0:T(8,128)}, f32[8,64,128]{2,1,0:T(8,128)S(1)}, u32[]{:S(2)}, u32[]{:S(2)}) %collective-permute-start.8) | collective-permute-done | bytes 262176 | tf_op jit(solution)/shard_map/ppermute | solution.py:639
  215.9 2.7 %collective-permute-done.9 = f32[8,64,128]{2,1,0:T(8,128)S(1)} collective-permute-done((f32[8,64,128]{2,1,0:T(8,128)}, f32[8,64,128]{2,1,0:T(8,128)S(1)}, u32[]{:S(2)}, u32[]{:S(2)}) %collective-permute-start.9) | collective-permute-done | bytes 262176 | tf_op jit(solution)/shard_map/ppermute | solution.py:639
  218.6 4.9 %collective-permute-done.10 = f32[8,64,128]{2,1,0:T(8,128)S(1)} collective-permute-done((f32[8,64,128]{2,1,0:T(8,128)}, f32[8,64,128]{2,1,0:T(8,128)S(1)}, u32[]{:S(2)}, u32[]{:S(2)}) %collective-permute-start.10) | collective-permute-done | bytes 262176 | tf_op jit(solution)/shard_map/ppermute | solution.py:639
  223.5 1.7 add_add_fusion
  (2 shorter events, 0.0 us)
Async XLA Ops:
  6.3 116.4 %collective-permute-start.1 = (s16[39,272,128]{2,1,0:T(8,128)(2,1)}, s16[39,272,128]{2,1,0:T(8,128)(2,1)S(1)}, u32[]{:S(2)}, u32[]{:S(2)}) collective-permute-start(s16[39,272,128]{2,1,0:T(8,128)(2,1)} %get-tuple-element.15), channel_id=1, source_target_pairs={{0,1},{1,2},{2,3},{4,5},{5,6},{6,7},{8,9},{9,10},{10,11},{12,13},{... | collective-permute-start | bytes 8146952 | tf_op jit(solution)/shard_map/ppermute | solution.py:583
  8.9 122.3 %collective-permute-start.3 = (s16[39,272,128]{2,1,0:T(8,128)(2,1)}, s16[39,272,128]{2,1,0:T(8,128)(2,1)}, u32[]{:S(2)}, u32[]{:S(2)}) collective-permute-start(s16[39,272,128]{2,1,0:T(8,128)(2,1)} %get-tuple-element.17), channel_id=1, source_target_pairs={{1,0},{2,1},{3,2},{5,4},{6,5},{7,6},{9,8},{10,9},{11,10},{13,12},{... | collective-permute-start | bytes 8146952 | tf_op jit(solution)/shard_map/ppermute | solution.py:584
  13.7 78.5 %collective-permute-start.5 = (s16[17,272,128]{2,1,0:T(8,128)(2,1)}, s16[17,272,128]{2,1,0:T(8,128)(2,1)}, u32[]{:S(2)}, u32[]{:S(2)}) collective-permute-start(s16[17,272,128]{2,1,0:T(8,128)(2,1)} %pack_rows.5), channel_id=1, source_target_pairs={{0,16},{4,20},{8,24},{12,28},{16,0},{20,4},{24,8},{28,12},{1,17},{... | collective-permute-start | bytes 3551240 | tf_op jit(solution)/shard_map/ppermute | solution.py:569
  20.4 103.7 %copy-start.3 = (s32[8,2]{0,1:T(2,128)S(1)}, s32[8,2]{0,1:T(2,128)}, u32[]{:S(2)}) copy-start(s32[8,2]{0,1:T(2,128)} %param.22) | copy-start | bytes 196
  20.4 105.6 %copy-start.4 = (s32[8]{0:T(128)S(1)}, s32[8]{0:T(128)}, u32[]{:S(2)}) copy-start(s32[8]{0:T(128)} %param.21) | copy-start | bytes 100
  20.4 105.5 %copy-start.5 = (s32[8]{0:T(128)S(1)}, s32[8]{0:T(128)}, u32[]{:S(2)}) copy-start(s32[8]{0:T(128)} %param.20) | copy-start | bytes 100
  20.4 108.8 %copy-start.2 = (s32[4]{0:T(128)S(1)}, s32[4]{0:T(128)}, u32[]{:S(2)}) copy-start(s32[4]{0:T(128)} %param.23) | copy-start | bytes 52
  20.4 110.0 %copy-start.1 = (f32[8,7]{1,0:T(8,128)S(1)}, f32[8,7]{1,0:T(8,128)}, u32[]{:S(2)}) copy-start(f32[8,7]{1,0:T(8,128)} %param.19) | copy-start | bytes 676
  20.5 95.6 %collective-permute-start = (s16[16,272,128]{2,1,0:T(8,128)(2,1)}, s16[16,272,128]{2,1,0:T(8,128)(2,1)}, u32[]{:S(2)}, u32[]{:S(2)}) collective-permute-start(s16[16,272,128]{2,1,0:T(8,128)(2,1)} %pack_rows.3), channel_id=1, source_target_pairs={{0,16},{4,20},{8,24},{12,28},{16,0},{20,4},{24,8},{28,12},{1,17},{... | collective-permute-start | bytes 3342344 | tf_op jit(solution)/shard_map/ppermute | solution.py:571
  94.8 74.4 %collective-permute-start.6 = (s16[14,272,128]{2,1,0:T(8,128)(2,1)}, s16[14,272,128]{2,1,0:T(8,128)(2,1)}, u32[]{:S(2)}, u32[]{:S(2)}) collective-permute-start(s16[14,272,128]{2,1,0:T(8,128)(2,1)} %get-tuple-element.19), channel_id=1, source_target_pairs={{0,1},{1,2},{2,3},{4,5},{5,6},{6,7},{8,9},{9,10},{10,11},{12,13},{... | collective-permute-start | bytes 2924552 | tf_op jit(solution)/shard_map/ppermute | solution.py:614
  100.6 68.6 %collective-permute-start.7 = (s16[14,272,128]{2,1,0:T(8,128)(2,1)}, s16[14,272,128]{2,1,0:T(8,128)(2,1)}, u32[]{:S(2)}, u32[]{:S(2)}) collective-permute-start(s16[14,272,128]{2,1,0:T(8,128)(2,1)} %get-tuple-element.20), channel_id=1, source_target_pairs={{1,0},{2,1},{3,2},{5,4},{6,5},{7,6},{9,8},{10,9},{11,10},{13,12},{... | collective-permute-start | bytes 2924552 | tf_op jit(solution)/shard_map/ppermute | solution.py:615
  118.6 69.6 %collective-permute-start.2 = (s16[13,272,128]{2,1,0:T(8,128)(2,1)}, s16[13,272,128]{2,1,0:T(8,128)(2,1)}, u32[]{:S(2)}, u32[]{:S(2)}) collective-permute-start(s16[13,272,128]{2,1,0:T(8,128)(2,1)} %get-tuple-element.16), channel_id=1, source_target_pairs={{0,1},{1,2},{2,3},{4,5},{5,6},{6,7},{8,9},{9,10},{10,11},{12,13},{... | collective-permute-start | bytes 2715656 | tf_op jit(solution)/shard_map/ppermute | solution.py:614
  122.7 8.4 %copy-start = (s16[39,272,128]{2,1,0:T(8,128)(2,1)}, s16[39,272,128]{2,1,0:T(8,128)(2,1)S(1)}, u32[]{:S(2)}) copy-start(s16[39,272,128]{2,1,0:T(8,128)(2,1)S(1)} %collective-permute-done.1.refs_6_.refs_5_.refs_7_) | copy-start | bytes 8146948
  122.7 65.4 %collective-permute-start.4 = (s16[13,272,128]{2,1,0:T(8,128)(2,1)}, s16[13,272,128]{2,1,0:T(8,128)(2,1)}, u32[]{:S(2)}, u32[]{:S(2)}) collective-permute-start(s16[13,272,128]{2,1,0:T(8,128)(2,1)} %get-tuple-element.18), channel_id=1, source_target_pairs={{1,0},{2,1},{3,2},{5,4},{6,5},{7,6},{9,8},{10,9},{11,10},{13,12},{... | collective-permute-start | bytes 2715656 | tf_op jit(solution)/shard_map/ppermute | solution.py:615
  207.6 8.3 %collective-permute-start.8 = (f32[8,64,128]{2,1,0:T(8,128)}, f32[8,64,128]{2,1,0:T(8,128)S(1)}, u32[]{:S(2)}, u32[]{:S(2)}) collective-permute-start(f32[8,64,128]{2,1,0:T(8,128)} %get-tuple-element.22), channel_id=1, source_target_pairs={{0,4},{4,8},{8,12},{12,0},{16,20},{20,24},{24,28},{28,16},{1,5},{5... | collective-permute-start | bytes 786440 | tf_op jit(solution)/shard_map/ppermute | solution.py:639
  210.4 8.2 %collective-permute-start.9 = (f32[8,64,128]{2,1,0:T(8,128)}, f32[8,64,128]{2,1,0:T(8,128)S(1)}, u32[]{:S(2)}, u32[]{:S(2)}) collective-permute-start(f32[8,64,128]{2,1,0:T(8,128)} %get-tuple-element.23), channel_id=1, source_target_pairs={{0,8},{4,12},{8,0},{12,4},{16,24},{20,28},{24,16},{28,20},{1,9},{5... | collective-permute-start | bytes 786440 | tf_op jit(solution)/shard_map/ppermute | solution.py:639
  210.4 13.1 %collective-permute-start.10 = (f32[8,64,128]{2,1,0:T(8,128)}, f32[8,64,128]{2,1,0:T(8,128)S(1)}, u32[]{:S(2)}, u32[]{:S(2)}) collective-permute-start(f32[8,64,128]{2,1,0:T(8,128)} %get-tuple-element.24), channel_id=1, source_target_pairs={{0,12},{4,0},{8,4},{12,8},{16,28},{20,16},{24,20},{28,24},{1,13},{... | collective-permute-start | bytes 786440 | tf_op jit(solution)/shard_map/ppermute | solution.py:639

commit v2 on v1

--- a/solution.py
+++ b/solution.py
@@ -29,39 +29,43 @@
 def stencil_step(src, dst, coefs, lo, hi, rows, beside, sums, surface=None):
     centre, hor, vel = coefs
 
-    def body(i, carry):
-        x = lo + 2 * i
-        for j in range(2):
-            for r0, size in spans(rows, 144):
-                c = src[x + j, pl.ds(PAD + r0, size), :]
-                high = c.astype(jnp.bfloat16)
-                low = (c - high.astype(jnp.float32)).astype(jnp.bfloat16)
-                sums[j, pl.ds(r0, size), :] = jnp.dot(
-                    jnp.concatenate([high, low], axis=1), beside[...],
-                    preferred_element_type=jnp.float32,
-                )
-        shifts = [None, None] if surface is None else [surface[1](x), surface[1](x + 1)]
+    def vertical_sums(x, j):
+        for r0, size in spans(rows, 144):
+            c = src[x, pl.ds(PAD + r0, size), :]
+            high = c.astype(jnp.bfloat16)
+            low = (c - high.astype(jnp.float32)).astype(jnp.bfloat16)
+            sums[j, pl.ds(r0, size), :] = jnp.dot(
+                jnp.concatenate([high, low], axis=1), beside[...],
+                preferred_element_type=jnp.float32,
+            )
+
+    def one_layer(x, j):
         for r0, size in spans(rows, 32):
             at = pl.ds(PAD + r0, size)
             here = pl.ds(r0, size)
-            c = [src[x - 1 + j, at, :] for j in range(4)]
-            for j in range(2):
-                mid = c[j + 1]
-                lateral = c[j] + c[j + 2]
-                lateral = lateral + src[x + j, pl.ds(PAD + r0 - 1, size), :]
-                lateral = lateral + src[x + j, pl.ds(PAD + r0 + 1, size), :]
-                vertical = sums[j, here, :]
-                if surface is not None:
-                    lane = lax.broadcasted_iota(jnp.int32, (size, LANES), 1)
-                    plane, shift = shifts[j]
-                    data = pltpu.roll(surface[0][plane, here, :], shift, 1)
-                    vertical = vertical + jnp.where(lane == 0, data, 0.0)
-                new = centre[x + j, here, :] * mid - dst[x + j, at, :]
-                new = new + hor[x + j, here, :] * lateral
-                new = new + vel[x + j, here, :] * vertical
-                dst[x + j, at, :] = new
+            lateral = src[x - 1, at, :] + src[x + 1, at, :]
+            lateral = lateral + src[x, pl.ds(PAD + r0 - 1, size), :]
+            lateral = lateral + src[x, pl.ds(PAD + r0 + 1, size), :]
+            vertical = sums[j, here, :]
+            if surface is not None:
+                lane = lax.broadcasted_iota(jnp.int32, (size, LANES), 1)
+                plane, shift = surface[1](x)
+                data = pltpu.roll(surface[0][plane, here, :], shift, 1)
+                vertical = vertical + jnp.where(lane == 0, data, 0.0)
+            new = centre[x, here, :] * src[x, at, :] - dst[x, at, :]
+            new = new + hor[x, here, :] * lateral
+            new = new + vel[x, here, :] * vertical
+            dst[x, at, :] = new
+
+    def body(i, carry):
+        x = lo + 2 * i
+        vertical_sums(x + 1, 1)
+        one_layer(x, 0)
+        vertical_sums(x + 2, 0)
+        one_layer(x + 1, 1)
         return carry
 
+    vertical_sums(lo, 0)
     lax.fori_loop(0, (hi - lo) // 2, body, 0)
 
 
@@ -567,21 +571,26 @@
     whole = ((0, 0, width), (1, 0, width))
     (send_w,) = pack_rows(at(their_first), (w8, w9), (whole,), ((0, 1),), data)
     import_w = lax.ppermute(send_w, "shot", across)
+
+    def sides(fields, depths, groups, data):
+        send_up, send_down = pack_rows(
+            at(my_first), fields,
+            (
+                [(i, width - d, width) for i, d in enumerate(depths)],
+                [(i, 0, d) for i, d in enumerate(depths)],
+            ),
+            groups, data,
+        )
+        from_left = lax.ppermute(send_up, "xy", up)
+        from_right = lax.ppermute(send_down, "xy", down)
+        return from_left, from_right
+
+    left, right = sides(
+        (u1, u0, velocity_term, anisotropy), (reach, near, near, near), ((0, 1),), None
+    )
+    left_l, right_l = sides((w8, w9), (reach, near), ((0, 1),), data)
     (send_u,) = pack_rows(at(their_first), (u1, u0), (whole,), ((0, 1),), None)
     import_u = lax.ppermute(send_u, "shot", across)
-
-    local = (u1, u0, velocity_term, anisotropy, w8, w9)
-    depths = (reach, near, near, near, reach, near)
-    up_m, down_m = pack_rows(
-        at(my_first), local,
-        (
-            [(i, width - d, width) for i, d in enumerate(depths)],
-            [(i, 0, d) for i, d in enumerate(depths)],
-        ),
-        ((0, 1), (4, 5)), data,
-    )
-    left = lax.ppermute(up_m, "xy", up)
-    right = lax.ppermute(down_m, "xy", down)
 
     def numbers(shot):
         chosen = (jnp.arange(shots, dtype=jnp.int32) == shot).astype(jnp.int32)
@@ -596,7 +605,6 @@
     ints_partner, amps_partner = numbers(partner)
     common = dict(half_rows=half_rows, reach=reach, n_snaps=n_snaps)
     at_v, at_a = (0, reach + near), (0, reach + 2 * near)
-    at_w = reach + 3 * near
     (snaps,) = wave_pass(
         "snaps", (u1, u0), None, velocity_term, anisotropy, [left], [right],
         ((0, 0), (0, reach), at_v, at_a), ints_me, amps_me, **common,
@@ -616,8 +624,8 @@
         return from_left, from_right
 
     (waves,) = wave_pass(
-        "waves", (w8, w9), None, velocity_term, anisotropy, [left], [right],
-        ((0, at_w), (0, at_w + reach), at_v, at_a, (0, at_w + reach + near)),
+        "waves", (w8, w9), None, velocity_term, anisotropy, [left, left_l], [right, right_l],
+        ((1, 0), (1, reach), at_v, at_a, (1, reach + near)),
         ints_partner, amps_partner, data=data, **common,
     )
     left_w, right_w = from_sides(import_w, True)

time: 228 us -> 236 us (1.035)
  Pallas kernels: 94.6 us -> 104 us
  waiting for transfers between devices: 97.4 us -> 88.1 us
  starting transfers between devices: 24.3 us -> 31.6 us
    ppermute x1, waiting for transfers between devices: 71.6 us -> 62.9 us  [on_device(): import_w = lax.ppermute(send_w, 'shot', across)]
    pallas_call x4, Pallas kernels: 76.4 us -> 84.3 us  [wave_pass(): pl.pallas_call(kernel, out_shape=out_shape, in_specs=[smem, smem] + [any_...]
    ppermute x2 -> x4, starting transfers between devices: 3.86 us -> 10.1 us  [the longest x2 7.54 us: sides(): from_left = lax.ppermute(send_up, 'xy', up)]
    pallas_call x3 -> x4, Pallas kernels: 13 us -> 14.4 us  [pack_rows(): pl.pallas_call(kernel, out_shape=tuple((jax.ShapeDtypeStruct((m, rows, de...]
  transfers between devices with their start and end apart: 11 -> 13, of which waited for: 5 -> 5; matrix products, arithmetic and copies ran while one was open for 1% -> 1% of each run, Pallas kernels for 31% -> 34%
where the time goes in v2:
time: 236 us; the launch traced here: 233 us
  Pallas kernels  104 us (44%)
  waiting for transfers between devices  88.1 us (37%)
  starting transfers between devices  31.6 us (13%)
  between operations  4.33 us (2%)
  other arithmetic  3.85 us (2%)
    pallas_call x4, Pallas kernels, wave_pass(): pl.pallas_call(kernel, out_shape=out_shape, in_specs=[smem, smem] + [any_...  84.3 us
    ppermute x1, waiting for transfers between devices, on_device(): import_w = lax.ppermute(send_w, 'shot', across)  62.9 us
    pallas_call x4, Pallas kernels, pack_rows(): pl.pallas_call(kernel, out_shape=tuple((jax.ShapeDtypeStruct((m, rows, de...  14.4 us
    ppermute x1, waiting for transfers between devices, on_device(): import_u = lax.ppermute(send_u, 'shot', across)  13.4 us
    ppermute x3, waiting for transfers between devices, on_device(): arrived = lax.ppermute(blocks[d], 'shot', route)  11.8 us
    ppermute x2, starting transfers between devices, from_sides(): from_left = lax.ppermute(send_up, 'xy', up)  11.2 us
    ppermute x2, starting transfers between devices, sides(): from_left = lax.ppermute(send_up, 'xy', up)  7.54 us
    pallas_call x2, Pallas kernels, repack(): pl.pallas_call(kernel, out_shape=tuple((jax.ShapeDtypeStruct((m,) + packe...  5.3 us
  transfers between devices with their start and end apart: 13, of which 5 were waited for; matrix products, arithmetic and copies ran while one was open for 1% of the time, Pallas kernels for 34%

profile of v2, /device:TPU:0, one launch (start us, length us, event | category | flops | bytes accessed | tf_op | source)
XLA Modules:
  0.0 233.2 jit_solution(34413673618924209)
XLA Ops:
  0.0 4.0 %pack_rows.5 = (s16[25,272,128]{2,1,0:T(8,128)(2,1)}, s16[25,272,128]{2,1,0:T(8,128)(2,1)}) custom-call(s32[1]{0:T(128)} %bitcast.first_ref, f32[8,512,128]{2,1,0:T(8,128)} %bitcast.15, f32[8,512,128]{2,1,0:T(8,128)} %bitcast.18, f32[8,512,128]{2,1,0:T(8,128)} %refs_3_.5, f32[8,512,128]{2,1,0:T(8,128)} %refs_4_.5), custom_call_target="tpu_custom_call" | custom-call | flops 1114112 | bytes 8912896 | tf_op jit(solution)/shard_map/pack_rows/pallas_call | solution.py:480
  4.0 2.5 %collective-permute-start.1 = (s16[25,272,128]{2,1,0:T(8,128)(2,1)}, s16[25,272,128]{2,1,0:T(8,128)(2,1)S(1)}, u32[]{:S(2)}, u32[]{:S(2)}) collective-permute-start(s16[25,272,128]{2,1,0:T(8,128)(2,1)} %get-tuple-element.17), channel_id=1, source_target_pairs={{0,1},{1,2},{2,3},{4,5},{5,6},{6,7},{8,9},{9,10},{10,11},{12,13},{... | collective-permute-start | bytes 5222408 | tf_op jit(solution)/shard_map/ppermute | solution.py:584
  6.5 1.3 collective-permute-start.3
  7.8 3.5 %pack_rows.6 = s16[17,272,128]{2,1,0:T(8,128)(2,1)} custom-call(s32[1]{0:T(128)} %bitcast.6.first_ref, f32[8,512,128]{2,1,0:T(8,128)} %bitcast.21, f32[8,512,128]{2,1,0:T(8,128)} %bitcast.24, f32[56,512]{1,0:T(8,128)} %bitcast.27), custom_call_target="tpu_custom_call" | custom-call | flops 557056 | bytes 4456448 | tf_op jit(solution)/shard_map/pack_rows/pallas_call | solution.py:480
  11.4 3.5 %collective-permute-start.5 = (s16[17,272,128]{2,1,0:T(8,128)(2,1)}, s16[17,272,128]{2,1,0:T(8,128)(2,1)}, u32[]{:S(2)}, u32[]{:S(2)}) collective-permute-start(s16[17,272,128]{2,1,0:T(8,128)(2,1)} %pack_rows.6), channel_id=1, source_target_pairs={{0,16},{4,20},{8,24},{12,28},{16,0},{20,4},{24,8},{28,12},{1,17},{... | collective-permute-start | bytes 3551240 | tf_op jit(solution)/shard_map/ppermute | solution.py:573
  14.9 3.2 %pack_rows.4 = s16[16,272,128]{2,1,0:T(8,128)(2,1)} custom-call(s32[1]{0:T(128)} %bitcast.6.first_ref, f32[8,512,128]{2,1,0:T(8,128)} %bitcast.16, f32[8,512,128]{2,1,0:T(8,128)} %bitcast.19), custom_call_target="tpu_custom_call" | custom-call | flops 557056 | bytes 4456448 | tf_op jit(solution)/shard_map/pack_rows/pallas_call | solution.py:480
  18.1 0.1 collective-permute-start
  18.2 3.7 %pack_rows.7 = (s16[14,272,128]{2,1,0:T(8,128)(2,1)}, s16[14,272,128]{2,1,0:T(8,128)(2,1)}) custom-call(s32[1]{0:T(128)} %bitcast.first_ref, f32[8,512,128]{2,1,0:T(8,128)} %bitcast.22, f32[8,512,128]{2,1,0:T(8,128)} %bitcast.25, f32[56,512]{1,0:T(8,128)} %bitcast.28), custom_call_target="tpu_custom_call" | custom-call | flops 557056 | bytes 4456448 | tf_op jit(solution)/shard_map/pack_rows/pallas_call | solution.py:480
  21.8 0.0 copy-start.5
  21.9 0.0 copy-start.6
  21.9 0.0 copy-start.4
  21.9 0.0 copy-start.3
  21.9 0.0 copy-start.2
  21.9 5.0 %collective-permute-start.8 = (s16[14,272,128]{2,1,0:T(8,128)(2,1)}, s16[14,272,128]{2,1,0:T(8,128)(2,1)}, u32[]{:S(2)}, u32[]{:S(2)}) collective-permute-start(s16[14,272,128]{2,1,0:T(8,128)(2,1)} %get-tuple-element.23), channel_id=1, source_target_pairs={{0,1},{1,2},{2,3},{4,5},{5,6},{6,7},{8,9},{9,10},{10,11},{12,13},{... | collective-permute-start | bytes 2924552 | tf_op jit(solution)/shard_map/ppermute | solution.py:584
  26.9 62.9 %collective-permute-done.5.packed_ref.refs_2_ = s16[17,272,128]{2,1,0:T(8,128)(2,1)} collective-permute-done((s16[17,272,128]{2,1,0:T(8,128)(2,1)}, s16[17,272,128]{2,1,0:T(8,128)(2,1)}, u32[]{:S(2)}, u32[]{:S(2)}) %collective-permute-start.5) | collective-permute-done | bytes 1183776 | tf_op jit(solution)/shard_map/ppermute | solution.py:573
  89.9 1.3 collective-permute-start.9
  91.2 2.7 %repack.3 = (s16[14,272,128]{2,1,0:T(8,128)(2,1)}, s16[14,272,128]{2,1,0:T(8,128)(2,1)}) custom-call(s16[17,272,128]{2,1,0:T(8,128)(2,1)} %collective-permute-done.5.packed_ref.refs_2_), custom_call_target="tpu_custom_call" | custom-call | bytes 3551232 | tf_op jit(solution)/shard_map/repack/pallas_call | solution.py:516
  93.9 0.0 collective-permute-done.8.refs_8_
  93.9 6.5 %collective-permute-start.6 = (s16[14,272,128]{2,1,0:T(8,128)(2,1)}, s16[14,272,128]{2,1,0:T(8,128)(2,1)}, u32[]{:S(2)}, u32[]{:S(2)}) collective-permute-start(s16[14,272,128]{2,1,0:T(8,128)(2,1)} %get-tuple-element.21), channel_id=1, source_target_pairs={{0,1},{1,2},{2,3},{4,5},{5,6},{6,7},{8,9},{9,10},{10,11},{12,13},{... | collective-permute-start | bytes 2924552 | tf_op jit(solution)/shard_map/ppermute | solution.py:622
  100.4 13.4 %collective-permute-done.packed_ref.refs_2_ = s16[16,272,128]{2,1,0:T(8,128)(2,1)} collective-permute-done((s16[16,272,128]{2,1,0:T(8,128)(2,1)}, s16[16,272,128]{2,1,0:T(8,128)(2,1)}, u32[]{:S(2)}, u32[]{:S(2)}) %collective-permute-start) | collective-permute-done | bytes 1114144 | tf_op jit(solution)/shard_map/ppermute | solution.py:593
  113.8 1.3 collective-permute-start.7
  115.1 2.6 %repack.2 = (s16[13,272,128]{2,1,0:T(8,128)(2,1)}, s16[13,272,128]{2,1,0:T(8,128)(2,1)}) custom-call(s16[16,272,128]{2,1,0:T(8,128)(2,1)} %collective-permute-done.packed_ref.refs_2_), custom_call_target="tpu_custom_call" | custom-call | bytes 3342336 | tf_op jit(solution)/shard_map/repack/pallas_call | solution.py:516
  117.7 0.0 collective-permute-done.1.refs_6_.refs_5_.refs_7_
  117.7 4.7 %collective-permute-start.2 = (s16[13,272,128]{2,1,0:T(8,128)(2,1)}, s16[13,272,128]{2,1,0:T(8,128)(2,1)}, u32[]{:S(2)}, u32[]{:S(2)}) collective-permute-start(s16[13,272,128]{2,1,0:T(8,128)(2,1)} %get-tuple-element.18), channel_id=1, source_target_pairs={{0,1},{1,2},{2,3},{4,5},{5,6},{6,7},{8,9},{9,10},{10,11},{12,13},{... | collective-permute-start | bytes 2715656 | tf_op jit(solution)/shard_map/ppermute | solution.py:622
  122.4 0.0 collective-permute-done.3.refs_7_.refs_9_
  122.4 1.3 collective-permute-start.4
  123.7 0.8 select_reduce_fusion.2
  125.8 0.0 copy-done.4
  125.9 0.7 and_reduce_fusion
  129.3 0.7 concatenate.7.refs_0_
  129.9 0.6 concatenate.6.refs_0_
  130.5 0.7 select_reduce_fusion
  131.2 20.5 %shard_map.118.refs_9_ = bf16[4,8,256,128]{3,2,1,0:T(8,128)(2,1)} custom-call(s32[10]{0:T(128)} %concatenate.7.refs_0_, f32[7]{0:T(128)} %get-tuple-element.29.refs_1_, f32[8,512,128]{2,1,0:T(8,128)} %bitcast.17, f32[8,512,128]{2,1,0:T(8,128)} %bitcast.20, f32[8,512,128]{2,1,0:T(8,128)} %refs_3_.5, f32[8,512,128]{2,1,0:T(8,128)} %refs_4_.5, ...), custom_call_target="tpu_custom_call" | custom-call | flops 80424960 | bytes 15319040 | tf_op jit(solution)/shard_map/pallas_call | solution.py:350
  151.7 0.0 collective-permute-done.9.refs_10_
  151.7 21.4 %shard_map.120.refs_10_ = f32[4,8,256,128]{3,2,1,0:T(8,128)} custom-call(s32[10]{0:T(128)} %concatenate.6.refs_0_, f32[7]{0:T(128)} %get-tuple-element.30.refs_1_, f32[8,512,128]{2,1,0:T(8,128)} %bitcast.23, f32[8,512,128]{2,1,0:T(8,128)} %bitcast.26, f32[56,512]{1,0:T(8,128)} %bitcast.29, f32[8,512,128]{2,1,0:T(8,128)} %refs_3_.5, f32[8,512,128]{2,1,0:T(8,128)} %refs_4_.5, ...), custom_call_target="tpu_custom_call" | custom-call | flops 80424960 | bytes 15319040 | tf_op jit(solution)/shard_map/pallas_call | solution.py:350
  173.1 0.0 collective-permute-done.6.refs_6_
  173.1 0.0 collective-permute-done.7.refs_8_
  173.2 20.7 %shard_map.119.refs_9_ = f32[8,256,128]{2,1,0:T(8,128)} custom-call(s32[10]{0:T(128)} %concatenate.7.refs_0_, f32[7]{0:T(128)} %get-tuple-element.29.refs_1_, s16[17,272,128]{2,1,0:T(8,128)(2,1)} %collective-permute-done.5.packed_ref.refs_2_, f32[8,512,128]{2,1,0:T(8,128)} %refs_3_.5, f32[8,512,128]{2,1,0:T(8,128)} %refs_4_.5, s16[25,272,128]{2,1,0:T(8,128)(2,1)} %copy-done, ...), custom_call_target="tpu_custom_call" | custom-call | flops 80424960 | bytes 15319040 | tf_op jit(solution)/shard_map/pallas_call | solution.py:350
  193.9 0.0 collective-permute-done.2.refs_6_
  193.9 0.0 collective-permute-done.4.refs_8_
  193.9 21.6 %shard_map.121 = (f32[8,64,128]{2,1,0:T(8,128)}, f32[8,64,128]{2,1,0:T(8,128)}, f32[8,64,128]{2,1,0:T(8,128)}, f32[8,64,128]{2,1,0:T(8,128)}) custom-call(s32[10]{0:T(128)} %concatenate.6.refs_0_, f32[7]{0:T(128)} %get-tuple-element.30.refs_1_, s16[16,272,128]{2,1,0:T(8,128)(2,1)} %collective-permute-done.packed_ref.refs_2_, f32[8,512,128]{2,1,0:T(8,128)} %refs_3_.5, ...), custom_call_target="tpu_custom_call" | custom-call | flops 80424960 | bytes 15319040 | tf_op jit(solution)/shard_map/pallas_call | solution.py:350
  215.5 2.6 %collective-permute-start.10 = (f32[8,64,128]{2,1,0:T(8,128)}, f32[8,64,128]{2,1,0:T(8,128)S(1)}, u32[]{:S(2)}, u32[]{:S(2)}) collective-permute-start(f32[8,64,128]{2,1,0:T(8,128)} %get-tuple-element.26), channel_id=1, source_target_pairs={{0,4},{4,8},{8,12},{12,0},{16,20},{20,24},{24,28},{28,16},{1,5},{5... | collective-permute-start | bytes 786440 | tf_op jit(solution)/shard_map/ppermute | solution.py:647
  218.2 0.0 collective-permute-start.11
  218.2 1.5 collective-permute-start.12
  219.7 5.3 %collective-permute-done.10 = f32[8,64,128]{2,1,0:T(8,128)S(1)} collective-permute-done((f32[8,64,128]{2,1,0:T(8,128)}, f32[8,64,128]{2,1,0:T(8,128)S(1)}, u32[]{:S(2)}, u32[]{:S(2)}) %collective-permute-start.10) | collective-permute-done | bytes 262176 | tf_op jit(solution)/shard_map/ppermute | solution.py:647
  225.0 2.5 %collective-permute-done.11 = f32[8,64,128]{2,1,0:T(8,128)S(1)} collective-permute-done((f32[8,64,128]{2,1,0:T(8,128)}, f32[8,64,128]{2,1,0:T(8,128)S(1)}, u32[]{:S(2)}, u32[]{:S(2)}) %collective-permute-start.11) | collective-permute-done | bytes 262176 | tf_op jit(solution)/shard_map/ppermute | solution.py:647
  227.6 3.9 %collective-permute-done.12 = f32[8,64,128]{2,1,0:T(8,128)S(1)} collective-permute-done((f32[8,64,128]{2,1,0:T(8,128)}, f32[8,64,128]{2,1,0:T(8,128)S(1)}, u32[]{:S(2)}, u32[]{:S(2)}) %collective-permute-start.12) | collective-permute-done | bytes 262176 | tf_op jit(solution)/shard_map/ppermute | solution.py:647
  231.5 1.7 add_add_fusion
  (9 shorter events, 0.0 us)
Async XLA Ops:
  4.0 113.6 %collective-permute-start.1 = (s16[25,272,128]{2,1,0:T(8,128)(2,1)}, s16[25,272,128]{2,1,0:T(8,128)(2,1)S(1)}, u32[]{:S(2)}, u32[]{:S(2)}) collective-permute-start(s16[25,272,128]{2,1,0:T(8,128)(2,1)} %get-tuple-element.17), channel_id=1, source_target_pairs={{0,1},{1,2},{2,3},{4,5},{5,6},{6,7},{8,9},{9,10},{10,11},{12,13},{... | collective-permute-start | bytes 5222408 | tf_op jit(solution)/shard_map/ppermute | solution.py:584
  6.5 115.9 %collective-permute-start.3 = (s16[25,272,128]{2,1,0:T(8,128)(2,1)}, s16[25,272,128]{2,1,0:T(8,128)(2,1)S(1)}, u32[]{:S(2)}, u32[]{:S(2)}) collective-permute-start(s16[25,272,128]{2,1,0:T(8,128)(2,1)} %get-tuple-element.19), channel_id=1, source_target_pairs={{1,0},{2,1},{3,2},{5,4},{6,5},{7,6},{9,8},{10,9},{11,10},{13,12},{... | collective-permute-start | bytes 5222408 | tf_op jit(solution)/shard_map/ppermute | solution.py:585
  11.4 78.5 %collective-permute-start.5 = (s16[17,272,128]{2,1,0:T(8,128)(2,1)}, s16[17,272,128]{2,1,0:T(8,128)(2,1)}, u32[]{:S(2)}, u32[]{:S(2)}) collective-permute-start(s16[17,272,128]{2,1,0:T(8,128)(2,1)} %pack_rows.6), channel_id=1, source_target_pairs={{0,16},{4,20},{8,24},{12,28},{16,0},{20,4},{24,8},{28,12},{1,17},{... | collective-permute-start | bytes 3551240 | tf_op jit(solution)/shard_map/ppermute | solution.py:573
  18.1 95.7 %collective-permute-start = (s16[16,272,128]{2,1,0:T(8,128)(2,1)}, s16[16,272,128]{2,1,0:T(8,128)(2,1)}, u32[]{:S(2)}, u32[]{:S(2)}) collective-permute-start(s16[16,272,128]{2,1,0:T(8,128)(2,1)} %pack_rows.4), channel_id=1, source_target_pairs={{0,16},{4,20},{8,24},{12,28},{16,0},{20,4},{24,8},{28,12},{1,17},{... | collective-permute-start | bytes 3342344 | tf_op jit(solution)/shard_map/ppermute | solution.py:593
  21.8 101.9 %copy-start.5 = (s32[8]{0:T(128)S(1)}, s32[8]{0:T(128)}, u32[]{:S(2)}) copy-start(s32[8]{0:T(128)} %param.21) | copy-start | bytes 100
  21.9 101.9 %copy-start.6 = (s32[8]{0:T(128)S(1)}, s32[8]{0:T(128)}, u32[]{:S(2)}) copy-start(s32[8]{0:T(128)} %param.20) | copy-start | bytes 100
  21.9 104.0 %copy-start.4 = (s32[8,2]{0,1:T(2,128)S(1)}, s32[8,2]{0,1:T(2,128)}, u32[]{:S(2)}) copy-start(s32[8,2]{0,1:T(2,128)} %param.22) | copy-start | bytes 196
  21.9 107.4 %copy-start.3 = (s32[4]{0:T(128)S(1)}, s32[4]{0:T(128)}, u32[]{:S(2)}) copy-start(s32[4]{0:T(128)} %param.23) | copy-start | bytes 52
  21.9 108.6 %copy-start.2 = (f32[8,7]{1,0:T(8,128)S(1)}, f32[8,7]{1,0:T(8,128)}, u32[]{:S(2)}) copy-start(f32[8,7]{1,0:T(8,128)} %param.19) | copy-start | bytes 676
  21.9 72.0 %collective-permute-start.8 = (s16[14,272,128]{2,1,0:T(8,128)(2,1)}, s16[14,272,128]{2,1,0:T(8,128)(2,1)}, u32[]{:S(2)}, u32[]{:S(2)}) collective-permute-start(s16[14,272,128]{2,1,0:T(8,128)(2,1)} %get-tuple-element.23), channel_id=1, source_target_pairs={{0,1},{1,2},{2,3},{4,5},{5,6},{6,7},{8,9},{9,10},{10,11},{12,13},{... | collective-permute-start | bytes 2924552 | tf_op jit(solution)/shard_map/ppermute | solution.py:584
  89.9 61.8 %collective-permute-start.9 = (s16[14,272,128]{2,1,0:T(8,128)(2,1)}, s16[14,272,128]{2,1,0:T(8,128)(2,1)}, u32[]{:S(2)}, u32[]{:S(2)}) collective-permute-start(s16[14,272,128]{2,1,0:T(8,128)(2,1)} %get-tuple-element.24), channel_id=1, source_target_pairs={{1,0},{2,1},{3,2},{5,4},{6,5},{7,6},{9,8},{10,9},{11,10},{13,12},{... | collective-permute-start | bytes 2924552 | tf_op jit(solution)/shard_map/ppermute | solution.py:585
  93.9 79.2 %collective-permute-start.6 = (s16[14,272,128]{2,1,0:T(8,128)(2,1)}, s16[14,272,128]{2,1,0:T(8,128)(2,1)}, u32[]{:S(2)}, u32[]{:S(2)}) collective-permute-start(s16[14,272,128]{2,1,0:T(8,128)(2,1)} %get-tuple-element.21), channel_id=1, source_target_pairs={{0,1},{1,2},{2,3},{4,5},{5,6},{6,7},{8,9},{9,10},{10,11},{12,13},{... | collective-permute-start | bytes 2924552 | tf_op jit(solution)/shard_map/ppermute | solution.py:622
  113.8 59.4 %collective-permute-start.7 = (s16[14,272,128]{2,1,0:T(8,128)(2,1)}, s16[14,272,128]{2,1,0:T(8,128)(2,1)}, u32[]{:S(2)}, u32[]{:S(2)}) collective-permute-start(s16[14,272,128]{2,1,0:T(8,128)(2,1)} %get-tuple-element.22), channel_id=1, source_target_pairs={{1,0},{2,1},{3,2},{5,4},{6,5},{7,6},{9,8},{10,9},{11,10},{13,12},{... | collective-permute-start | bytes 2924552 | tf_op jit(solution)/shard_map/ppermute | solution.py:623
  117.7 13.5 %copy-start = (s16[25,272,128]{2,1,0:T(8,128)(2,1)}, s16[25,272,128]{2,1,0:T(8,128)(2,1)S(1)}, u32[]{:S(2)}) copy-start(s16[25,272,128]{2,1,0:T(8,128)(2,1)S(1)} %collective-permute-done.1.refs_6_.refs_5_.refs_7_) | copy-start | bytes 5222404
  117.7 76.2 %collective-permute-start.2 = (s16[13,272,128]{2,1,0:T(8,128)(2,1)}, s16[13,272,128]{2,1,0:T(8,128)(2,1)}, u32[]{:S(2)}, u32[]{:S(2)}) collective-permute-start(s16[13,272,128]{2,1,0:T(8,128)(2,1)} %get-tuple-element.18), channel_id=1, source_target_pairs={{0,1},{1,2},{2,3},{4,5},{5,6},{6,7},{8,9},{9,10},{10,11},{12,13},{... | collective-permute-start | bytes 2715656 | tf_op jit(solution)/shard_map/ppermute | solution.py:622
  122.4 8.8 %copy-start.1 = (s16[25,272,128]{2,1,0:T(8,128)(2,1)}, s16[25,272,128]{2,1,0:T(8,128)(2,1)S(1)}, u32[]{:S(2)}) copy-start(s16[25,272,128]{2,1,0:T(8,128)(2,1)S(1)} %collective-permute-done.3.refs_7_.refs_9_) | copy-start | bytes 5222404
  122.4 71.5 %collective-permute-start.4 = (s16[13,272,128]{2,1,0:T(8,128)(2,1)}, s16[13,272,128]{2,1,0:T(8,128)(2,1)}, u32[]{:S(2)}, u32[]{:S(2)}) collective-permute-start(s16[13,272,128]{2,1,0:T(8,128)(2,1)} %get-tuple-element.20), channel_id=1, source_target_pairs={{1,0},{2,1},{3,2},{5,4},{6,5},{7,6},{9,8},{10,9},{11,10},{13,12},{... | collective-permute-start | bytes 2715656 | tf_op jit(solution)/shard_map/ppermute | solution.py:623
  215.5 9.5 %collective-permute-start.10 = (f32[8,64,128]{2,1,0:T(8,128)}, f32[8,64,128]{2,1,0:T(8,128)S(1)}, u32[]{:S(2)}, u32[]{:S(2)}) collective-permute-start(f32[8,64,128]{2,1,0:T(8,128)} %get-tuple-element.26), channel_id=1, source_target_pairs={{0,4},{4,8},{8,12},{12,0},{16,20},{20,24},{24,28},{28,16},{1,5},{5... | collective-permute-start | bytes 786440 | tf_op jit(solution)/shard_map/ppermute | solution.py:647
  218.2 9.4 %collective-permute-start.11 = (f32[8,64,128]{2,1,0:T(8,128)}, f32[8,64,128]{2,1,0:T(8,128)S(1)}, u32[]{:S(2)}, u32[]{:S(2)}) collective-permute-start(f32[8,64,128]{2,1,0:T(8,128)} %get-tuple-element.27), channel_id=1, source_target_pairs={{0,8},{4,12},{8,0},{12,4},{16,24},{20,28},{24,16},{28,20},{1,9},{5... | collective-permute-start | bytes 786440 | tf_op jit(solution)/shard_map/ppermute | solution.py:647
  218.2 13.3 %collective-permute-start.12 = (f32[8,64,128]{2,1,0:T(8,128)}, f32[8,64,128]{2,1,0:T(8,128)S(1)}, u32[]{:S(2)}, u32[]{:S(2)}) collective-permute-start(f32[8,64,128]{2,1,0:T(8,128)} %get-tuple-element.28), channel_id=1, source_target_pairs={{0,12},{4,0},{8,4},{12,8},{16,28},{20,16},{24,20},{28,24},{1,13},{... | collective-permute-start | bytes 786440 | tf_op jit(solution)/shard_map/ppermute | solution.py:647

commit v3 on v2

--- a/solution.py
+++ b/solution.py
@@ -9,6 +9,9 @@
 PAD = 8
 EDGE = 16
 LANES = 128
+BY_MATRIX = ((True, False), (True, True))
+CHUNK = 32
+VMEM_OF_PASS = 67043328
 WIRE = jnp.int16
 STEPS_OF_SCALE = (32, 16, 8, 4, 2, 1)
 FIXED = 65536.0
@@ -28,6 +31,7 @@
 
 def stencil_step(src, dst, coefs, lo, hi, rows, beside, sums, surface=None):
     centre, hor, vel = coefs
+    by_matrix = BY_MATRIX[surface is not None]
 
     def vertical_sums(x, j):
         for r0, size in spans(rows, 144):
@@ -39,33 +43,44 @@
                 preferred_element_type=jnp.float32,
             )
 
-    def one_layer(x, j):
-        for r0, size in spans(rows, 32):
+    def ahead(x):
+        for j in range(2):
+            if by_matrix[j]:
+                vertical_sums(x + j, j)
+
+    def body(i, carry):
+        x = lo + 2 * i
+        shifts = [None, None] if surface is None else [surface[1](x), surface[1](x + 1)]
+        for r0, size in spans(rows, CHUNK):
             at = pl.ds(PAD + r0, size)
             here = pl.ds(r0, size)
-            lateral = src[x - 1, at, :] + src[x + 1, at, :]
-            lateral = lateral + src[x, pl.ds(PAD + r0 - 1, size), :]
-            lateral = lateral + src[x, pl.ds(PAD + r0 + 1, size), :]
-            vertical = sums[j, here, :]
-            if surface is not None:
-                lane = lax.broadcasted_iota(jnp.int32, (size, LANES), 1)
-                plane, shift = surface[1](x)
-                data = pltpu.roll(surface[0][plane, here, :], shift, 1)
-                vertical = vertical + jnp.where(lane == 0, data, 0.0)
-            new = centre[x, here, :] * src[x, at, :] - dst[x, at, :]
-            new = new + hor[x, here, :] * lateral
-            new = new + vel[x, here, :] * vertical
-            dst[x, at, :] = new
-
-    def body(i, carry):
-        x = lo + 2 * i
-        vertical_sums(x + 1, 1)
-        one_layer(x, 0)
-        vertical_sums(x + 2, 0)
-        one_layer(x + 1, 1)
+            lane = lax.broadcasted_iota(jnp.int32, (size, LANES), 1)
+            c = [src[x - 1 + j, at, :] for j in range(4)]
+            for j in range(2):
+                mid = c[j + 1]
+                lateral = c[j] + c[j + 2]
+                lateral = lateral + src[x + j, pl.ds(PAD + r0 - 1, size), :]
+                lateral = lateral + src[x + j, pl.ds(PAD + r0 + 1, size), :]
+                data = 0.0
+                if surface is not None:
+                    plane, shift = shifts[j]
+                    data = pltpu.roll(surface[0][plane, here, :], shift, 1)
+                if by_matrix[j]:
+                    vertical = sums[j, here, :]
+                    if surface is not None:
+                        vertical = vertical + jnp.where(lane == 0, data, 0.0)
+                else:
+                    above = jnp.where(lane == 0, data, pltpu.roll(mid, 1, 1))
+                    deeper = jnp.where(lane == LANES - 1, 0.0, pltpu.roll(mid, LANES - 1, 1))
+                    vertical = above + deeper
+                new = centre[x + j, here, :] * mid - dst[x + j, at, :]
+                new = new + hor[x + j, here, :] * lateral
+                new = new + vel[x + j, here, :] * vertical
+                dst[x + j, at, :] = new
+        ahead(jnp.minimum(x + 2, hi - 2))
         return carry
 
-    vertical_sums(lo, 0)
+    ahead(lo)
     lax.fori_loop(0, (hi - lo) // 2, body, 0)
 
 
@@ -110,8 +125,8 @@
     return slot, found > 0
 
 
-def wave_pass(kind, field, field_at, vel, ani, left, right, halo_at, ints, amps, half_rows, reach,
-              n_snaps, blocks=1, others=(), data=None):
+def wave_pass(kind, field, field_at, vel, ani, left, right, halo_at, shot, ints, amps, half_rows, reach,
+              n_snaps, blocks=1, others=(), data=None, model=None):
     width, all_rows, depth_cells = vel.shape
     rows = half_rows + EDGE
     layers = width + 2 * reach
@@ -119,7 +134,9 @@
     backward = kind in ("waves", "image")
     packed = not isinstance(field, tuple)
     fields = [field] if packed else list(field) + ([data] if backward else [])
-    depths = (reach, near, near, near) + ((1,) if backward else ())
+    first_pass = model is None
+    depths = (reach, near) + ((near, near) if first_pass else ()) + ((1,) if backward else ())
+    inputs_m = [vel, ani] if first_pass else list(model)
     n_side = len(left)
 
     def kernel(*refs):
@@ -127,8 +144,8 @@
         pos = 2
         field_refs = refs[pos : pos + len(fields)]
         pos += len(fields)
-        vel_ref, ani_ref = refs[pos : pos + 2]
-        pos += 2
+        model_refs = refs[pos : pos + len(inputs_m)]
+        pos += len(inputs_m)
         left_refs = refs[pos : pos + n_side]
         pos += n_side
         right_refs = refs[pos : pos + n_side]
@@ -136,27 +153,37 @@
         other_hbm = refs[pos : pos + len(others)]
         pos += len(others)
         n_out = blocks if kind == "blocks" else 1
+        n_model = 3 if first_pass else 0
         outs = refs[pos : pos + n_out]
         pos += n_out
+        model_outs = refs[pos : pos + n_model]
+        pos += n_model
         buf_a, buf_b, v_buf, h_buf, c_buf, stage_l, stage_r, stage_t, top, beside, sums, sem = refs[
             pos : pos + 12
         ]
+        model_bufs = (c_buf, h_buf, v_buf)
 
         steps = [ints_ref[k] for k in range(n_snaps)]
-        first_row, skip, inside, source_x, source_y, place = [
-            ints_ref[n_snaps + k] for k in range(6)
+        first_row, skip, place = [ints_ref[n_snaps + k] for k in range(3)]
+        inside, source_x, source_y = [
+            ints_ref[n_snaps + 3 + 2 * k + shot] for k in range(3)
         ]
         window = pl.ds(pl.multiple_of(first_row, 8), rows)
         inner = pl.ds(PAD, rows)
 
-        tile_copies = [
-            pltpu.make_async_copy(
-                vel_ref.at[:, window], v_buf.at[pl.ds(reach, width)], sem.at[0]
-            ),
-            pltpu.make_async_copy(
-                ani_ref.at[:, window], h_buf.at[pl.ds(reach, width)], sem.at[1]
-            ),
-        ]
+        tile_copies = []
+        if first_pass:
+            tile_copies = [
+                pltpu.make_async_copy(
+                    ref.at[:, window], buf.at[pl.ds(reach, width)], sem.at[n]
+                )
+                for n, (ref, buf) in enumerate(zip(model_refs, (v_buf, h_buf)))
+            ]
+        else:
+            tile_copies = [
+                pltpu.make_async_copy(ref, buf, sem.at[18 + n])
+                for n, (ref, buf) in enumerate(zip(model_refs, model_bufs))
+            ]
         side_copies = []
         where = 0
         offsets = []
@@ -201,7 +228,10 @@
             pltpu.make_async_copy(source, target, sem.at[15 + n])
             for n, (source, target) in enumerate(zip(other_hbm, other_refs))
         ]
-        for copy in tile_copies + side_copies + field_copies + other_copies:
+        in_order = tile_copies + side_copies + field_copies
+        if not first_pass:
+            in_order = side_copies + field_copies + tile_copies
+        for copy in in_order + other_copies:
             copy.start()
         beside[...] = neighbour_matrix()
         zeros = jnp.zeros((layers, PAD, LANES), jnp.float32)
@@ -224,13 +254,15 @@
         for stage, starts in ((stage_l, (0, 1, 1, 1)), (stage_r, (reach + width,) * 4)):
             scale = decode_scale(stage, offsets[0], first_row, half_rows)
             side_scales.append(scale)
+            targets = (buf_a, buf_b) + ((v_buf, h_buf) if first_pass else ())
             for dst, at, start, depth, row0, unit in zip(
-                (buf_a, buf_b, v_buf, h_buf), offsets, starts, depths, (PAD, PAD, 0, 0),
+                targets, offsets, starts, depths, (PAD, PAD, 0, 0),
                 (scale, scale, 1.0 / FIXED, 1.0 / FIXED),
             ):
                 widen(stage, at, dst, start, depth, row0, unit)
-        for copy in tile_copies:
-            copy.wait()
+        if first_pass:
+            for copy in tile_copies:
+                copy.wait()
 
         def coefficients(x, carry):
             for r0, size in spans(rows, 64):
@@ -241,7 +273,19 @@
                 c_buf[x, at, :] = 2.0 - (4.0 * h + 2.0 * v)
             return carry
 
-        lax.fori_loop(1, layers - 1, coefficients, 0)
+        model_copies = []
+        if first_pass:
+            edge = jnp.zeros((rows, LANES), jnp.float32)
+            for buf in model_bufs:
+                buf[0] = edge
+                buf[layers - 1] = edge
+            lax.fori_loop(1, layers - 1, coefficients, 0)
+            model_copies = [
+                pltpu.make_async_copy(buf, out, sem.at[18 + n])
+                for n, (buf, out) in enumerate(zip(model_bufs, model_outs))
+            ]
+            for copy in model_copies:
+                copy.start()
         for copy in field_copies:
             copy.wait()
         if packed:
@@ -250,14 +294,14 @@
             widen(stage_t, field_at[1], buf_b, reach, width, PAD, scale)
         surface = None
         if backward:
-            widen(stage_l, offsets[4], top, 0, 1, 0, side_scales[0])
+            widen(stage_l, offsets[-1], top, 0, 1, 0, side_scales[0])
             if packed:
                 widen(stage_t, field_at[2], top, 1, 1, 0, scale)
             else:
                 turned = refs[-1]
                 turned[...] = flat[...].T
                 top[1] = turned[window, :]
-            widen(stage_r, offsets[4], top, 2, 1, 0, side_scales[1])
+            widen(stage_r, offsets[-1], top, 2, 1, 0, side_scales[1])
 
         if kind in ("image", "blocks"):
             image = outs[0] if kind == "image" else refs[-1]
@@ -289,6 +333,9 @@
 
         src, dst = buf_a, buf_b
         coefs = (c_buf, h_buf, v_buf)
+        if not first_pass:
+            for copy in tile_copies:
+                copy.wait()
         for copy in other_copies:
             copy.wait()
         record(src, reach + 1 if backward else 1)
@@ -313,12 +360,14 @@
                     base = pl.multiple_of((source_y // 8) * 8, 8)
                     at = pl.ds(pl.multiple_of(base + PAD, 8), 8)
                     mask = (row8 == source_y - base) & (lane8 == 0)
-                    add = v_buf[source_x, pl.ds(base, 8), :] * amps_ref[step - 1]
+                    add = v_buf[source_x, pl.ds(base, 8), :] * amps_ref[shot * reach + step - 1]
                     dst[source_x, at, :] = dst[source_x, at, :] + jnp.where(mask, add, 0.0)
 
             src, dst = dst, src
             record(src, reach + 1 - step if backward else step + 1)
 
+        for copy in model_copies:
+            copy.wait()
         if kind == "blocks":
             block = half_rows // blocks
             for d, out in enumerate(outs):
@@ -331,7 +380,7 @@
 
                 lax.fori_loop(0, width, cut, 0)
 
-    any_spec = pl.BlockSpec(memory_space=pl.ANY)
+    any_spec = pl.BlockSpec(memory_space=pltpu.HBM)
     smem = pl.BlockSpec(memory_space=pltpu.SMEM)
     vmem = pl.BlockSpec(memory_space=pltpu.VMEM)
     shape = (width, half_rows, depth_cells)
@@ -342,6 +391,9 @@
     else:
         dtype = jnp.bfloat16 if kind == "snaps" else jnp.float32
         out_shape = (jax.ShapeDtypeStruct((n_snaps,) + shape, dtype),)
+    n_model = 3 if first_pass else 0
+    if first_pass:
+        out_shape += (jax.ShapeDtypeStruct((layers, rows, depth_cells), jnp.float32),) * 3
     cells = layers * rows * depth_cells
     grid_buf = pltpu.VMEM((layers, rows, depth_cells), jnp.float32)
     field_buf = pltpu.VMEM((layers, rows + 2 * PAD, depth_cells), jnp.float32)
@@ -350,15 +402,17 @@
     return pl.pallas_call(
         kernel,
         out_shape=out_shape,
-        in_specs=[smem, smem] + [any_spec] * (len(fields) + 2 + 2 * n_side + len(others)),
-        out_specs=(vmem,) * len(out_shape),
+        in_specs=[smem, smem]
+        + [any_spec] * len(fields)
+        + [any_spec] * (len(inputs_m) + 2 * n_side + len(others)),
+        out_specs=(vmem,) * (len(out_shape) - n_model) + (any_spec,) * n_model,
         scratch_shapes=[
             field_buf, field_buf, grid_buf, grid_buf, grid_buf, side, side,
             pltpu.VMEM((stage_layers, rows, depth_cells), WIRE),
             pltpu.VMEM((3, rows, depth_cells), jnp.float32),
             pltpu.VMEM((2 * LANES, LANES), jnp.bfloat16),
             pltpu.VMEM((2, rows, depth_cells), jnp.float32),
-            pltpu.SemaphoreType.DMA((18,)),
+            pltpu.SemaphoreType.DMA((21,)),
         ]
         + [pltpu.VMEM(other.shape, other.dtype) for other in others]
         + ([pltpu.VMEM(shape, jnp.float32)] if kind == "blocks" else [])
@@ -370,11 +424,12 @@
         cost_estimate=pl.CostEstimate(
             flops=15 * cells * reach, bytes_accessed=20 * cells, transcendentals=0
         ),
-    )(ints, amps, *fields, vel, ani, *left, *right, *others)
+        compiler_params=pltpu.CompilerParams(vmem_limit_bytes=VMEM_OF_PASS),
+    )(ints, amps, *fields, *inputs_m, *left, *right, *others)
 
 
 def any_specs(n):
-    return [pl.BlockSpec(memory_space=pl.ANY)] * n
+    return [pl.BlockSpec(memory_space=pltpu.HBM)] * n
 
 
 def pack_rows(first, fields, ranges, groups, data):
@@ -592,22 +647,20 @@
     (send_u,) = pack_rows(at(their_first), (u1, u0), (whole,), ((0, 1),), None)
     import_u = lax.ppermute(send_u, "shot", across)
 
-    def numbers(shot):
-        chosen = (jnp.arange(shots, dtype=jnp.int32) == shot).astype(jnp.int32)
-        source_x = jnp.sum(chosen * shot_x) - tile * width + reach
-        source_y = jnp.sum(chosen * shot_y) - my_first
-        inside = jnp.any((chosen[:, None] > 0) & (aperture == tile)).astype(jnp.int32)
-        amps = jnp.sum(jnp.where(chosen[:, None] > 0, wavelet, 0.0), axis=0)
-        parts = jnp.stack([my_first, side * EDGE, inside, source_x, source_y, me % half])
-        return jnp.concatenate([snap_steps, parts]).astype(jnp.int32), amps
-
-    ints_me, amps_me = numbers(me)
-    ints_partner, amps_partner = numbers(partner)
+    two = jnp.stack([me, partner])
+    chosen = (jnp.arange(shots, dtype=jnp.int32)[None] == two[:, None]).astype(jnp.int32)
+    source_x = jnp.sum(chosen * shot_x[None], axis=1) - tile * width + reach
+    source_y = jnp.sum(chosen * shot_y[None], axis=1) - my_first
+    here = jnp.any(aperture == tile, axis=1).astype(jnp.int32)
+    inside = jnp.sum(chosen * here[None], axis=1)
+    amps = jnp.sum(jnp.where(chosen[:, :, None] > 0, wavelet[None], 0.0), axis=1).reshape(-1)
+    places = jnp.stack([my_first, side * EDGE, me % half])
+    ints = jnp.concatenate([snap_steps, places, inside, source_x, source_y]).astype(jnp.int32)
     common = dict(half_rows=half_rows, reach=reach, n_snaps=n_snaps)
     at_v, at_a = (0, reach + near), (0, reach + 2 * near)
-    (snaps,) = wave_pass(
+    snaps, *model = wave_pass(
         "snaps", (u1, u0), None, velocity_term, anisotropy, [left], [right],
-        ((0, 0), (0, reach), at_v, at_a), ints_me, amps_me, **common,
+        ((0, 0), (0, reach), at_v, at_a), 0, ints, amps, **common,
     )
 
     def from_sides(packed, tail):
@@ -624,22 +677,21 @@
         return from_left, from_right
 
     (waves,) = wave_pass(
-        "waves", (w8, w9), None, velocity_term, anisotropy, [left, left_l], [right, right_l],
-        ((1, 0), (1, reach), at_v, at_a, (1, reach + near)),
-        ints_partner, amps_partner, data=data, **common,
+        "waves", (w8, w9), None, velocity_term, anisotropy, [left_l], [right_l],
+        ((0, 0), (0, reach), (0, reach + near)),
+        1, ints, amps, data=data, model=model, **common,
     )
     left_w, right_w = from_sides(import_w, True)
     (image,) = wave_pass(
         "image", import_w, (0, width, 2 * width), velocity_term, anisotropy,
-        [left, left_w], [right, right_w],
-        ((1, 0), (1, reach), at_v, at_a, (1, reach + near)),
-        ints_me, amps_me, others=(snaps,), **common,
+        [left_w], [right_w], ((0, 0), (0, reach), (0, reach + near)),
+        0, ints, amps, others=(snaps,), model=model, **common,
     )
     left_u, right_u = from_sides(import_u, False)
     blocks = wave_pass(
         "blocks", import_u, (0, width), velocity_term, anisotropy,
-        [left, left_u], [right, right_u], ((1, 0), (1, reach), at_v, at_a),
-        ints_partner, amps_partner, blocks=half, others=(image, waves), **common,
+        [left_u], [right_u], ((0, 0), (0, reach)),
+        1, ints, amps, blocks=half, others=(image, waves), model=model, **common,
     )
     total = blocks[0]
     for d in range(1, half):

time: 236 us -> 225 us (0.953); the launches traced: 233 us -> 225 us
  Pallas kernels: 104 us -> 98.6 us
  waiting for transfers between devices: 88.1 us -> 93.5 us
  between operations: 4.33 us -> 0.32 us
  starting transfers between devices: 31.6 us -> 28.6 us
    pallas_call x4, Pallas kernels: 84.3 us -> 79 us  [wave_pass(): pl.pallas_call(kernel, out_shape=out_shape, in_specs=[smem, smem] + [any_...]
    ppermute x1, waiting for transfers between devices: 62.9 us -> 65.6 us  [on_device(): import_w = lax.ppermute(send_w, 'shot', across)]
    ppermute x2, starting transfers between devices: 11.2 us -> 8.81 us  [from_sides(): from_left = lax.ppermute(send_up, 'xy', up)]
  transfers between devices with their start and end apart: 13 -> 13, of which waited for: 5 -> 4; matrix products, arithmetic and copies ran while one was open for 1% -> 1% of each run, Pallas kernels for 34% -> 33%
where the time goes in v3:
time: 225 us
  Pallas kernels  98.6 us (44%)
  waiting for transfers between devices  93.5 us (42%)
  starting transfers between devices  28.6 us (13%)
    pallas_call x4, Pallas kernels, wave_pass(): pl.pallas_call(kernel, out_shape=out_shape, in_specs=[smem, smem] + [any_...  79 us
    ppermute x1, waiting for transfers between devices, on_device(): import_w = lax.ppermute(send_w, 'shot', across)  65.6 us
    ppermute x1, waiting for transfers between devices, on_device(): import_u = lax.ppermute(send_u, 'shot', across)  15.2 us
    pallas_call x4, Pallas kernels, pack_rows(): pl.pallas_call(kernel, out_shape=tuple((jax.ShapeDtypeStruct((m, rows, de...  14.5 us
    ppermute x3, waiting for transfers between devices, on_device(): arrived = lax.ppermute(blocks[d], 'shot', route)  12.7 us
    ppermute x2, starting transfers between devices, from_sides(): from_left = lax.ppermute(send_up, 'xy', up)  8.81 us
    ppermute x2, starting transfers between devices, sides(): from_left = lax.ppermute(send_up, 'xy', up)  6.67 us
    pallas_call x2, Pallas kernels, repack(): pl.pallas_call(kernel, out_shape=tuple((jax.ShapeDtypeStruct((m,) + packe...  5.13 us
  transfers between devices with their start and end apart: 13, of which 4 were waited for; matrix products, arithmetic and copies ran while one was open for 1% of the time, Pallas kernels for 33%

profile of v3, /device:TPU:0, one launch (start us, length us, event | category | flops | bytes accessed | tf_op | source)
XLA Modules:
  0.0 224.7 jit_solution(10760911950493519981)
XLA Ops:
  0.0 4.0 %pack_rows.5 = (s16[25,272,128]{2,1,0:T(8,128)(2,1)}, s16[25,272,128]{2,1,0:T(8,128)(2,1)}) custom-call(s32[1]{0:T(128)} %bitcast.first_ref, f32[8,512,128]{2,1,0:T(8,128)} %bitcast.11, f32[8,512,128]{2,1,0:T(8,128)} %bitcast.14, f32[8,512,128]{2,1,0:T(8,128)} %refs_4_.1, f32[8,512,128]{2,1,0:T(8,128)} %refs_5_.1), custom_call_target="tpu_custom_call" | custom-call | flops 1114112 | bytes 8912896 | tf_op jit(solution)/shard_map/pack_rows/pallas_call | solution.py:535
  4.0 3.6 %collective-permute-start.1 = (s16[25,272,128]{2,1,0:T(8,128)(2,1)}, s16[25,272,128]{2,1,0:T(8,128)(2,1)}, u32[]{:S(2)}, u32[]{:S(2)}) collective-permute-start(s16[25,272,128]{2,1,0:T(8,128)(2,1)} %get-tuple-element.21), channel_id=1, source_target_pairs={{0,1},{1,2},{2,3},{4,5},{5,6},{6,7},{8,9},{9,10},{10,11},{12,13},{... | collective-permute-start | bytes 5222408 | tf_op jit(solution)/shard_map/ppermute | solution.py:639
  7.6 1.3 collective-permute-start.2
  8.9 3.5 %pack_rows.6 = s16[17,272,128]{2,1,0:T(8,128)(2,1)} custom-call(s32[1]{0:T(128)} %bitcast.5.first_ref, f32[8,512,128]{2,1,0:T(8,128)} %bitcast.17, f32[8,512,128]{2,1,0:T(8,128)} %bitcast.20, f32[56,512]{1,0:T(8,128)} %bitcast.23), custom_call_target="tpu_custom_call" | custom-call | flops 557056 | bytes 4456448 | tf_op jit(solution)/shard_map/pack_rows/pallas_call | solution.py:535
  12.4 3.5 %collective-permute-start.5 = (s16[17,272,128]{2,1,0:T(8,128)(2,1)}, s16[17,272,128]{2,1,0:T(8,128)(2,1)S(1)}, u32[]{:S(2)}, u32[]{:S(2)}) collective-permute-start(s16[17,272,128]{2,1,0:T(8,128)(2,1)} %pack_rows.6), channel_id=1, source_target_pairs={{0,16},{4,20},{8,24},{12,28},{16,0},{20,4},{24,8},{28,12},{1,17},{... | collective-permute-start | bytes 3551240 | tf_op jit(solution)/shard_map/ppermute | solution.py:628
  15.9 3.3 %pack_rows.4 = s16[16,272,128]{2,1,0:T(8,128)(2,1)} custom-call(s32[1]{0:T(128)} %bitcast.5.first_ref, f32[8,512,128]{2,1,0:T(8,128)} %bitcast.12, f32[8,512,128]{2,1,0:T(8,128)} %bitcast.15), custom_call_target="tpu_custom_call" | custom-call | flops 557056 | bytes 4456448 | tf_op jit(solution)/shard_map/pack_rows/pallas_call | solution.py:535
  19.2 0.1 collective-permute-start
  19.3 3.7 %pack_rows.7 = (s16[14,272,128]{2,1,0:T(8,128)(2,1)}, s16[14,272,128]{2,1,0:T(8,128)(2,1)}) custom-call(s32[1]{0:T(128)} %bitcast.first_ref, f32[8,512,128]{2,1,0:T(8,128)} %bitcast.18, f32[8,512,128]{2,1,0:T(8,128)} %bitcast.21, f32[56,512]{1,0:T(8,128)} %bitcast.24), custom_call_target="tpu_custom_call" | custom-call | flops 557056 | bytes 4456448 | tf_op jit(solution)/shard_map/pack_rows/pallas_call | solution.py:535
  23.0 0.0 copy-start.4
  23.0 0.0 copy-start.3
  23.0 0.0 copy-start.5
  23.0 0.0 copy-start.6
  23.0 0.0 copy-start.7
  23.1 3.1 %collective-permute-start.8 = (s16[14,272,128]{2,1,0:T(8,128)(2,1)}, s16[14,272,128]{2,1,0:T(8,128)(2,1)S(1)}, u32[]{:S(2)}, u32[]{:S(2)}) collective-permute-start(s16[14,272,128]{2,1,0:T(8,128)(2,1)} %get-tuple-element.31), channel_id=1, source_target_pairs={{0,1},{1,2},{2,3},{4,5},{5,6},{6,7},{8,9},{9,10},{10,11},{12,13},{... | collective-permute-start | bytes 2924552 | tf_op jit(solution)/shard_map/ppermute | solution.py:639
  26.1 65.6 %collective-permute-done.5.packed_ref.refs_2_ = s16[17,272,128]{2,1,0:T(8,128)(2,1)S(1)} collective-permute-done((s16[17,272,128]{2,1,0:T(8,128)(2,1)}, s16[17,272,128]{2,1,0:T(8,128)(2,1)S(1)}, u32[]{:S(2)}, u32[]{:S(2)}) %collective-permute-start.5) | collective-permute-done | bytes 1183776 | tf_op jit(solution)/shard_map/ppermute | solution.py:628
  91.7 1.3 collective-permute-start.9
  93.0 2.6 %repack.3 = (s16[14,272,128]{2,1,0:T(8,128)(2,1)}, s16[14,272,128]{2,1,0:T(8,128)(2,1)}) custom-call(s16[17,272,128]{2,1,0:T(8,128)(2,1)} %copy-done), custom_call_target="tpu_custom_call" | custom-call | bytes 3551232 | tf_op jit(solution)/shard_map/repack/pallas_call | solution.py:571
  95.6 0.0 collective-permute-done.8.refs_8_
  95.6 4.8 %collective-permute-start.6 = (s16[14,272,128]{2,1,0:T(8,128)(2,1)}, s16[14,272,128]{2,1,0:T(8,128)(2,1)}, u32[]{:S(2)}, u32[]{:S(2)}) collective-permute-start(s16[14,272,128]{2,1,0:T(8,128)(2,1)} %get-tuple-element.28), channel_id=1, source_target_pairs={{0,1},{1,2},{2,3},{4,5},{5,6},{6,7},{8,9},{9,10},{10,11},{12,13},{... | collective-permute-start | bytes 2924552 | tf_op jit(solution)/shard_map/ppermute | solution.py:675
  100.4 15.2 %collective-permute-done.packed_ref.refs_2_ = s16[16,272,128]{2,1,0:T(8,128)(2,1)S(1)} collective-permute-done((s16[16,272,128]{2,1,0:T(8,128)(2,1)}, s16[16,272,128]{2,1,0:T(8,128)(2,1)S(1)}, u32[]{:S(2)}, u32[]{:S(2)}) %collective-permute-start) | collective-permute-done | bytes 1114144 | tf_op jit(solution)/shard_map/ppermute | solution.py:648
  115.6 1.3 collective-permute-start.7
  116.9 2.5 %repack.2 = (s16[13,272,128]{2,1,0:T(8,128)(2,1)}, s16[13,272,128]{2,1,0:T(8,128)(2,1)}) custom-call(s16[16,272,128]{2,1,0:T(8,128)(2,1)} %copy-done.1), custom_call_target="tpu_custom_call" | custom-call | bytes 3342336 | tf_op jit(solution)/shard_map/repack/pallas_call | solution.py:571
  119.4 4.0 %collective-permute-start.3 = (s16[13,272,128]{2,1,0:T(8,128)(2,1)}, s16[13,272,128]{2,1,0:T(8,128)(2,1)}, u32[]{:S(2)}, u32[]{:S(2)}) collective-permute-start(s16[13,272,128]{2,1,0:T(8,128)(2,1)} %get-tuple-element.26), channel_id=1, source_target_pairs={{0,1},{1,2},{2,3},{4,5},{5,6},{6,7},{8,9},{9,10},{10,11},{12,13},{... | collective-permute-start | bytes 2715656 | tf_op jit(solution)/shard_map/ppermute | solution.py:675
  123.5 0.0 collective-permute-done.2.refs_7_
  123.5 1.3 collective-permute-start.4
  124.8 0.1 copy.13
  124.9 0.1 pad_add_fusion
  125.0 0.1 convert_compare_fusion
  125.1 0.1 select_reduce_fusion
  125.2 0.1 copy.14
  125.3 0.6 reshape.38.refs_1_
  125.9 0.2 select_reduce_fusion.1
  126.1 0.7 concatenate.3.refs_0_
  126.8 17.7 %shard_map.118 = (bf16[4,8,256,128]{3,2,1,0:T(8,128)(2,1)}, f32[22,272,128]{2,1,0:T(8,128)}, f32[22,272,128]{2,1,0:T(8,128)}, f32[22,272,128]{2,1,0:T(8,128)}) custom-call(s32[13]{0:T(128)} %concatenate.3.refs_0_, f32[14]{0:T(128)} %reshape.38.refs_1_, f32[8,512,128]{2,1,0:T(8,128)} %bitcast.13, f32[8,512,128]{2,1,0:T(8,128)} %bitcast.16, ...), custom_call_target="tpu_custom_call" | custom-call | flops 80424960 | bytes 15319040 | tf_op jit(solution)/shard_map/pallas_call | solution.py:402
  144.5 0.0 collective-permute-done.9.refs_9_
  144.5 21.2 %shard_map.120.refs_9_ = f32[4,8,256,128]{3,2,1,0:T(8,128)} custom-call(s32[13]{0:T(128)} %concatenate.3.refs_0_, f32[14]{0:T(128)} %reshape.38.refs_1_, f32[8,512,128]{2,1,0:T(8,128)} %bitcast.19, f32[8,512,128]{2,1,0:T(8,128)} %bitcast.22, f32[56,512]{1,0:T(8,128)} %bitcast.25, f32[22,272,128]{2,1,0:T(8,128)} %get-tuple-element.23.refs_3_.refs_5_, ...), custom_call_target="tpu_custom_call" | custom-call | flops 80424960 | bytes 15319040 | tf_op jit(solution)/shard_map/pallas_call | solution.py:402
  165.7 0.0 collective-permute-done.7.refs_7_
  165.7 20.3 %shard_map.119.refs_8_ = f32[8,256,128]{2,1,0:T(8,128)} custom-call(s32[13]{0:T(128)} %concatenate.3.refs_0_, f32[14]{0:T(128)} %reshape.38.refs_1_, s16[17,272,128]{2,1,0:T(8,128)(2,1)} %copy-done, f32[22,272,128]{2,1,0:T(8,128)} %get-tuple-element.23.refs_3_.refs_5_, f32[22,272,128]{2,1,0:T(8,128)} %get-tuple-element.24.refs_4_.refs_6_, ...), custom_call_target="tpu_custom_call" | custom-call | flops 80424960 | bytes 15319040 | tf_op jit(solution)/shard_map/pallas_call | solution.py:402
  186.1 0.0 collective-permute-done.3.refs_6_
  186.1 0.0 collective-permute-done.4.refs_7_
  186.1 19.8 %shard_map.121 = (f32[8,64,128]{2,1,0:T(8,128)}, f32[8,64,128]{2,1,0:T(8,128)}, f32[8,64,128]{2,1,0:T(8,128)}, f32[8,64,128]{2,1,0:T(8,128)}) custom-call(s32[13]{0:T(128)} %concatenate.3.refs_0_, f32[14]{0:T(128)} %reshape.38.refs_1_, s16[16,272,128]{2,1,0:T(8,128)(2,1)} %copy-done.1, f32[22,272,128]{2,1,0:T(8,128)} %get-tuple-element.23.refs_3_.refs_5_, ...), custom_call_target="tpu_custom_call" | custom-call | flops 80424960 | bytes 15319040 | tf_op jit(solution)/shard_map/pallas_call | solution.py:402
  205.8 1.6 collective-permute-start.12
  207.5 2.8 %collective-permute-start.11 = (f32[8,64,128]{2,1,0:T(8,128)}, f32[8,64,128]{2,1,0:T(8,128)S(1)}, u32[]{:S(2)}, u32[]{:S(2)}) collective-permute-start(f32[8,64,128]{2,1,0:T(8,128)} %get-tuple-element.35), channel_id=1, source_target_pairs={{0,8},{4,12},{8,0},{12,4},{16,24},{20,28},{24,16},{28,20},{1,9},{5... | collective-permute-start | bytes 786440 | tf_op jit(solution)/shard_map/ppermute | solution.py:699
  210.3 0.0 collective-permute-start.10
  210.3 5.8 %collective-permute-done.12 = f32[8,64,128]{2,1,0:T(8,128)S(1)} collective-permute-done((f32[8,64,128]{2,1,0:T(8,128)}, f32[8,64,128]{2,1,0:T(8,128)S(1)}, u32[]{:S(2)}, u32[]{:S(2)}) %collective-permute-start.12) | collective-permute-done | bytes 262176 | tf_op jit(solution)/shard_map/ppermute | solution.py:699
  216.1 6.8 %collective-permute-done.11 = f32[8,64,128]{2,1,0:T(8,128)S(1)} collective-permute-done((f32[8,64,128]{2,1,0:T(8,128)}, f32[8,64,128]{2,1,0:T(8,128)S(1)}, u32[]{:S(2)}, u32[]{:S(2)}) %collective-permute-start.11) | collective-permute-done | bytes 262176 | tf_op jit(solution)/shard_map/ppermute | solution.py:699
  223.0 0.0 collective-permute-done.10
  223.0 1.7 add_add_fusion
  (16 shorter events, 0.1 us)
Async XLA Ops:
  4.0 115.4 %collective-permute-start.1 = (s16[25,272,128]{2,1,0:T(8,128)(2,1)}, s16[25,272,128]{2,1,0:T(8,128)(2,1)}, u32[]{:S(2)}, u32[]{:S(2)}) collective-permute-start(s16[25,272,128]{2,1,0:T(8,128)(2,1)} %get-tuple-element.21), channel_id=1, source_target_pairs={{0,1},{1,2},{2,3},{4,5},{5,6},{6,7},{8,9},{9,10},{10,11},{12,13},{... | collective-permute-start | bytes 5222408 | tf_op jit(solution)/shard_map/ppermute | solution.py:639
  7.6 115.9 %collective-permute-start.2 = (s16[25,272,128]{2,1,0:T(8,128)(2,1)}, s16[25,272,128]{2,1,0:T(8,128)(2,1)}, u32[]{:S(2)}, u32[]{:S(2)}) collective-permute-start(s16[25,272,128]{2,1,0:T(8,128)(2,1)} %get-tuple-element.22), channel_id=1, source_target_pairs={{1,0},{2,1},{3,2},{5,4},{6,5},{7,6},{9,8},{10,9},{11,10},{13,12},{... | collective-permute-start | bytes 5222408 | tf_op jit(solution)/shard_map/ppermute | solution.py:640
  12.4 79.3 %collective-permute-start.5 = (s16[17,272,128]{2,1,0:T(8,128)(2,1)}, s16[17,272,128]{2,1,0:T(8,128)(2,1)S(1)}, u32[]{:S(2)}, u32[]{:S(2)}) collective-permute-start(s16[17,272,128]{2,1,0:T(8,128)(2,1)} %pack_rows.6), channel_id=1, source_target_pairs={{0,16},{4,20},{8,24},{12,28},{16,0},{20,4},{24,8},{28,12},{1,17},{... | collective-permute-start | bytes 3551240 | tf_op jit(solution)/shard_map/ppermute | solution.py:628
  19.2 96.4 %collective-permute-start = (s16[16,272,128]{2,1,0:T(8,128)(2,1)}, s16[16,272,128]{2,1,0:T(8,128)(2,1)S(1)}, u32[]{:S(2)}, u32[]{:S(2)}) collective-permute-start(s16[16,272,128]{2,1,0:T(8,128)(2,1)} %pack_rows.4), channel_id=1, source_target_pairs={{0,16},{4,20},{8,24},{12,28},{16,0},{20,4},{24,8},{28,12},{1,17},{... | collective-permute-start | bytes 3342344 | tf_op jit(solution)/shard_map/ppermute | solution.py:648
  23.0 101.8 %copy-start.4 = (s32[8,2]{0,1:T(2,128)S(1)}, s32[8,2]{0,1:T(2,128)}, u32[]{:S(2)}) copy-start(s32[8,2]{0,1:T(2,128)} %param.22) | copy-start | bytes 196
  23.0 101.8 %copy-start.3 = (f32[8,7]{1,0:T(8,128)S(1)}, f32[8,7]{1,0:T(8,128)}, u32[]{:S(2)}) copy-start(f32[8,7]{1,0:T(8,128)} %param.19) | copy-start | bytes 676
  23.0 102.8 %copy-start.5 = (s32[8]{0:T(128)S(1)}, s32[8]{0:T(128)}, u32[]{:S(2)}) copy-start(s32[8]{0:T(128)} %param.21) | copy-start | bytes 100
  23.0 102.8 %copy-start.6 = (s32[8]{0:T(128)S(1)}, s32[8]{0:T(128)}, u32[]{:S(2)}) copy-start(s32[8]{0:T(128)} %param.20) | copy-start | bytes 100
  23.0 103.0 %copy-start.7 = (s32[4]{0:T(128)S(1)}, s32[4]{0:T(128)}, u32[]{:S(2)}) copy-start(s32[4]{0:T(128)} %param.23) | copy-start | bytes 52
  23.1 72.6 %collective-permute-start.8 = (s16[14,272,128]{2,1,0:T(8,128)(2,1)}, s16[14,272,128]{2,1,0:T(8,128)(2,1)S(1)}, u32[]{:S(2)}, u32[]{:S(2)}) collective-permute-start(s16[14,272,128]{2,1,0:T(8,128)(2,1)} %get-tuple-element.31), channel_id=1, source_target_pairs={{0,1},{1,2},{2,3},{4,5},{5,6},{6,7},{8,9},{9,10},{10,11},{12,13},{... | collective-permute-start | bytes 2924552 | tf_op jit(solution)/shard_map/ppermute | solution.py:639
  91.7 1.3 copy-start
  91.7 52.8 %collective-permute-start.9 = (s16[14,272,128]{2,1,0:T(8,128)(2,1)}, s16[14,272,128]{2,1,0:T(8,128)(2,1)}, u32[]{:S(2)}, u32[]{:S(2)}) collective-permute-start(s16[14,272,128]{2,1,0:T(8,128)(2,1)} %get-tuple-element.32), channel_id=1, source_target_pairs={{1,0},{2,1},{3,2},{5,4},{6,5},{7,6},{9,8},{10,9},{11,10},{13,12},{... | collective-permute-start | bytes 2924552 | tf_op jit(solution)/shard_map/ppermute | solution.py:640
  95.6 23.8 %copy-start.2 = (s16[14,272,128]{2,1,0:T(8,128)(2,1)}, s16[14,272,128]{2,1,0:T(8,128)(2,1)S(1)}, u32[]{:S(2)}) copy-start(s16[14,272,128]{2,1,0:T(8,128)(2,1)S(1)} %collective-permute-done.8.refs_8_) | copy-start | bytes 2924548
  95.6 70.1 %collective-permute-start.6 = (s16[14,272,128]{2,1,0:T(8,128)(2,1)}, s16[14,272,128]{2,1,0:T(8,128)(2,1)}, u32[]{:S(2)}, u32[]{:S(2)}) collective-permute-start(s16[14,272,128]{2,1,0:T(8,128)(2,1)} %get-tuple-element.28), channel_id=1, source_target_pairs={{0,1},{1,2},{2,3},{4,5},{5,6},{6,7},{8,9},{9,10},{10,11},{12,13},{... | collective-permute-start | bytes 2924552 | tf_op jit(solution)/shard_map/ppermute | solution.py:675
  115.6 1.3 copy-start.1
  115.6 50.1 %collective-permute-start.7 = (s16[14,272,128]{2,1,0:T(8,128)(2,1)}, s16[14,272,128]{2,1,0:T(8,128)(2,1)}, u32[]{:S(2)}, u32[]{:S(2)}) collective-permute-start(s16[14,272,128]{2,1,0:T(8,128)(2,1)} %get-tuple-element.29), channel_id=1, source_target_pairs={{1,0},{2,1},{3,2},{5,4},{6,5},{7,6},{9,8},{10,9},{11,10},{13,12},{... | collective-permute-start | bytes 2924552 | tf_op jit(solution)/shard_map/ppermute | solution.py:676
  119.4 66.6 %collective-permute-start.3 = (s16[13,272,128]{2,1,0:T(8,128)(2,1)}, s16[13,272,128]{2,1,0:T(8,128)(2,1)}, u32[]{:S(2)}, u32[]{:S(2)}) collective-permute-start(s16[13,272,128]{2,1,0:T(8,128)(2,1)} %get-tuple-element.26), channel_id=1, source_target_pairs={{0,1},{1,2},{2,3},{4,5},{5,6},{6,7},{8,9},{9,10},{10,11},{12,13},{... | collective-permute-start | bytes 2715656 | tf_op jit(solution)/shard_map/ppermute | solution.py:675
  123.5 62.6 %collective-permute-start.4 = (s16[13,272,128]{2,1,0:T(8,128)(2,1)}, s16[13,272,128]{2,1,0:T(8,128)(2,1)}, u32[]{:S(2)}, u32[]{:S(2)}) collective-permute-start(s16[13,272,128]{2,1,0:T(8,128)(2,1)} %get-tuple-element.27), channel_id=1, source_target_pairs={{1,0},{2,1},{3,2},{5,4},{6,5},{7,6},{9,8},{10,9},{11,10},{13,12},{... | collective-permute-start | bytes 2715656 | tf_op jit(solution)/shard_map/ppermute | solution.py:676
  205.8 10.3 %collective-permute-start.12 = (f32[8,64,128]{2,1,0:T(8,128)}, f32[8,64,128]{2,1,0:T(8,128)S(1)}, u32[]{:S(2)}, u32[]{:S(2)}) collective-permute-start(f32[8,64,128]{2,1,0:T(8,128)} %get-tuple-element.36), channel_id=1, source_target_pairs={{0,12},{4,0},{8,4},{12,8},{16,28},{20,16},{24,20},{28,24},{1,13},{... | collective-permute-start | bytes 786440 | tf_op jit(solution)/shard_map/ppermute | solution.py:699
  207.5 15.5 %collective-permute-start.11 = (f32[8,64,128]{2,1,0:T(8,128)}, f32[8,64,128]{2,1,0:T(8,128)S(1)}, u32[]{:S(2)}, u32[]{:S(2)}) collective-permute-start(f32[8,64,128]{2,1,0:T(8,128)} %get-tuple-element.35), channel_id=1, source_target_pairs={{0,8},{4,12},{8,0},{12,4},{16,24},{20,28},{24,16},{28,20},{1,9},{5... | collective-permute-start | bytes 786440 | tf_op jit(solution)/shard_map/ppermute | solution.py:699
  210.3 12.7 %collective-permute-start.10 = (f32[8,64,128]{2,1,0:T(8,128)}, f32[8,64,128]{2,1,0:T(8,128)S(1)}, u32[]{:S(2)}, u32[]{:S(2)}) collective-permute-start(f32[8,64,128]{2,1,0:T(8,128)} %get-tuple-element.34), channel_id=1, source_target_pairs={{0,4},{4,8},{8,12},{12,0},{16,20},{20,24},{24,28},{28,16},{1,5},{5... | collective-permute-start | bytes 786440 | tf_op jit(solution)/shard_map/ppermute | solution.py:699

commit v4 on v3

--- a/solution.py
+++ b/solution.py
@@ -336,9 +336,6 @@
         if not first_pass:
             for copy in tile_copies:
                 copy.wait()
-        for copy in other_copies:
-            copy.wait()
-        record(src, reach + 1 if backward else 1)
         for step in range(1, reach + 1):
             lo, hi = step, layers - step
             if backward:
@@ -363,10 +360,14 @@
                     add = v_buf[source_x, pl.ds(base, 8), :] * amps_ref[shot * reach + step - 1]
                     dst[source_x, at, :] = dst[source_x, at, :] + jnp.where(mask, add, 0.0)
 
+            if step == 1:
+                for copy in other_copies[-1:]:
+                    copy.wait()
+                record(src, reach + 1 if backward else 1)
             src, dst = dst, src
             record(src, reach + 1 - step if backward else step + 1)
 
-        for copy in model_copies:
+        for copy in model_copies + other_copies[:-1]:
             copy.wait()
         if kind == "blocks":
             block = half_rows // blocks
@@ -375,7 +376,7 @@
 
                 def cut(x, carry, out=out, base=base):
                     at = pl.ds(base, block)
-                    out[x] = other_refs[0][x, at, :] + image[x, at, :]
+                    out[x] = (other_refs[0][x, at, :] + image[x, at, :]).astype(out.dtype)
                     return carry
 
                 lax.fori_loop(0, width, cut, 0)
@@ -385,7 +386,9 @@
     vmem = pl.BlockSpec(memory_space=pltpu.VMEM)
     shape = (width, half_rows, depth_cells)
     if kind == "blocks":
-        out_shape = (jax.ShapeDtypeStruct((width, half_rows // blocks, depth_cells), jnp.float32),) * blocks
+        block_shape = (width, half_rows // blocks, depth_cells)
+        out_shape = (jax.ShapeDtypeStruct(block_shape, jnp.float32),)
+        out_shape += (jax.ShapeDtypeStruct(block_shape, jnp.bfloat16),) * (blocks - 1)
     elif kind == "image":
         out_shape = (jax.ShapeDtypeStruct(shape, jnp.float32),)
     else:
@@ -697,7 +700,7 @@
     for d in range(1, half):
         route = [(i, (i // half) * half + (i % half + d) % half) for i in range(shots)]
         arrived = lax.ppermute(blocks[d], "shot", route)
-        total = total + arrived
+        total = total + arrived.astype(jnp.float32)
     return total
 
 

time: 225 us -> 218 us (0.969)
  waiting for transfers between devices: 93.5 us -> 87.8 us
    ppermute x3, waiting for transfers between devices: 12.7 us -> 7.07 us  [on_device(): arrived = lax.ppermute(blocks[d], 'shot', route)]
  transfers between devices with their start and end apart: 13 -> 13, of which waited for: 4 -> 4; matrix products, arithmetic and copies ran while one was open for 1% -> 1% of each run, Pallas kernels for 33% -> 34%
where the time goes in v4:
time: 218 us; the launch traced here: 217 us
  Pallas kernels  96.4 us (44%)
  waiting for transfers between devices  87.8 us (40%)
  starting transfers between devices  28.6 us (13%)
  other arithmetic  2.2 us (1%)
    pallas_call x4, Pallas kernels, wave_pass(): pl.pallas_call(kernel, out_shape=out_shape, in_specs=[smem, smem] + [any_...  76.8 us
    ppermute x1, waiting for transfers between devices, on_device(): import_w = lax.ppermute(send_w, 'shot', across)  65.6 us
    ppermute x1, waiting for transfers between devices, on_device(): import_u = lax.ppermute(send_u, 'shot', across)  15.2 us
    pallas_call x4, Pallas kernels, pack_rows(): pl.pallas_call(kernel, out_shape=tuple((jax.ShapeDtypeStruct((m, rows, de...  14.5 us
    ppermute x2, starting transfers between devices, from_sides(): from_left = lax.ppermute(send_up, 'xy', up)  8.81 us
    ppermute x3, waiting for transfers between devices, on_device(): arrived = lax.ppermute(blocks[d], 'shot', route)  7.07 us
    ppermute x2, starting transfers between devices, sides(): from_left = lax.ppermute(send_up, 'xy', up)  6.67 us
    pallas_call x2, Pallas kernels, repack(): pl.pallas_call(kernel, out_shape=tuple((jax.ShapeDtypeStruct((m,) + packe...  5.13 us
  transfers between devices with their start and end apart: 13, of which 4 were waited for; matrix products, arithmetic and copies ran while one was open for 1% of the time, Pallas kernels for 34%

profile of v4, /device:TPU:0, one launch (start us, length us, event | category | flops | bytes accessed | tf_op | source)
XLA Modules:
  0.0 216.9 jit_solution(17196066635761735104)
XLA Ops:
  0.0 4.0 %pack_rows.5 = (s16[25,272,128]{2,1,0:T(8,128)(2,1)}, s16[25,272,128]{2,1,0:T(8,128)(2,1)}) custom-call(s32[1]{0:T(128)} %bitcast.first_ref, f32[8,512,128]{2,1,0:T(8,128)} %bitcast.11, f32[8,512,128]{2,1,0:T(8,128)} %bitcast.14, f32[8,512,128]{2,1,0:T(8,128)} %refs_4_.1, f32[8,512,128]{2,1,0:T(8,128)} %refs_5_.1), custom_call_target="tpu_custom_call" | custom-call | flops 1114112 | bytes 8912896 | tf_op jit(solution)/shard_map/pack_rows/pallas_call | solution.py:538
  4.0 3.6 %collective-permute-start.1 = (s16[25,272,128]{2,1,0:T(8,128)(2,1)}, s16[25,272,128]{2,1,0:T(8,128)(2,1)}, u32[]{:S(2)}, u32[]{:S(2)}) collective-permute-start(s16[25,272,128]{2,1,0:T(8,128)(2,1)} %get-tuple-element.21), channel_id=1, source_target_pairs={{0,1},{1,2},{2,3},{4,5},{5,6},{6,7},{8,9},{9,10},{10,11},{12,13},{... | collective-permute-start | bytes 5222408 | tf_op jit(solution)/shard_map/ppermute | solution.py:642
  7.6 1.3 collective-permute-start.2
  8.9 3.5 %pack_rows.6 = s16[17,272,128]{2,1,0:T(8,128)(2,1)} custom-call(s32[1]{0:T(128)} %bitcast.5.first_ref, f32[8,512,128]{2,1,0:T(8,128)} %bitcast.17, f32[8,512,128]{2,1,0:T(8,128)} %bitcast.20, f32[56,512]{1,0:T(8,128)} %bitcast.23), custom_call_target="tpu_custom_call" | custom-call | flops 557056 | bytes 4456448 | tf_op jit(solution)/shard_map/pack_rows/pallas_call | solution.py:538
  12.4 3.5 %collective-permute-start.5 = (s16[17,272,128]{2,1,0:T(8,128)(2,1)}, s16[17,272,128]{2,1,0:T(8,128)(2,1)S(1)}, u32[]{:S(2)}, u32[]{:S(2)}) collective-permute-start(s16[17,272,128]{2,1,0:T(8,128)(2,1)} %pack_rows.6), channel_id=1, source_target_pairs={{0,16},{4,20},{8,24},{12,28},{16,0},{20,4},{24,8},{28,12},{1,17},{... | collective-permute-start | bytes 3551240 | tf_op jit(solution)/shard_map/ppermute | solution.py:631
  15.9 3.3 %pack_rows.4 = s16[16,272,128]{2,1,0:T(8,128)(2,1)} custom-call(s32[1]{0:T(128)} %bitcast.5.first_ref, f32[8,512,128]{2,1,0:T(8,128)} %bitcast.12, f32[8,512,128]{2,1,0:T(8,128)} %bitcast.15), custom_call_target="tpu_custom_call" | custom-call | flops 557056 | bytes 4456448 | tf_op jit(solution)/shard_map/pack_rows/pallas_call | solution.py:538
  19.2 0.1 collective-permute-start
  19.3 3.7 %pack_rows.7 = (s16[14,272,128]{2,1,0:T(8,128)(2,1)}, s16[14,272,128]{2,1,0:T(8,128)(2,1)}) custom-call(s32[1]{0:T(128)} %bitcast.first_ref, f32[8,512,128]{2,1,0:T(8,128)} %bitcast.18, f32[8,512,128]{2,1,0:T(8,128)} %bitcast.21, f32[56,512]{1,0:T(8,128)} %bitcast.24), custom_call_target="tpu_custom_call" | custom-call | flops 557056 | bytes 4456448 | tf_op jit(solution)/shard_map/pack_rows/pallas_call | solution.py:538
  23.0 0.0 copy-start.4
  23.0 0.0 copy-start.3
  23.0 0.0 copy-start.5
  23.0 0.0 copy-start.6
  23.0 0.0 copy-start.7
  23.1 3.1 %collective-permute-start.8 = (s16[14,272,128]{2,1,0:T(8,128)(2,1)}, s16[14,272,128]{2,1,0:T(8,128)(2,1)S(1)}, u32[]{:S(2)}, u32[]{:S(2)}) collective-permute-start(s16[14,272,128]{2,1,0:T(8,128)(2,1)} %get-tuple-element.31), channel_id=1, source_target_pairs={{0,1},{1,2},{2,3},{4,5},{5,6},{6,7},{8,9},{9,10},{10,11},{12,13},{... | collective-permute-start | bytes 2924552 | tf_op jit(solution)/shard_map/ppermute | solution.py:642
  26.1 65.6 %collective-permute-done.5.packed_ref.refs_2_ = s16[17,272,128]{2,1,0:T(8,128)(2,1)S(1)} collective-permute-done((s16[17,272,128]{2,1,0:T(8,128)(2,1)}, s16[17,272,128]{2,1,0:T(8,128)(2,1)S(1)}, u32[]{:S(2)}, u32[]{:S(2)}) %collective-permute-start.5) | collective-permute-done | bytes 1183776 | tf_op jit(solution)/shard_map/ppermute | solution.py:631
  91.7 1.3 collective-permute-start.9
  93.0 2.6 %repack.3 = (s16[14,272,128]{2,1,0:T(8,128)(2,1)}, s16[14,272,128]{2,1,0:T(8,128)(2,1)}) custom-call(s16[17,272,128]{2,1,0:T(8,128)(2,1)} %copy-done), custom_call_target="tpu_custom_call" | custom-call | bytes 3551232 | tf_op jit(solution)/shard_map/repack/pallas_call | solution.py:574
  95.6 0.0 collective-permute-done.8.refs_8_
  95.6 4.8 %collective-permute-start.6 = (s16[14,272,128]{2,1,0:T(8,128)(2,1)}, s16[14,272,128]{2,1,0:T(8,128)(2,1)}, u32[]{:S(2)}, u32[]{:S(2)}) collective-permute-start(s16[14,272,128]{2,1,0:T(8,128)(2,1)} %get-tuple-element.28), channel_id=1, source_target_pairs={{0,1},{1,2},{2,3},{4,5},{5,6},{6,7},{8,9},{9,10},{10,11},{12,13},{... | collective-permute-start | bytes 2924552 | tf_op jit(solution)/shard_map/ppermute | solution.py:678
  100.4 15.2 %collective-permute-done.packed_ref.refs_2_ = s16[16,272,128]{2,1,0:T(8,128)(2,1)S(1)} collective-permute-done((s16[16,272,128]{2,1,0:T(8,128)(2,1)}, s16[16,272,128]{2,1,0:T(8,128)(2,1)S(1)}, u32[]{:S(2)}, u32[]{:S(2)}) %collective-permute-start) | collective-permute-done | bytes 1114144 | tf_op jit(solution)/shard_map/ppermute | solution.py:651
  115.6 1.3 collective-permute-start.7
  116.9 2.5 %repack.2 = (s16[13,272,128]{2,1,0:T(8,128)(2,1)}, s16[13,272,128]{2,1,0:T(8,128)(2,1)}) custom-call(s16[16,272,128]{2,1,0:T(8,128)(2,1)} %copy-done.1), custom_call_target="tpu_custom_call" | custom-call | bytes 3342336 | tf_op jit(solution)/shard_map/repack/pallas_call | solution.py:574
  119.4 0.0 collective-permute-done.1.refs_6_
  119.4 4.0 %collective-permute-start.3 = (s16[13,272,128]{2,1,0:T(8,128)(2,1)}, s16[13,272,128]{2,1,0:T(8,128)(2,1)}, u32[]{:S(2)}, u32[]{:S(2)}) collective-permute-start(s16[13,272,128]{2,1,0:T(8,128)(2,1)} %get-tuple-element.26), channel_id=1, source_target_pairs={{0,1},{1,2},{2,3},{4,5},{5,6},{6,7},{8,9},{9,10},{10,11},{12,13},{... | collective-permute-start | bytes 2715656 | tf_op jit(solution)/shard_map/ppermute | solution.py:678
  123.5 0.0 collective-permute-done.2.refs_7_
  123.5 1.3 collective-permute-start.4
  124.8 0.1 copy.13
  124.9 0.1 pad_add_fusion
  125.0 0.1 convert_compare_fusion
  125.1 0.1 select_reduce_fusion
  125.2 0.1 copy.14
  125.3 0.6 reshape.38.refs_1_
  125.9 0.2 select_reduce_fusion.1
  126.1 0.7 concatenate.3.refs_0_
  126.8 17.7 %shard_map.118 = (bf16[4,8,256,128]{3,2,1,0:T(8,128)(2,1)}, f32[22,272,128]{2,1,0:T(8,128)}, f32[22,272,128]{2,1,0:T(8,128)}, f32[22,272,128]{2,1,0:T(8,128)}) custom-call(s32[13]{0:T(128)} %concatenate.3.refs_0_, f32[14]{0:T(128)} %reshape.38.refs_1_, f32[8,512,128]{2,1,0:T(8,128)} %bitcast.13, f32[8,512,128]{2,1,0:T(8,128)} %bitcast.16, ...), custom_call_target="tpu_custom_call" | custom-call | flops 80424960 | bytes 15319040 | tf_op jit(solution)/shard_map/pallas_call | solution.py:405
  144.5 0.0 collective-permute-done.9.refs_9_
  144.5 21.2 %shard_map.120.refs_9_ = f32[4,8,256,128]{3,2,1,0:T(8,128)} custom-call(s32[13]{0:T(128)} %concatenate.3.refs_0_, f32[14]{0:T(128)} %reshape.38.refs_1_, f32[8,512,128]{2,1,0:T(8,128)} %bitcast.19, f32[8,512,128]{2,1,0:T(8,128)} %bitcast.22, f32[56,512]{1,0:T(8,128)} %bitcast.25, f32[22,272,128]{2,1,0:T(8,128)} %get-tuple-element.23.refs_3_.refs_5_, ...), custom_call_target="tpu_custom_call" | custom-call | flops 80424960 | bytes 15319040 | tf_op jit(solution)/shard_map/pallas_call | solution.py:405
  165.7 0.0 collective-permute-done.6.refs_6_
  165.7 0.0 collective-permute-done.7.refs_7_
  165.7 19.7 %shard_map.119.refs_8_ = f32[8,256,128]{2,1,0:T(8,128)} custom-call(s32[13]{0:T(128)} %concatenate.3.refs_0_, f32[14]{0:T(128)} %reshape.38.refs_1_, s16[17,272,128]{2,1,0:T(8,128)(2,1)} %copy-done, f32[22,272,128]{2,1,0:T(8,128)} %get-tuple-element.23.refs_3_.refs_5_, f32[22,272,128]{2,1,0:T(8,128)} %get-tuple-element.24.refs_4_.refs_6_, ...), custom_call_target="tpu_custom_call" | custom-call | flops 80424960 | bytes 15319040 | tf_op jit(solution)/shard_map/pallas_call | solution.py:405
  185.5 0.0 collective-permute-done.3.refs_6_
  185.5 18.1 %shard_map.121 = (f32[8,64,128]{2,1,0:T(8,128)}, bf16[8,64,128]{2,1,0:T(8,128)(2,1)}, bf16[8,64,128]{2,1,0:T(8,128)(2,1)}, bf16[8,64,128]{2,1,0:T(8,128)(2,1)}) custom-call(s32[13]{0:T(128)} %concatenate.3.refs_0_, f32[14]{0:T(128)} %reshape.38.refs_1_, s16[16,272,128]{2,1,0:T(8,128)(2,1)} %copy-done.1, f32[22,272,128]{2,1,0:T(8,128)} %get-tuple-element.23.refs_3_.refs_5_, ...), custom_call_target="tpu_custom_call" | custom-call | flops 80424960 | bytes 15319040 | tf_op jit(solution)/shard_map/pallas_call | solution.py:405
  203.7 1.7 collective-permute-start.12
  205.3 2.8 %collective-permute-start.11 = (bf16[8,64,128]{2,1,0:T(8,128)(2,1)}, bf16[8,64,128]{2,1,0:T(8,128)(2,1)S(1)}, u32[]{:S(2)}, u32[]{:S(2)}) collective-permute-start(bf16[8,64,128]{2,1,0:T(8,128)(2,1)} %get-tuple-element.35), channel_id=1, source_target_pairs={{0,8},{4,12},{8,0},{12,4},{16,24},{20,28},{24,16},{28,20},{1,9},{5... | collective-permute-start | bytes 393224 | tf_op jit(solution)/shard_map/ppermute | solution.py:702
  208.1 3.0 %collective-permute-done.12 = bf16[8,64,128]{2,1,0:T(8,128)(2,1)S(1)} collective-permute-done((bf16[8,64,128]{2,1,0:T(8,128)(2,1)}, bf16[8,64,128]{2,1,0:T(8,128)(2,1)S(1)}, u32[]{:S(2)}, u32[]{:S(2)}) %collective-permute-start.12) | collective-permute-done | bytes 131104 | tf_op jit(solution)/shard_map/ppermute | solution.py:702
  211.1 4.0 %collective-permute-done.11 = bf16[8,64,128]{2,1,0:T(8,128)(2,1)S(1)} collective-permute-done((bf16[8,64,128]{2,1,0:T(8,128)(2,1)}, bf16[8,64,128]{2,1,0:T(8,128)(2,1)S(1)}, u32[]{:S(2)}, u32[]{:S(2)}) %collective-permute-start.11) | collective-permute-done | bytes 131104 | tf_op jit(solution)/shard_map/ppermute | solution.py:702
  215.2 0.0 collective-permute-done.10
  215.2 1.7 convert_add_fusion
  (16 shorter events, 0.1 us)
Async XLA Ops:
  4.0 115.4 %collective-permute-start.1 = (s16[25,272,128]{2,1,0:T(8,128)(2,1)}, s16[25,272,128]{2,1,0:T(8,128)(2,1)}, u32[]{:S(2)}, u32[]{:S(2)}) collective-permute-start(s16[25,272,128]{2,1,0:T(8,128)(2,1)} %get-tuple-element.21), channel_id=1, source_target_pairs={{0,1},{1,2},{2,3},{4,5},{5,6},{6,7},{8,9},{9,10},{10,11},{12,13},{... | collective-permute-start | bytes 5222408 | tf_op jit(solution)/shard_map/ppermute | solution.py:642
  7.6 115.9 %collective-permute-start.2 = (s16[25,272,128]{2,1,0:T(8,128)(2,1)}, s16[25,272,128]{2,1,0:T(8,128)(2,1)}, u32[]{:S(2)}, u32[]{:S(2)}) collective-permute-start(s16[25,272,128]{2,1,0:T(8,128)(2,1)} %get-tuple-element.22), channel_id=1, source_target_pairs={{1,0},{2,1},{3,2},{5,4},{6,5},{7,6},{9,8},{10,9},{11,10},{13,12},{... | collective-permute-start | bytes 5222408 | tf_op jit(solution)/shard_map/ppermute | solution.py:643
  12.4 79.3 %collective-permute-start.5 = (s16[17,272,128]{2,1,0:T(8,128)(2,1)}, s16[17,272,128]{2,1,0:T(8,128)(2,1)S(1)}, u32[]{:S(2)}, u32[]{:S(2)}) collective-permute-start(s16[17,272,128]{2,1,0:T(8,128)(2,1)} %pack_rows.6), channel_id=1, source_target_pairs={{0,16},{4,20},{8,24},{12,28},{16,0},{20,4},{24,8},{28,12},{1,17},{... | collective-permute-start | bytes 3551240 | tf_op jit(solution)/shard_map/ppermute | solution.py:631
  19.2 96.4 %collective-permute-start = (s16[16,272,128]{2,1,0:T(8,128)(2,1)}, s16[16,272,128]{2,1,0:T(8,128)(2,1)S(1)}, u32[]{:S(2)}, u32[]{:S(2)}) collective-permute-start(s16[16,272,128]{2,1,0:T(8,128)(2,1)} %pack_rows.4), channel_id=1, source_target_pairs={{0,16},{4,20},{8,24},{12,28},{16,0},{20,4},{24,8},{28,12},{1,17},{... | collective-permute-start | bytes 3342344 | tf_op jit(solution)/shard_map/ppermute | solution.py:651
  23.0 101.8 %copy-start.4 = (s32[8,2]{0,1:T(2,128)S(1)}, s32[8,2]{0,1:T(2,128)}, u32[]{:S(2)}) copy-start(s32[8,2]{0,1:T(2,128)} %param.22) | copy-start | bytes 196
  23.0 101.8 %copy-start.3 = (f32[8,7]{1,0:T(8,128)S(1)}, f32[8,7]{1,0:T(8,128)}, u32[]{:S(2)}) copy-start(f32[8,7]{1,0:T(8,128)} %param.19) | copy-start | bytes 676
  23.0 102.8 %copy-start.5 = (s32[8]{0:T(128)S(1)}, s32[8]{0:T(128)}, u32[]{:S(2)}) copy-start(s32[8]{0:T(128)} %param.21) | copy-start | bytes 100
  23.0 102.8 %copy-start.6 = (s32[8]{0:T(128)S(1)}, s32[8]{0:T(128)}, u32[]{:S(2)}) copy-start(s32[8]{0:T(128)} %param.20) | copy-start | bytes 100
  23.0 103.0 %copy-start.7 = (s32[4]{0:T(128)S(1)}, s32[4]{0:T(128)}, u32[]{:S(2)}) copy-start(s32[4]{0:T(128)} %param.23) | copy-start | bytes 52
  23.1 72.6 %collective-permute-start.8 = (s16[14,272,128]{2,1,0:T(8,128)(2,1)}, s16[14,272,128]{2,1,0:T(8,128)(2,1)S(1)}, u32[]{:S(2)}, u32[]{:S(2)}) collective-permute-start(s16[14,272,128]{2,1,0:T(8,128)(2,1)} %get-tuple-element.31), channel_id=1, source_target_pairs={{0,1},{1,2},{2,3},{4,5},{5,6},{6,7},{8,9},{9,10},{10,11},{12,13},{... | collective-permute-start | bytes 2924552 | tf_op jit(solution)/shard_map/ppermute | solution.py:642
  91.7 1.3 copy-start
  91.7 52.8 %collective-permute-start.9 = (s16[14,272,128]{2,1,0:T(8,128)(2,1)}, s16[14,272,128]{2,1,0:T(8,128)(2,1)}, u32[]{:S(2)}, u32[]{:S(2)}) collective-permute-start(s16[14,272,128]{2,1,0:T(8,128)(2,1)} %get-tuple-element.32), channel_id=1, source_target_pairs={{1,0},{2,1},{3,2},{5,4},{6,5},{7,6},{9,8},{10,9},{11,10},{13,12},{... | collective-permute-start | bytes 2924552 | tf_op jit(solution)/shard_map/ppermute | solution.py:643
  95.6 23.8 %copy-start.2 = (s16[14,272,128]{2,1,0:T(8,128)(2,1)}, s16[14,272,128]{2,1,0:T(8,128)(2,1)S(1)}, u32[]{:S(2)}) copy-start(s16[14,272,128]{2,1,0:T(8,128)(2,1)S(1)} %collective-permute-done.8.refs_8_) | copy-start | bytes 2924548
  95.6 70.1 %collective-permute-start.6 = (s16[14,272,128]{2,1,0:T(8,128)(2,1)}, s16[14,272,128]{2,1,0:T(8,128)(2,1)}, u32[]{:S(2)}, u32[]{:S(2)}) collective-permute-start(s16[14,272,128]{2,1,0:T(8,128)(2,1)} %get-tuple-element.28), channel_id=1, source_target_pairs={{0,1},{1,2},{2,3},{4,5},{5,6},{6,7},{8,9},{9,10},{10,11},{12,13},{... | collective-permute-start | bytes 2924552 | tf_op jit(solution)/shard_map/ppermute | solution.py:678
  115.6 1.3 copy-start.1
  115.6 50.1 %collective-permute-start.7 = (s16[14,272,128]{2,1,0:T(8,128)(2,1)}, s16[14,272,128]{2,1,0:T(8,128)(2,1)}, u32[]{:S(2)}, u32[]{:S(2)}) collective-permute-start(s16[14,272,128]{2,1,0:T(8,128)(2,1)} %get-tuple-element.29), channel_id=1, source_target_pairs={{1,0},{2,1},{3,2},{5,4},{6,5},{7,6},{9,8},{10,9},{11,10},{13,12},{... | collective-permute-start | bytes 2924552 | tf_op jit(solution)/shard_map/ppermute | solution.py:679
  119.4 66.0 %collective-permute-start.3 = (s16[13,272,128]{2,1,0:T(8,128)(2,1)}, s16[13,272,128]{2,1,0:T(8,128)(2,1)}, u32[]{:S(2)}, u32[]{:S(2)}) collective-permute-start(s16[13,272,128]{2,1,0:T(8,128)(2,1)} %get-tuple-element.26), channel_id=1, source_target_pairs={{0,1},{1,2},{2,3},{4,5},{5,6},{6,7},{8,9},{9,10},{10,11},{12,13},{... | collective-permute-start | bytes 2715656 | tf_op jit(solution)/shard_map/ppermute | solution.py:678
  123.5 62.0 %collective-permute-start.4 = (s16[13,272,128]{2,1,0:T(8,128)(2,1)}, s16[13,272,128]{2,1,0:T(8,128)(2,1)}, u32[]{:S(2)}, u32[]{:S(2)}) collective-permute-start(s16[13,272,128]{2,1,0:T(8,128)(2,1)} %get-tuple-element.27), channel_id=1, source_target_pairs={{1,0},{2,1},{3,2},{5,4},{6,5},{7,6},{9,8},{10,9},{11,10},{13,12},{... | collective-permute-start | bytes 2715656 | tf_op jit(solution)/shard_map/ppermute | solution.py:679
  203.7 7.5 %collective-permute-start.12 = (bf16[8,64,128]{2,1,0:T(8,128)(2,1)}, bf16[8,64,128]{2,1,0:T(8,128)(2,1)S(1)}, u32[]{:S(2)}, u32[]{:S(2)}) collective-permute-start(bf16[8,64,128]{2,1,0:T(8,128)(2,1)} %get-tuple-element.36), channel_id=1, source_target_pairs={{0,12},{4,0},{8,4},{12,8},{16,28},{20,16},{24,20},{28,24},{1,13},{... | collective-permute-start | bytes 393224 | tf_op jit(solution)/shard_map/ppermute | solution.py:702
  205.3 9.9 %collective-permute-start.11 = (bf16[8,64,128]{2,1,0:T(8,128)(2,1)}, bf16[8,64,128]{2,1,0:T(8,128)(2,1)S(1)}, u32[]{:S(2)}, u32[]{:S(2)}) collective-permute-start(bf16[8,64,128]{2,1,0:T(8,128)(2,1)} %get-tuple-element.35), channel_id=1, source_target_pairs={{0,8},{4,12},{8,0},{12,4},{16,24},{20,28},{24,16},{28,20},{1,9},{5... | collective-permute-start | bytes 393224 | tf_op jit(solution)/shard_map/ppermute | solution.py:702
  208.1 7.1 %collective-permute-start.10 = (bf16[8,64,128]{2,1,0:T(8,128)(2,1)}, bf16[8,64,128]{2,1,0:T(8,128)(2,1)S(1)}, u32[]{:S(2)}, u32[]{:S(2)}) collective-permute-start(bf16[8,64,128]{2,1,0:T(8,128)(2,1)} %get-tuple-element.34), channel_id=1, source_target_pairs={{0,4},{4,8},{8,12},{12,0},{16,20},{20,24},{24,28},{28,16},{1,5},{5... | collective-permute-start | bytes 393224 | tf_op jit(solution)/shard_map/ppermute | solution.py:702

commit v5 on v4

--- a/solution.py
+++ b/solution.py
@@ -7,7 +7,7 @@
 
 
 PAD = 8
-EDGE = 16
+EDGE = 8
 LANES = 128
 BY_MATRIX = ((True, False), (True, True))
 CHUNK = 32
@@ -26,11 +26,11 @@
     column = lax.broadcasted_iota(jnp.int32, (2 * LANES, LANES), 1)
     row = jnp.where(row >= LANES, row - LANES, row)
     beside = (row - column == 1) | (column - row == 1)
-    return jnp.where(beside, 1.0, 0.0).astype(jnp.bfloat16)
+    return jnp.where(beside, 1.0, jnp.where(row == column, -2.0, 0.0)).astype(jnp.bfloat16)
 
 
 def stencil_step(src, dst, coefs, lo, hi, rows, beside, sums, surface=None):
-    centre, hor, vel = coefs
+    hor, vel = coefs
     by_matrix = BY_MATRIX[surface is not None]
 
     def vertical_sums(x, j):
@@ -50,6 +50,8 @@
 
     def body(i, carry):
         x = lo + 2 * i
+        if surface is None:
+            ahead(x)
         shifts = [None, None] if surface is None else [surface[1](x), surface[1](x + 1)]
         for r0, size in spans(rows, CHUNK):
             at = pl.ds(PAD + r0, size)
@@ -72,20 +74,23 @@
                 else:
                     above = jnp.where(lane == 0, data, pltpu.roll(mid, 1, 1))
                     deeper = jnp.where(lane == LANES - 1, 0.0, pltpu.roll(mid, LANES - 1, 1))
-                    vertical = above + deeper
-                new = centre[x + j, here, :] * mid - dst[x + j, at, :]
-                new = new + hor[x + j, here, :] * lateral
+                    vertical = above + deeper - (mid + mid)
+                twice = mid + mid
+                new = twice - dst[x + j, at, :]
+                new = new + hor[x + j, here, :] * (lateral - (twice + twice))
                 new = new + vel[x + j, here, :] * vertical
                 dst[x + j, at, :] = new
-        ahead(jnp.minimum(x + 2, hi - 2))
+        if surface is not None:
+            ahead(jnp.minimum(x + 2, hi - 2))
         return carry
 
-    ahead(lo)
+    if surface is not None:
+        ahead(lo)
     lax.fori_loop(0, (hi - lo) // 2, body, 0)
 
 
-def header_rows(first, half_rows):
-    return jnp.where(first == 0, half_rows + 8, 0)
+def spare_row(first, half_rows):
+    return pl.multiple_of(jnp.where(first == 0, half_rows, 0), 8), jnp.where(first == 0, 7, 0)
 
 
 def encode_scale(top):
@@ -101,11 +106,9 @@
 
 
 def decode_scale(stage, layer, first, half_rows):
-    base = pl.multiple_of(jnp.where(first == 0, half_rows, 0), 16)
-    block = stage[layer, pl.ds(base, 16), :].astype(jnp.int32).astype(jnp.float32)
-    row = lax.broadcasted_iota(jnp.int32, (16, LANES), 0)
-    skip = jnp.where(first == 0, 8, 0)
-    held = (row >= skip) & (row < skip + 8)
+    base, spare = spare_row(first, half_rows)
+    block = stage[layer, pl.ds(base, 8), :].astype(jnp.int32).astype(jnp.float32)
+    held = lax.broadcasted_iota(jnp.int32, (8, LANES), 0) == spare
     exponent = jnp.max(jnp.where(held, block, 0.0), axis=(0, 1), keepdims=True)
     scale = jnp.full_like(exponent, 1.0 / 2048.0)
     for j in STEPS_OF_SCALE:
@@ -153,15 +156,15 @@
         other_hbm = refs[pos : pos + len(others)]
         pos += len(others)
         n_out = blocks if kind == "blocks" else 1
-        n_model = 3 if first_pass else 0
+        n_model = 2 if first_pass else 0
         outs = refs[pos : pos + n_out]
         pos += n_out
         model_outs = refs[pos : pos + n_model]
         pos += n_model
-        buf_a, buf_b, v_buf, h_buf, c_buf, stage_l, stage_r, stage_t, top, beside, sums, sem = refs[
-            pos : pos + 12
+        buf_a, buf_b, v_buf, h_buf, stage_l, stage_r, stage_t, top, beside, sums, sem = refs[
+            pos : pos + 11
         ]
-        model_bufs = (c_buf, h_buf, v_buf)
+        model_bufs = (h_buf, v_buf)
 
         steps = [ints_ref[k] for k in range(n_snaps)]
         first_row, skip, place = [ints_ref[n_snaps + k] for k in range(3)]
@@ -181,7 +184,9 @@
             ]
         else:
             tile_copies = [
-                pltpu.make_async_copy(ref, buf, sem.at[18 + n])
+                pltpu.make_async_copy(
+                    ref.at[pl.ds(1, layers - 2)], buf.at[pl.ds(1, layers - 2)], sem.at[18 + n]
+                )
                 for n, (ref, buf) in enumerate(zip(model_refs, model_bufs))
             ]
         side_copies = []
@@ -223,7 +228,7 @@
                     pltpu.make_async_copy(field_refs[2], flat.at[pl.ds(0, n_data)], sem.at[14])
                 )
                 flat[n_data:, :] = jnp.zeros((LANES - n_data, all_rows), jnp.float32)
-        other_refs = refs[pos + 12 : pos + 12 + len(others)]
+        other_refs = refs[pos + 11 : pos + 11 + len(others)]
         other_copies = [
             pltpu.make_async_copy(source, target, sem.at[15 + n])
             for n, (source, target) in enumerate(zip(other_hbm, other_refs))
@@ -267,21 +272,16 @@
         def coefficients(x, carry):
             for r0, size in spans(rows, 64):
                 at = pl.ds(r0, size)
-                v = v_buf[x, at, :]
-                h = v * (1.0 + 2.0 * h_buf[x, at, :])
-                h_buf[x, at, :] = h
-                c_buf[x, at, :] = 2.0 - (4.0 * h + 2.0 * v)
+                h_buf[x, at, :] = v_buf[x, at, :] * (1.0 + 2.0 * h_buf[x, at, :])
             return carry
 
         model_copies = []
         if first_pass:
-            edge = jnp.zeros((rows, LANES), jnp.float32)
-            for buf in model_bufs:
-                buf[0] = edge
-                buf[layers - 1] = edge
             lax.fori_loop(1, layers - 1, coefficients, 0)
             model_copies = [
-                pltpu.make_async_copy(buf, out, sem.at[18 + n])
+                pltpu.make_async_copy(
+                    buf.at[pl.ds(1, layers - 2)], out.at[pl.ds(1, layers - 2)], sem.at[18 + n]
+                )
                 for n, (buf, out) in enumerate(zip(model_bufs, model_outs))
             ]
             for copy in model_copies:
@@ -332,7 +332,7 @@
                 lax.fori_loop(0, width, body, 0)
 
         src, dst = buf_a, buf_b
-        coefs = (c_buf, h_buf, v_buf)
+        coefs = (h_buf, v_buf)
         if not first_pass:
             for copy in tile_copies:
                 copy.wait()
@@ -394,9 +394,9 @@
     else:
         dtype = jnp.bfloat16 if kind == "snaps" else jnp.float32
         out_shape = (jax.ShapeDtypeStruct((n_snaps,) + shape, dtype),)
-    n_model = 3 if first_pass else 0
+    n_model = 2 if first_pass else 0
     if first_pass:
-        out_shape += (jax.ShapeDtypeStruct((layers, rows, depth_cells), jnp.float32),) * 3
+        out_shape += (jax.ShapeDtypeStruct((layers, rows, depth_cells), jnp.float32),) * 2
     cells = layers * rows * depth_cells
     grid_buf = pltpu.VMEM((layers, rows, depth_cells), jnp.float32)
     field_buf = pltpu.VMEM((layers, rows + 2 * PAD, depth_cells), jnp.float32)
@@ -410,7 +410,7 @@
         + [any_spec] * (len(inputs_m) + 2 * n_side + len(others)),
         out_specs=(vmem,) * (len(out_shape) - n_model) + (any_spec,) * n_model,
         scratch_shapes=[
-            field_buf, field_buf, grid_buf, grid_buf, grid_buf, side, side,
+            field_buf, field_buf, grid_buf, grid_buf, side, side,
             pltpu.VMEM((stage_layers, rows, depth_cells), WIRE),
             pltpu.VMEM((3, rows, depth_cells), jnp.float32),
             pltpu.VMEM((2 * LANES, LANES), jnp.bfloat16),
@@ -449,8 +449,8 @@
         outs = refs[n + tail : n + tail + len(ranges)]
         rest = refs[n + tail + len(ranges) :]
         wide, narrow, sem, out_sem = rest[:4]
-        window = pl.ds(pl.multiple_of(first_ref[0], 16), rows)
-        spare = pl.ds(pl.multiple_of(header_rows(first_ref[0], half_rows), 8), 8)
+        window = pl.ds(pl.multiple_of(first_ref[0], 8), rows)
+        base, spare = spare_row(first_ref[0], half_rows)
         copies = [
             pltpu.make_async_copy(ref.at[:, window], wide.at[i], sem.at[i])
             for i, ref in enumerate(field_refs)
@@ -508,8 +508,10 @@
             top = jnp.max(top, axis=(0, 1), keepdims=True)
             scale, unit, exponent = encode_scale(top)
             header = jnp.broadcast_to(exponent * unit, (8, LANES))
+            is_spare = lax.broadcasted_iota(jnp.int32, (8, LANES), 0) == spare
             for x in range(width):
-                wide[group[0], x, spare, :] = header
+                old = wide[group[0], x, pl.ds(base, 8), :]
+                wide[group[0], x, pl.ds(base, 8), :] = jnp.where(is_spare, header, old)
             for i in group:
                 put(i, scale)
             if with_data:

time: 218 us -> 215 us (0.986)
  waiting for transfers between devices: 87.8 us -> 85.2 us
  transfers between devices with their start and end apart: 13 -> 13, of which waited for: 4 -> 5; matrix products, arithmetic and copies ran while one was open for 1% -> 1% of each run, Pallas kernels for 34% -> 35%
where the time goes in v5:
time: 215 us; the launch traced here: 214 us
  Pallas kernels  96.1 us (45%)
  waiting for transfers between devices  85.2 us (40%)
  starting transfers between devices  28.6 us (13%)
  other arithmetic  2.2 us (1%)
    pallas_call x4, Pallas kernels, wave_pass(): pl.pallas_call(kernel, out_shape=out_shape, in_specs=[smem, smem] + [any_...  76.7 us
    ppermute x1, waiting for transfers between devices, on_device(): import_w = lax.ppermute(send_w, 'shot', across)  63.5 us
    ppermute x1, waiting for transfers between devices, on_device(): import_u = lax.ppermute(send_u, 'shot', across)  14.5 us
    pallas_call x4, Pallas kernels, pack_rows(): pl.pallas_call(kernel, out_shape=tuple((jax.ShapeDtypeStruct((m, rows, de...  14.3 us
    ppermute x2, starting transfers between devices, from_sides(): from_left = lax.ppermute(send_up, 'xy', up)  8.71 us
    ppermute x3, waiting for transfers between devices, on_device(): arrived = lax.ppermute(blocks[d], 'shot', route)  7.18 us
    ppermute x2, starting transfers between devices, sides(): from_left = lax.ppermute(send_up, 'xy', up)  6.67 us
    pallas_call x2, Pallas kernels, repack(): pl.pallas_call(kernel, out_shape=tuple((jax.ShapeDtypeStruct((m,) + packe...  5.06 us
  transfers between devices with their start and end apart: 13, of which 5 were waited for; matrix products, arithmetic and copies ran while one was open for 1% of the time, Pallas kernels for 35%

profile of v5, /device:TPU:0, one launch (start us, length us, event | category | flops | bytes accessed | tf_op | source)
XLA Modules:
  0.0 213.9 jit_solution(15590362125612067871)
XLA Ops:
  0.0 3.9 %pack_rows.5 = (s16[25,264,128]{2,1,0:T(8,128)(2,1)}, s16[25,264,128]{2,1,0:T(8,128)(2,1)}) custom-call(s32[1]{0:T(128)} %bitcast.first_ref, f32[8,512,128]{2,1,0:T(8,128)} %bitcast.17, f32[8,512,128]{2,1,0:T(8,128)} %bitcast.20, f32[8,512,128]{2,1,0:T(8,128)} %refs_4_.1, f32[8,512,128]{2,1,0:T(8,128)} %refs_5_.1), custom_call_target="tpu_custom_call" | custom-call | flops 1081344 | bytes 8650752 | tf_op jit(solution)/shard_map/pack_rows/pallas_call | solution.py:540
  4.0 3.6 %collective-permute-start.1 = (s16[25,264,128]{2,1,0:T(8,128)(2,1)}, s16[25,264,128]{2,1,0:T(8,128)(2,1)}, u32[]{:S(2)}, u32[]{:S(2)}) collective-permute-start(s16[25,264,128]{2,1,0:T(8,128)(2,1)} %get-tuple-element.20), channel_id=1, source_target_pairs={{0,1},{1,2},{2,3},{4,5},{5,6},{6,7},{8,9},{9,10},{10,11},{12,13},{... | collective-permute-start | bytes 5068808 | tf_op jit(solution)/shard_map/ppermute | solution.py:644
  7.6 1.3 collective-permute-start.2
  8.9 3.5 %pack_rows.6 = s16[17,264,128]{2,1,0:T(8,128)(2,1)} custom-call(s32[1]{0:T(128)} %bitcast.5.first_ref, f32[8,512,128]{2,1,0:T(8,128)} %bitcast.11, f32[8,512,128]{2,1,0:T(8,128)} %bitcast.14, f32[56,512]{1,0:T(8,128)} %bitcast.23), custom_call_target="tpu_custom_call" | custom-call | flops 540672 | bytes 4325376 | tf_op jit(solution)/shard_map/pack_rows/pallas_call | solution.py:540
  12.3 3.5 %collective-permute-start.5 = (s16[17,264,128]{2,1,0:T(8,128)(2,1)}, s16[17,264,128]{2,1,0:T(8,128)(2,1)S(1)}, u32[]{:S(2)}, u32[]{:S(2)}) collective-permute-start(s16[17,264,128]{2,1,0:T(8,128)(2,1)} %pack_rows.6), channel_id=1, source_target_pairs={{0,16},{4,20},{8,24},{12,28},{16,0},{20,4},{24,8},{28,12},{1,17},{... | collective-permute-start | bytes 3446792 | tf_op jit(solution)/shard_map/ppermute | solution.py:633
  15.8 3.2 %pack_rows.4 = s16[16,264,128]{2,1,0:T(8,128)(2,1)} custom-call(s32[1]{0:T(128)} %bitcast.5.first_ref, f32[8,512,128]{2,1,0:T(8,128)} %bitcast.18, f32[8,512,128]{2,1,0:T(8,128)} %bitcast.21), custom_call_target="tpu_custom_call" | custom-call | flops 540672 | bytes 4325376 | tf_op jit(solution)/shard_map/pack_rows/pallas_call | solution.py:540
  19.1 0.1 collective-permute-start
  19.1 3.6 %pack_rows.7 = (s16[14,264,128]{2,1,0:T(8,128)(2,1)}, s16[14,264,128]{2,1,0:T(8,128)(2,1)}) custom-call(s32[1]{0:T(128)} %bitcast.first_ref, f32[8,512,128]{2,1,0:T(8,128)} %bitcast.12, f32[8,512,128]{2,1,0:T(8,128)} %bitcast.15, f32[56,512]{1,0:T(8,128)} %bitcast.24), custom_call_target="tpu_custom_call" | custom-call | flops 540672 | bytes 4325376 | tf_op jit(solution)/shard_map/pack_rows/pallas_call | solution.py:540
  22.8 0.0 copy-start.4
  22.8 0.0 copy-start.3
  22.8 0.0 copy-start.5
  22.8 0.0 copy-start.6
  22.8 0.0 copy-start.7
  22.8 3.1 %collective-permute-start.8 = (s16[14,264,128]{2,1,0:T(8,128)(2,1)}, s16[14,264,128]{2,1,0:T(8,128)(2,1)S(1)}, u32[]{:S(2)}, u32[]{:S(2)}) collective-permute-start(s16[14,264,128]{2,1,0:T(8,128)(2,1)} %get-tuple-element.29), channel_id=1, source_target_pairs={{0,1},{1,2},{2,3},{4,5},{5,6},{6,7},{8,9},{9,10},{10,11},{12,13},{... | collective-permute-start | bytes 2838536 | tf_op jit(solution)/shard_map/ppermute | solution.py:644
  25.9 63.5 %collective-permute-done.5.packed_ref.refs_2_ = s16[17,264,128]{2,1,0:T(8,128)(2,1)S(1)} collective-permute-done((s16[17,264,128]{2,1,0:T(8,128)(2,1)}, s16[17,264,128]{2,1,0:T(8,128)(2,1)S(1)}, u32[]{:S(2)}, u32[]{:S(2)}) %collective-permute-start.5) | collective-permute-done | bytes 1148960 | tf_op jit(solution)/shard_map/ppermute | solution.py:633
  89.4 1.3 collective-permute-start.9
  90.7 2.6 %repack.3 = (s16[14,264,128]{2,1,0:T(8,128)(2,1)}, s16[14,264,128]{2,1,0:T(8,128)(2,1)}) custom-call(s16[17,264,128]{2,1,0:T(8,128)(2,1)} %copy-done), custom_call_target="tpu_custom_call" | custom-call | bytes 3446784 | tf_op jit(solution)/shard_map/repack/pallas_call | solution.py:576
  93.3 0.0 collective-permute-done.8.refs_7_
  93.3 4.7 %collective-permute-start.6 = (s16[14,264,128]{2,1,0:T(8,128)(2,1)}, s16[14,264,128]{2,1,0:T(8,128)(2,1)}, u32[]{:S(2)}, u32[]{:S(2)}) collective-permute-start(s16[14,264,128]{2,1,0:T(8,128)(2,1)} %get-tuple-element.26), channel_id=1, source_target_pairs={{0,1},{1,2},{2,3},{4,5},{5,6},{6,7},{8,9},{9,10},{10,11},{12,13},{... | collective-permute-start | bytes 2838536 | tf_op jit(solution)/shard_map/ppermute | solution.py:680
  98.0 14.5 %collective-permute-done.packed_ref.refs_2_ = s16[16,264,128]{2,1,0:T(8,128)(2,1)S(1)} collective-permute-done((s16[16,264,128]{2,1,0:T(8,128)(2,1)}, s16[16,264,128]{2,1,0:T(8,128)(2,1)S(1)}, u32[]{:S(2)}, u32[]{:S(2)}) %collective-permute-start) | collective-permute-done | bytes 1081376 | tf_op jit(solution)/shard_map/ppermute | solution.py:653
  112.6 1.3 collective-permute-start.7
  113.9 2.5 %repack.2 = (s16[13,264,128]{2,1,0:T(8,128)(2,1)}, s16[13,264,128]{2,1,0:T(8,128)(2,1)}) custom-call(s16[16,264,128]{2,1,0:T(8,128)(2,1)} %copy-done.1), custom_call_target="tpu_custom_call" | custom-call | bytes 3244032 | tf_op jit(solution)/shard_map/repack/pallas_call | solution.py:576
  116.4 0.0 collective-permute-done.1.refs_6_
  116.4 4.0 %collective-permute-start.3 = (s16[13,264,128]{2,1,0:T(8,128)(2,1)}, s16[13,264,128]{2,1,0:T(8,128)(2,1)}, u32[]{:S(2)}, u32[]{:S(2)}) collective-permute-start(s16[13,264,128]{2,1,0:T(8,128)(2,1)} %get-tuple-element.24), channel_id=1, source_target_pairs={{0,1},{1,2},{2,3},{4,5},{5,6},{6,7},{8,9},{9,10},{10,11},{12,13},{... | collective-permute-start | bytes 2635784 | tf_op jit(solution)/shard_map/ppermute | solution.py:680
  120.4 0.0 collective-permute-done.2.refs_7_
  120.4 1.3 collective-permute-start.4
  121.7 0.1 copy.13
  121.8 0.1 pad_add_fusion
  121.9 0.1 convert_compare_fusion
  122.0 0.1 select_reduce_fusion
  122.0 0.1 copy.14
  122.1 0.7 reshape.38.refs_1_
  122.8 0.2 select_reduce_fusion.1
  123.0 0.6 concatenate.3.refs_0_
  123.6 17.7 %shard_map.118 = (bf16[4,8,256,128]{3,2,1,0:T(8,128)(2,1)}, f32[22,264,128]{2,1,0:T(8,128)}, f32[22,264,128]{2,1,0:T(8,128)}) custom-call(s32[13]{0:T(128)} %concatenate.3.refs_0_, f32[14]{0:T(128)} %reshape.38.refs_1_, f32[8,512,128]{2,1,0:T(8,128)} %bitcast.19, f32[8,512,128]{2,1,0:T(8,128)} %bitcast.22, f32[8,512,128]{2,1,0:T(8,128)} %refs_4_.1, ...), custom_call_target="tpu_custom_call" | custom-call | flops 78059520 | bytes 14868480 | tf_op jit(solution)/shard_map/pallas_call | solution.py:405
  141.3 0.0 collective-permute-done.9.refs_8_
  141.3 21.6 %shard_map.120.refs_8_ = f32[4,8,256,128]{3,2,1,0:T(8,128)} custom-call(s32[13]{0:T(128)} %concatenate.3.refs_0_, f32[14]{0:T(128)} %reshape.38.refs_1_, f32[8,512,128]{2,1,0:T(8,128)} %bitcast.13, f32[8,512,128]{2,1,0:T(8,128)} %bitcast.16, f32[56,512]{1,0:T(8,128)} %bitcast.25, f32[22,264,128]{2,1,0:T(8,128)} %get-tuple-element.22.refs_3_.refs_5_, ...), custom_call_target="tpu_custom_call" | custom-call | flops 78059520 | bytes 14868480 | tf_op jit(solution)/shard_map/pallas_call | solution.py:405
  162.9 0.0 collective-permute-done.6.refs_5_
  162.9 0.0 collective-permute-done.7.refs_6_
  162.9 20.3 %shard_map.119.refs_7_ = f32[8,256,128]{2,1,0:T(8,128)} custom-call(s32[13]{0:T(128)} %concatenate.3.refs_0_, f32[14]{0:T(128)} %reshape.38.refs_1_, s16[17,264,128]{2,1,0:T(8,128)(2,1)} %copy-done, f32[22,264,128]{2,1,0:T(8,128)} %get-tuple-element.22.refs_3_.refs_5_, f32[22,264,128]{2,1,0:T(8,128)} %get-tuple-element.23.refs_4_.refs_6_, ...), custom_call_target="tpu_custom_call" | custom-call | flops 78059520 | bytes 14868480 | tf_op jit(solution)/shard_map/pallas_call | solution.py:405
  183.2 0.0 collective-permute-done.4.refs_6_
  183.2 17.2 %shard_map.121 = (f32[8,64,128]{2,1,0:T(8,128)}, bf16[8,64,128]{2,1,0:T(8,128)(2,1)}, bf16[8,64,128]{2,1,0:T(8,128)(2,1)}, bf16[8,64,128]{2,1,0:T(8,128)(2,1)}) custom-call(s32[13]{0:T(128)} %concatenate.3.refs_0_, f32[14]{0:T(128)} %reshape.38.refs_1_, s16[16,264,128]{2,1,0:T(8,128)(2,1)} %copy-done.1, f32[22,264,128]{2,1,0:T(8,128)} %get-tuple-element.22.refs_3_.refs_5_, ...), custom_call_target="tpu_custom_call" | custom-call | flops 78059520 | bytes 14868480 | tf_op jit(solution)/shard_map/pallas_call | solution.py:405
  200.5 1.8 collective-permute-start.12
  202.3 2.8 %collective-permute-start.11 = (bf16[8,64,128]{2,1,0:T(8,128)(2,1)}, bf16[8,64,128]{2,1,0:T(8,128)(2,1)S(1)}, u32[]{:S(2)}, u32[]{:S(2)}) collective-permute-start(bf16[8,64,128]{2,1,0:T(8,128)(2,1)} %get-tuple-element.33), channel_id=1, source_target_pairs={{0,8},{4,12},{8,0},{12,4},{16,24},{20,28},{24,16},{28,20},{1,9},{5... | collective-permute-start | bytes 393224 | tf_op jit(solution)/shard_map/ppermute | solution.py:704
  205.0 3.0 %collective-permute-done.12 = bf16[8,64,128]{2,1,0:T(8,128)(2,1)S(1)} collective-permute-done((bf16[8,64,128]{2,1,0:T(8,128)(2,1)}, bf16[8,64,128]{2,1,0:T(8,128)(2,1)S(1)}, u32[]{:S(2)}, u32[]{:S(2)}) %collective-permute-start.12) | collective-permute-done | bytes 131104 | tf_op jit(solution)/shard_map/ppermute | solution.py:704
  208.0 4.0 %collective-permute-done.11 = bf16[8,64,128]{2,1,0:T(8,128)(2,1)S(1)} collective-permute-done((bf16[8,64,128]{2,1,0:T(8,128)(2,1)}, bf16[8,64,128]{2,1,0:T(8,128)(2,1)S(1)}, u32[]{:S(2)}, u32[]{:S(2)}) %collective-permute-start.11) | collective-permute-done | bytes 131104 | tf_op jit(solution)/shard_map/ppermute | solution.py:704
  212.0 0.2 collective-permute-done.10
  212.2 1.7 convert_add_fusion
  (16 shorter events, 0.1 us)
Async XLA Ops:
  4.0 112.4 %collective-permute-start.1 = (s16[25,264,128]{2,1,0:T(8,128)(2,1)}, s16[25,264,128]{2,1,0:T(8,128)(2,1)}, u32[]{:S(2)}, u32[]{:S(2)}) collective-permute-start(s16[25,264,128]{2,1,0:T(8,128)(2,1)} %get-tuple-element.20), channel_id=1, source_target_pairs={{0,1},{1,2},{2,3},{4,5},{5,6},{6,7},{8,9},{9,10},{10,11},{12,13},{... | collective-permute-start | bytes 5068808 | tf_op jit(solution)/shard_map/ppermute | solution.py:644
  7.6 112.8 %collective-permute-start.2 = (s16[25,264,128]{2,1,0:T(8,128)(2,1)}, s16[25,264,128]{2,1,0:T(8,128)(2,1)}, u32[]{:S(2)}, u32[]{:S(2)}) collective-permute-start(s16[25,264,128]{2,1,0:T(8,128)(2,1)} %get-tuple-element.21), channel_id=1, source_target_pairs={{1,0},{2,1},{3,2},{5,4},{6,5},{7,6},{9,8},{10,9},{11,10},{13,12},{... | collective-permute-start | bytes 5068808 | tf_op jit(solution)/shard_map/ppermute | solution.py:645
  12.3 77.1 %collective-permute-start.5 = (s16[17,264,128]{2,1,0:T(8,128)(2,1)}, s16[17,264,128]{2,1,0:T(8,128)(2,1)S(1)}, u32[]{:S(2)}, u32[]{:S(2)}) collective-permute-start(s16[17,264,128]{2,1,0:T(8,128)(2,1)} %pack_rows.6), channel_id=1, source_target_pairs={{0,16},{4,20},{8,24},{12,28},{16,0},{20,4},{24,8},{28,12},{1,17},{... | collective-permute-start | bytes 3446792 | tf_op jit(solution)/shard_map/ppermute | solution.py:633
  19.1 93.5 %collective-permute-start = (s16[16,264,128]{2,1,0:T(8,128)(2,1)}, s16[16,264,128]{2,1,0:T(8,128)(2,1)S(1)}, u32[]{:S(2)}, u32[]{:S(2)}) collective-permute-start(s16[16,264,128]{2,1,0:T(8,128)(2,1)} %pack_rows.4), channel_id=1, source_target_pairs={{0,16},{4,20},{8,24},{12,28},{16,0},{20,4},{24,8},{28,12},{1,17},{... | collective-permute-start | bytes 3244040 | tf_op jit(solution)/shard_map/ppermute | solution.py:653
  22.8 98.9 %copy-start.4 = (s32[8,2]{0,1:T(2,128)S(1)}, s32[8,2]{0,1:T(2,128)}, u32[]{:S(2)}) copy-start(s32[8,2]{0,1:T(2,128)} %param.22) | copy-start | bytes 196
  22.8 98.9 %copy-start.3 = (f32[8,7]{1,0:T(8,128)S(1)}, f32[8,7]{1,0:T(8,128)}, u32[]{:S(2)}) copy-start(f32[8,7]{1,0:T(8,128)} %param.19) | copy-start | bytes 676
  22.8 100.0 %copy-start.5 = (s32[8]{0:T(128)S(1)}, s32[8]{0:T(128)}, u32[]{:S(2)}) copy-start(s32[8]{0:T(128)} %param.21) | copy-start | bytes 100
  22.8 100.0 %copy-start.6 = (s32[8]{0:T(128)S(1)}, s32[8]{0:T(128)}, u32[]{:S(2)}) copy-start(s32[8]{0:T(128)} %param.20) | copy-start | bytes 100
  22.8 100.2 %copy-start.7 = (s32[4]{0:T(128)S(1)}, s32[4]{0:T(128)}, u32[]{:S(2)}) copy-start(s32[4]{0:T(128)} %param.23) | copy-start | bytes 52
  22.8 70.4 %collective-permute-start.8 = (s16[14,264,128]{2,1,0:T(8,128)(2,1)}, s16[14,264,128]{2,1,0:T(8,128)(2,1)S(1)}, u32[]{:S(2)}, u32[]{:S(2)}) collective-permute-start(s16[14,264,128]{2,1,0:T(8,128)(2,1)} %get-tuple-element.29), channel_id=1, source_target_pairs={{0,1},{1,2},{2,3},{4,5},{5,6},{6,7},{8,9},{9,10},{10,11},{12,13},{... | collective-permute-start | bytes 2838536 | tf_op jit(solution)/shard_map/ppermute | solution.py:644
  89.4 1.3 copy-start
  89.4 51.9 %collective-permute-start.9 = (s16[14,264,128]{2,1,0:T(8,128)(2,1)}, s16[14,264,128]{2,1,0:T(8,128)(2,1)}, u32[]{:S(2)}, u32[]{:S(2)}) collective-permute-start(s16[14,264,128]{2,1,0:T(8,128)(2,1)} %get-tuple-element.30), channel_id=1, source_target_pairs={{1,0},{2,1},{3,2},{5,4},{6,5},{7,6},{9,8},{10,9},{11,10},{13,12},{... | collective-permute-start | bytes 2838536 | tf_op jit(solution)/shard_map/ppermute | solution.py:645
  93.3 23.1 %copy-start.2 = (s16[14,264,128]{2,1,0:T(8,128)(2,1)}, s16[14,264,128]{2,1,0:T(8,128)(2,1)S(1)}, u32[]{:S(2)}) copy-start(s16[14,264,128]{2,1,0:T(8,128)(2,1)S(1)} %collective-permute-done.8.refs_7_) | copy-start | bytes 2838532
  93.3 69.6 %collective-permute-start.6 = (s16[14,264,128]{2,1,0:T(8,128)(2,1)}, s16[14,264,128]{2,1,0:T(8,128)(2,1)}, u32[]{:S(2)}, u32[]{:S(2)}) collective-permute-start(s16[14,264,128]{2,1,0:T(8,128)(2,1)} %get-tuple-element.26), channel_id=1, source_target_pairs={{0,1},{1,2},{2,3},{4,5},{5,6},{6,7},{8,9},{9,10},{10,11},{12,13},{... | collective-permute-start | bytes 2838536 | tf_op jit(solution)/shard_map/ppermute | solution.py:680
  112.6 1.3 copy-start.1
  112.6 50.4 %collective-permute-start.7 = (s16[14,264,128]{2,1,0:T(8,128)(2,1)}, s16[14,264,128]{2,1,0:T(8,128)(2,1)}, u32[]{:S(2)}, u32[]{:S(2)}) collective-permute-start(s16[14,264,128]{2,1,0:T(8,128)(2,1)} %get-tuple-element.27), channel_id=1, source_target_pairs={{1,0},{2,1},{3,2},{5,4},{6,5},{7,6},{9,8},{10,9},{11,10},{13,12},{... | collective-permute-start | bytes 2838536 | tf_op jit(solution)/shard_map/ppermute | solution.py:681
  116.4 66.8 %collective-permute-start.3 = (s16[13,264,128]{2,1,0:T(8,128)(2,1)}, s16[13,264,128]{2,1,0:T(8,128)(2,1)}, u32[]{:S(2)}, u32[]{:S(2)}) collective-permute-start(s16[13,264,128]{2,1,0:T(8,128)(2,1)} %get-tuple-element.24), channel_id=1, source_target_pairs={{0,1},{1,2},{2,3},{4,5},{5,6},{6,7},{8,9},{9,10},{10,11},{12,13},{... | collective-permute-start | bytes 2635784 | tf_op jit(solution)/shard_map/ppermute | solution.py:680
  120.4 62.9 %collective-permute-start.4 = (s16[13,264,128]{2,1,0:T(8,128)(2,1)}, s16[13,264,128]{2,1,0:T(8,128)(2,1)}, u32[]{:S(2)}, u32[]{:S(2)}) collective-permute-start(s16[13,264,128]{2,1,0:T(8,128)(2,1)} %get-tuple-element.25), channel_id=1, source_target_pairs={{1,0},{2,1},{3,2},{5,4},{6,5},{7,6},{9,8},{10,9},{11,10},{13,12},{... | collective-permute-start | bytes 2635784 | tf_op jit(solution)/shard_map/ppermute | solution.py:681
  200.5 7.6 %collective-permute-start.12 = (bf16[8,64,128]{2,1,0:T(8,128)(2,1)}, bf16[8,64,128]{2,1,0:T(8,128)(2,1)S(1)}, u32[]{:S(2)}, u32[]{:S(2)}) collective-permute-start(bf16[8,64,128]{2,1,0:T(8,128)(2,1)} %get-tuple-element.34), channel_id=1, source_target_pairs={{0,12},{4,0},{8,4},{12,8},{16,28},{20,16},{24,20},{28,24},{1,13},{... | collective-permute-start | bytes 393224 | tf_op jit(solution)/shard_map/ppermute | solution.py:704
  202.3 9.8 %collective-permute-start.11 = (bf16[8,64,128]{2,1,0:T(8,128)(2,1)}, bf16[8,64,128]{2,1,0:T(8,128)(2,1)S(1)}, u32[]{:S(2)}, u32[]{:S(2)}) collective-permute-start(bf16[8,64,128]{2,1,0:T(8,128)(2,1)} %get-tuple-element.33), channel_id=1, source_target_pairs={{0,8},{4,12},{8,0},{12,4},{16,24},{20,28},{24,16},{28,20},{1,9},{5... | collective-permute-start | bytes 393224 | tf_op jit(solution)/shard_map/ppermute | solution.py:704
  205.0 7.2 %collective-permute-start.10 = (bf16[8,64,128]{2,1,0:T(8,128)(2,1)}, bf16[8,64,128]{2,1,0:T(8,128)(2,1)S(1)}, u32[]{:S(2)}, u32[]{:S(2)}) collective-permute-start(bf16[8,64,128]{2,1,0:T(8,128)(2,1)} %get-tuple-element.32), channel_id=1, source_target_pairs={{0,4},{4,8},{8,12},{12,0},{16,20},{20,24},{24,28},{28,16},{1,5},{5... | collective-permute-start | bytes 393224 | tf_op jit(solution)/shard_map/ppermute | solution.py:704

commit v6 on v5

--- a/solution.py
+++ b/solution.py
@@ -138,6 +138,7 @@
     packed = not isinstance(field, tuple)
     fields = [field] if packed else list(field) + ([data] if backward else [])
     first_pass = model is None
+    stacks = kind in ("snaps", "waves")
     depths = (reach, near) + ((near, near) if first_pass else ()) + ((1,) if backward else ())
     inputs_m = [vel, ani] if first_pass else list(model)
     n_side = len(left)
@@ -228,6 +229,8 @@
                     pltpu.make_async_copy(field_refs[2], flat.at[pl.ds(0, n_data)], sem.at[14])
                 )
                 flat[n_data:, :] = jnp.zeros((LANES - n_data, all_rows), jnp.float32)
+        held = refs[pos + 11] if stacks else None
+        out_copies = []
         other_refs = refs[pos + 11 : pos + 11 + len(others)]
         other_copies = [
             pltpu.make_async_copy(source, target, sem.at[15 + n])
@@ -319,8 +322,8 @@
                         base = pl.multiple_of(PAD + skip + r0, 8)
                         at = pl.ds(r0, size)
                         value = buf[reach + x, pl.ds(base, size), :]
-                        if kind in ("snaps", "waves"):
-                            outs[0][slot, x, at, :] = value.astype(outs[0].dtype)
+                        if stacks:
+                            held[slot, x, at, :] = value.astype(held.dtype)
                         elif kind == "image":
                             u = other_refs[0][slot, x, at, :].astype(jnp.float32)
                             image[x, at, :] = image[x, at, :] + u * value
@@ -330,6 +333,12 @@
                     return carry
 
                 lax.fori_loop(0, width, body, 0)
+
+            done = time - 1 if backward else time - 1 - (reach + 1 - n_snaps)
+            if stacks and 0 <= done < n_snaps:
+                copy = pltpu.make_async_copy(held.at[done], outs[0].at[done], sem.at[21 + done])
+                copy.start()
+                out_copies.append(copy)
 
         src, dst = buf_a, buf_b
         coefs = (h_buf, v_buf)
@@ -367,7 +376,7 @@
             src, dst = dst, src
             record(src, reach + 1 - step if backward else step + 1)
 
-        for copy in model_copies + other_copies[:-1]:
+        for copy in model_copies + other_copies[:-1] + out_copies:
             copy.wait()
         if kind == "blocks":
             block = half_rows // blocks
@@ -408,15 +417,16 @@
         in_specs=[smem, smem]
         + [any_spec] * len(fields)
         + [any_spec] * (len(inputs_m) + 2 * n_side + len(others)),
-        out_specs=(vmem,) * (len(out_shape) - n_model) + (any_spec,) * n_model,
+        out_specs=(any_spec if stacks else vmem,) * (len(out_shape) - n_model) + (any_spec,) * n_model,
         scratch_shapes=[
             field_buf, field_buf, grid_buf, grid_buf, side, side,
             pltpu.VMEM((stage_layers, rows, depth_cells), WIRE),
             pltpu.VMEM((3, rows, depth_cells), jnp.float32),
             pltpu.VMEM((2 * LANES, LANES), jnp.bfloat16),
             pltpu.VMEM((2, rows, depth_cells), jnp.float32),
-            pltpu.SemaphoreType.DMA((21,)),
+            pltpu.SemaphoreType.DMA((21 + n_snaps,)),
         ]
+        + ([pltpu.VMEM(out_shape[0].shape, out_shape[0].dtype)] if stacks else [])
         + [pltpu.VMEM(other.shape, other.dtype) for other in others]
         + ([pltpu.VMEM(shape, jnp.float32)] if kind == "blocks" else [])
         + (

time: 215 us -> 214 us (level)
  no operation moved by 1% of the time
where the time goes in v6:
time: 214 us; the launch traced here: 213 us
  Pallas kernels  94.7 us (44%)
  waiting for transfers between devices  85.2 us (40%)
  starting transfers between devices  28.6 us (13%)
  other arithmetic  2.2 us (1%)
    pallas_call x4, Pallas kernels, wave_pass(): pl.pallas_call(kernel, out_shape=out_shape, in_specs=[smem, smem] + [any_...  75.4 us
    ppermute x1, waiting for transfers between devices, on_device(): import_w = lax.ppermute(send_w, 'shot', across)  63.5 us
    ppermute x1, waiting for transfers between devices, on_device(): import_u = lax.ppermute(send_u, 'shot', across)  14.5 us
    pallas_call x4, Pallas kernels, pack_rows(): pl.pallas_call(kernel, out_shape=tuple((jax.ShapeDtypeStruct((m, rows, de...  14.3 us
    ppermute x2, starting transfers between devices, from_sides(): from_left = lax.ppermute(send_up, 'xy', up)  8.71 us
    ppermute x3, waiting for transfers between devices, on_device(): arrived = lax.ppermute(blocks[d], 'shot', route)  7.15 us
    ppermute x2, starting transfers between devices, sides(): from_left = lax.ppermute(send_up, 'xy', up)  6.67 us
    pallas_call x2, Pallas kernels, repack(): pl.pallas_call(kernel, out_shape=tuple((jax.ShapeDtypeStruct((m,) + packe...  5.06 us
  transfers between devices with their start and end apart: 13, of which 5 were waited for; matrix products, arithmetic and copies ran while one was open for 1% of the time, Pallas kernels for 35%

profile of v6, /device:TPU:0, one launch (start us, length us, event | category | flops | bytes accessed | tf_op | source)
XLA Modules:
  0.0 212.6 jit_solution(10708403282785268884)
XLA Ops:
  0.0 3.9 %pack_rows.5 = (s16[25,264,128]{2,1,0:T(8,128)(2,1)}, s16[25,264,128]{2,1,0:T(8,128)(2,1)}) custom-call(s32[1]{0:T(128)} %bitcast.first_ref, f32[8,512,128]{2,1,0:T(8,128)} %bitcast.17, f32[8,512,128]{2,1,0:T(8,128)} %bitcast.20, f32[8,512,128]{2,1,0:T(8,128)} %refs_4_.1, f32[8,512,128]{2,1,0:T(8,128)} %refs_5_.1), custom_call_target="tpu_custom_call" | custom-call | flops 1081344 | bytes 8650752 | tf_op jit(solution)/shard_map/pack_rows/pallas_call | solution.py:550
  4.0 3.6 %collective-permute-start.1 = (s16[25,264,128]{2,1,0:T(8,128)(2,1)}, s16[25,264,128]{2,1,0:T(8,128)(2,1)}, u32[]{:S(2)}, u32[]{:S(2)}) collective-permute-start(s16[25,264,128]{2,1,0:T(8,128)(2,1)} %get-tuple-element.20), channel_id=1, source_target_pairs={{0,1},{1,2},{2,3},{4,5},{5,6},{6,7},{8,9},{9,10},{10,11},{12,13},{... | collective-permute-start | bytes 5068808 | tf_op jit(solution)/shard_map/ppermute | solution.py:654
  7.6 1.3 collective-permute-start.2
  8.9 3.5 %pack_rows.6 = s16[17,264,128]{2,1,0:T(8,128)(2,1)} custom-call(s32[1]{0:T(128)} %bitcast.5.first_ref, f32[8,512,128]{2,1,0:T(8,128)} %bitcast.11, f32[8,512,128]{2,1,0:T(8,128)} %bitcast.14, f32[56,512]{1,0:T(8,128)} %bitcast.23), custom_call_target="tpu_custom_call" | custom-call | flops 540672 | bytes 4325376 | tf_op jit(solution)/shard_map/pack_rows/pallas_call | solution.py:550
  12.3 3.5 %collective-permute-start.5 = (s16[17,264,128]{2,1,0:T(8,128)(2,1)}, s16[17,264,128]{2,1,0:T(8,128)(2,1)S(1)}, u32[]{:S(2)}, u32[]{:S(2)}) collective-permute-start(s16[17,264,128]{2,1,0:T(8,128)(2,1)} %pack_rows.6), channel_id=1, source_target_pairs={{0,16},{4,20},{8,24},{12,28},{16,0},{20,4},{24,8},{28,12},{1,17},{... | collective-permute-start | bytes 3446792 | tf_op jit(solution)/shard_map/ppermute | solution.py:643
  15.8 3.2 %pack_rows.4 = s16[16,264,128]{2,1,0:T(8,128)(2,1)} custom-call(s32[1]{0:T(128)} %bitcast.5.first_ref, f32[8,512,128]{2,1,0:T(8,128)} %bitcast.18, f32[8,512,128]{2,1,0:T(8,128)} %bitcast.21), custom_call_target="tpu_custom_call" | custom-call | flops 540672 | bytes 4325376 | tf_op jit(solution)/shard_map/pack_rows/pallas_call | solution.py:550
  19.1 0.1 collective-permute-start
  19.1 3.6 %pack_rows.7 = (s16[14,264,128]{2,1,0:T(8,128)(2,1)}, s16[14,264,128]{2,1,0:T(8,128)(2,1)}) custom-call(s32[1]{0:T(128)} %bitcast.first_ref, f32[8,512,128]{2,1,0:T(8,128)} %bitcast.12, f32[8,512,128]{2,1,0:T(8,128)} %bitcast.15, f32[56,512]{1,0:T(8,128)} %bitcast.24), custom_call_target="tpu_custom_call" | custom-call | flops 540672 | bytes 4325376 | tf_op jit(solution)/shard_map/pack_rows/pallas_call | solution.py:550
  22.8 0.0 copy-start.4
  22.8 0.0 copy-start.3
  22.8 0.0 copy-start.5
  22.8 0.0 copy-start.6
  22.8 0.0 copy-start.7
  22.8 3.1 %collective-permute-start.8 = (s16[14,264,128]{2,1,0:T(8,128)(2,1)}, s16[14,264,128]{2,1,0:T(8,128)(2,1)S(1)}, u32[]{:S(2)}, u32[]{:S(2)}) collective-permute-start(s16[14,264,128]{2,1,0:T(8,128)(2,1)} %get-tuple-element.29), channel_id=1, source_target_pairs={{0,1},{1,2},{2,3},{4,5},{5,6},{6,7},{8,9},{9,10},{10,11},{12,13},{... | collective-permute-start | bytes 2838536 | tf_op jit(solution)/shard_map/ppermute | solution.py:654
  25.9 63.5 %collective-permute-done.5.packed_ref.refs_2_ = s16[17,264,128]{2,1,0:T(8,128)(2,1)S(1)} collective-permute-done((s16[17,264,128]{2,1,0:T(8,128)(2,1)}, s16[17,264,128]{2,1,0:T(8,128)(2,1)S(1)}, u32[]{:S(2)}, u32[]{:S(2)}) %collective-permute-start.5) | collective-permute-done | bytes 1148960 | tf_op jit(solution)/shard_map/ppermute | solution.py:643
  89.4 1.3 collective-permute-start.9
  90.7 2.6 %repack.3 = (s16[14,264,128]{2,1,0:T(8,128)(2,1)}, s16[14,264,128]{2,1,0:T(8,128)(2,1)}) custom-call(s16[17,264,128]{2,1,0:T(8,128)(2,1)} %copy-done), custom_call_target="tpu_custom_call" | custom-call | bytes 3446784 | tf_op jit(solution)/shard_map/repack/pallas_call | solution.py:586
  93.3 0.0 collective-permute-done.8.refs_7_
  93.3 4.7 %collective-permute-start.6 = (s16[14,264,128]{2,1,0:T(8,128)(2,1)}, s16[14,264,128]{2,1,0:T(8,128)(2,1)}, u32[]{:S(2)}, u32[]{:S(2)}) collective-permute-start(s16[14,264,128]{2,1,0:T(8,128)(2,1)} %get-tuple-element.26), channel_id=1, source_target_pairs={{0,1},{1,2},{2,3},{4,5},{5,6},{6,7},{8,9},{9,10},{10,11},{12,13},{... | collective-permute-start | bytes 2838536 | tf_op jit(solution)/shard_map/ppermute | solution.py:690
  98.0 14.5 %collective-permute-done.packed_ref.refs_2_ = s16[16,264,128]{2,1,0:T(8,128)(2,1)S(1)} collective-permute-done((s16[16,264,128]{2,1,0:T(8,128)(2,1)}, s16[16,264,128]{2,1,0:T(8,128)(2,1)S(1)}, u32[]{:S(2)}, u32[]{:S(2)}) %collective-permute-start) | collective-permute-done | bytes 1081376 | tf_op jit(solution)/shard_map/ppermute | solution.py:663
  112.6 1.3 collective-permute-start.7
  113.9 2.5 %repack.2 = (s16[13,264,128]{2,1,0:T(8,128)(2,1)}, s16[13,264,128]{2,1,0:T(8,128)(2,1)}) custom-call(s16[16,264,128]{2,1,0:T(8,128)(2,1)} %copy-done.1), custom_call_target="tpu_custom_call" | custom-call | bytes 3244032 | tf_op jit(solution)/shard_map/repack/pallas_call | solution.py:586
  116.4 0.0 collective-permute-done.1.refs_6_
  116.4 4.0 %collective-permute-start.3 = (s16[13,264,128]{2,1,0:T(8,128)(2,1)}, s16[13,264,128]{2,1,0:T(8,128)(2,1)}, u32[]{:S(2)}, u32[]{:S(2)}) collective-permute-start(s16[13,264,128]{2,1,0:T(8,128)(2,1)} %get-tuple-element.24), channel_id=1, source_target_pairs={{0,1},{1,2},{2,3},{4,5},{5,6},{6,7},{8,9},{9,10},{10,11},{12,13},{... | collective-permute-start | bytes 2635784 | tf_op jit(solution)/shard_map/ppermute | solution.py:690
  120.4 0.0 collective-permute-done.2.refs_7_
  120.4 1.3 collective-permute-start.4
  121.7 0.1 copy.13
  121.8 0.1 pad_add_fusion
  121.9 0.1 convert_compare_fusion
  122.0 0.1 select_reduce_fusion
  122.0 0.1 copy.14
  122.1 0.7 reshape.38.refs_1_
  122.8 0.2 select_reduce_fusion.1
  123.0 0.6 concatenate.3.refs_0_
  123.6 17.2 %shard_map.118 = (bf16[4,8,256,128]{3,2,1,0:T(8,128)(2,1)}, f32[22,264,128]{2,1,0:T(8,128)}, f32[22,264,128]{2,1,0:T(8,128)}) custom-call(s32[13]{0:T(128)} %concatenate.3.refs_0_, f32[14]{0:T(128)} %reshape.38.refs_1_, f32[8,512,128]{2,1,0:T(8,128)} %bitcast.19, f32[8,512,128]{2,1,0:T(8,128)} %bitcast.22, f32[8,512,128]{2,1,0:T(8,128)} %refs_4_.1, ...), custom_call_target="tpu_custom_call" | custom-call | flops 78059520 | bytes 14868480 | tf_op jit(solution)/shard_map/pallas_call | solution.py:414
  140.9 0.0 collective-permute-done.9.refs_8_
  140.9 20.6 %shard_map.120.refs_8_ = f32[4,8,256,128]{3,2,1,0:T(8,128)} custom-call(s32[13]{0:T(128)} %concatenate.3.refs_0_, f32[14]{0:T(128)} %reshape.38.refs_1_, f32[8,512,128]{2,1,0:T(8,128)} %bitcast.13, f32[8,512,128]{2,1,0:T(8,128)} %bitcast.16, f32[56,512]{1,0:T(8,128)} %bitcast.25, f32[22,264,128]{2,1,0:T(8,128)} %get-tuple-element.22.refs_3_.refs_5_, ...), custom_call_target="tpu_custom_call" | custom-call | flops 78059520 | bytes 14868480 | tf_op jit(solution)/shard_map/pallas_call | solution.py:414
  161.5 0.0 collective-permute-done.7.refs_6_
  161.5 20.3 %shard_map.119.refs_7_ = f32[8,256,128]{2,1,0:T(8,128)} custom-call(s32[13]{0:T(128)} %concatenate.3.refs_0_, f32[14]{0:T(128)} %reshape.38.refs_1_, s16[17,264,128]{2,1,0:T(8,128)(2,1)} %copy-done, f32[22,264,128]{2,1,0:T(8,128)} %get-tuple-element.22.refs_3_.refs_5_, f32[22,264,128]{2,1,0:T(8,128)} %get-tuple-element.23.refs_4_.refs_6_, ...), custom_call_target="tpu_custom_call" | custom-call | flops 78059520 | bytes 14868480 | tf_op jit(solution)/shard_map/pallas_call | solution.py:414
  181.9 0.0 collective-permute-done.3.refs_5_
  181.9 17.3 %shard_map.121 = (f32[8,64,128]{2,1,0:T(8,128)}, bf16[8,64,128]{2,1,0:T(8,128)(2,1)}, bf16[8,64,128]{2,1,0:T(8,128)(2,1)}, bf16[8,64,128]{2,1,0:T(8,128)(2,1)}) custom-call(s32[13]{0:T(128)} %concatenate.3.refs_0_, f32[14]{0:T(128)} %reshape.38.refs_1_, s16[16,264,128]{2,1,0:T(8,128)(2,1)} %copy-done.1, f32[22,264,128]{2,1,0:T(8,128)} %get-tuple-element.22.refs_3_.refs_5_, ...), custom_call_target="tpu_custom_call" | custom-call | flops 78059520 | bytes 14868480 | tf_op jit(solution)/shard_map/pallas_call | solution.py:414
  199.1 1.8 collective-permute-start.12
  200.9 2.8 %collective-permute-start.11 = (bf16[8,64,128]{2,1,0:T(8,128)(2,1)}, bf16[8,64,128]{2,1,0:T(8,128)(2,1)S(1)}, u32[]{:S(2)}, u32[]{:S(2)}) collective-permute-start(bf16[8,64,128]{2,1,0:T(8,128)(2,1)} %get-tuple-element.33), channel_id=1, source_target_pairs={{0,8},{4,12},{8,0},{12,4},{16,24},{20,28},{24,16},{28,20},{1,9},{5... | collective-permute-start | bytes 393224 | tf_op jit(solution)/shard_map/ppermute | solution.py:714
  203.7 0.0 collective-permute-start.10
  203.7 3.0 %collective-permute-done.12 = bf16[8,64,128]{2,1,0:T(8,128)(2,1)S(1)} collective-permute-done((bf16[8,64,128]{2,1,0:T(8,128)(2,1)}, bf16[8,64,128]{2,1,0:T(8,128)(2,1)S(1)}, u32[]{:S(2)}, u32[]{:S(2)}) %collective-permute-start.12) | collective-permute-done | bytes 131104 | tf_op jit(solution)/shard_map/ppermute | solution.py:714
  206.7 4.0 %collective-permute-done.11 = bf16[8,64,128]{2,1,0:T(8,128)(2,1)S(1)} collective-permute-done((bf16[8,64,128]{2,1,0:T(8,128)(2,1)}, bf16[8,64,128]{2,1,0:T(8,128)(2,1)S(1)}, u32[]{:S(2)}, u32[]{:S(2)}) %collective-permute-start.11) | collective-permute-done | bytes 131104 | tf_op jit(solution)/shard_map/ppermute | solution.py:714
  210.7 0.2 collective-permute-done.10
  210.9 1.7 convert_add_fusion
  (16 shorter events, 0.1 us)
Async XLA Ops:
  4.0 112.4 %collective-permute-start.1 = (s16[25,264,128]{2,1,0:T(8,128)(2,1)}, s16[25,264,128]{2,1,0:T(8,128)(2,1)}, u32[]{:S(2)}, u32[]{:S(2)}) collective-permute-start(s16[25,264,128]{2,1,0:T(8,128)(2,1)} %get-tuple-element.20), channel_id=1, source_target_pairs={{0,1},{1,2},{2,3},{4,5},{5,6},{6,7},{8,9},{9,10},{10,11},{12,13},{... | collective-permute-start | bytes 5068808 | tf_op jit(solution)/shard_map/ppermute | solution.py:654
  7.6 112.8 %collective-permute-start.2 = (s16[25,264,128]{2,1,0:T(8,128)(2,1)}, s16[25,264,128]{2,1,0:T(8,128)(2,1)}, u32[]{:S(2)}, u32[]{:S(2)}) collective-permute-start(s16[25,264,128]{2,1,0:T(8,128)(2,1)} %get-tuple-element.21), channel_id=1, source_target_pairs={{1,0},{2,1},{3,2},{5,4},{6,5},{7,6},{9,8},{10,9},{11,10},{13,12},{... | collective-permute-start | bytes 5068808 | tf_op jit(solution)/shard_map/ppermute | solution.py:655
  12.3 77.1 %collective-permute-start.5 = (s16[17,264,128]{2,1,0:T(8,128)(2,1)}, s16[17,264,128]{2,1,0:T(8,128)(2,1)S(1)}, u32[]{:S(2)}, u32[]{:S(2)}) collective-permute-start(s16[17,264,128]{2,1,0:T(8,128)(2,1)} %pack_rows.6), channel_id=1, source_target_pairs={{0,16},{4,20},{8,24},{12,28},{16,0},{20,4},{24,8},{28,12},{1,17},{... | collective-permute-start | bytes 3446792 | tf_op jit(solution)/shard_map/ppermute | solution.py:643
  19.1 93.5 %collective-permute-start = (s16[16,264,128]{2,1,0:T(8,128)(2,1)}, s16[16,264,128]{2,1,0:T(8,128)(2,1)S(1)}, u32[]{:S(2)}, u32[]{:S(2)}) collective-permute-start(s16[16,264,128]{2,1,0:T(8,128)(2,1)} %pack_rows.4), channel_id=1, source_target_pairs={{0,16},{4,20},{8,24},{12,28},{16,0},{20,4},{24,8},{28,12},{1,17},{... | collective-permute-start | bytes 3244040 | tf_op jit(solution)/shard_map/ppermute | solution.py:663
  22.8 98.9 %copy-start.4 = (s32[8,2]{0,1:T(2,128)S(1)}, s32[8,2]{0,1:T(2,128)}, u32[]{:S(2)}) copy-start(s32[8,2]{0,1:T(2,128)} %param.22) | copy-start | bytes 196
  22.8 98.9 %copy-start.3 = (f32[8,7]{1,0:T(8,128)S(1)}, f32[8,7]{1,0:T(8,128)}, u32[]{:S(2)}) copy-start(f32[8,7]{1,0:T(8,128)} %param.19) | copy-start | bytes 676
  22.8 100.0 %copy-start.5 = (s32[8]{0:T(128)S(1)}, s32[8]{0:T(128)}, u32[]{:S(2)}) copy-start(s32[8]{0:T(128)} %param.21) | copy-start | bytes 100
  22.8 100.0 %copy-start.6 = (s32[8]{0:T(128)S(1)}, s32[8]{0:T(128)}, u32[]{:S(2)}) copy-start(s32[8]{0:T(128)} %param.20) | copy-start | bytes 100
  22.8 100.2 %copy-start.7 = (s32[4]{0:T(128)S(1)}, s32[4]{0:T(128)}, u32[]{:S(2)}) copy-start(s32[4]{0:T(128)} %param.23) | copy-start | bytes 52
  22.8 70.4 %collective-permute-start.8 = (s16[14,264,128]{2,1,0:T(8,128)(2,1)}, s16[14,264,128]{2,1,0:T(8,128)(2,1)S(1)}, u32[]{:S(2)}, u32[]{:S(2)}) collective-permute-start(s16[14,264,128]{2,1,0:T(8,128)(2,1)} %get-tuple-element.29), channel_id=1, source_target_pairs={{0,1},{1,2},{2,3},{4,5},{5,6},{6,7},{8,9},{9,10},{10,11},{12,13},{... | collective-permute-start | bytes 2838536 | tf_op jit(solution)/shard_map/ppermute | solution.py:654
  89.4 1.3 copy-start
  89.4 51.5 %collective-permute-start.9 = (s16[14,264,128]{2,1,0:T(8,128)(2,1)}, s16[14,264,128]{2,1,0:T(8,128)(2,1)}, u32[]{:S(2)}, u32[]{:S(2)}) collective-permute-start(s16[14,264,128]{2,1,0:T(8,128)(2,1)} %get-tuple-element.30), channel_id=1, source_target_pairs={{1,0},{2,1},{3,2},{5,4},{6,5},{7,6},{9,8},{10,9},{11,10},{13,12},{... | collective-permute-start | bytes 2838536 | tf_op jit(solution)/shard_map/ppermute | solution.py:655
  93.3 23.1 %copy-start.2 = (s16[14,264,128]{2,1,0:T(8,128)(2,1)}, s16[14,264,128]{2,1,0:T(8,128)(2,1)S(1)}, u32[]{:S(2)}) copy-start(s16[14,264,128]{2,1,0:T(8,128)(2,1)S(1)} %collective-permute-done.8.refs_7_) | copy-start | bytes 2838532
  93.3 68.2 %collective-permute-start.6 = (s16[14,264,128]{2,1,0:T(8,128)(2,1)}, s16[14,264,128]{2,1,0:T(8,128)(2,1)}, u32[]{:S(2)}, u32[]{:S(2)}) collective-permute-start(s16[14,264,128]{2,1,0:T(8,128)(2,1)} %get-tuple-element.26), channel_id=1, source_target_pairs={{0,1},{1,2},{2,3},{4,5},{5,6},{6,7},{8,9},{9,10},{10,11},{12,13},{... | collective-permute-start | bytes 2838536 | tf_op jit(solution)/shard_map/ppermute | solution.py:690
  112.6 1.3 copy-start.1
  112.6 49.0 %collective-permute-start.7 = (s16[14,264,128]{2,1,0:T(8,128)(2,1)}, s16[14,264,128]{2,1,0:T(8,128)(2,1)}, u32[]{:S(2)}, u32[]{:S(2)}) collective-permute-start(s16[14,264,128]{2,1,0:T(8,128)(2,1)} %get-tuple-element.27), channel_id=1, source_target_pairs={{1,0},{2,1},{3,2},{5,4},{6,5},{7,6},{9,8},{10,9},{11,10},{13,12},{... | collective-permute-start | bytes 2838536 | tf_op jit(solution)/shard_map/ppermute | solution.py:691
  116.4 65.4 %collective-permute-start.3 = (s16[13,264,128]{2,1,0:T(8,128)(2,1)}, s16[13,264,128]{2,1,0:T(8,128)(2,1)}, u32[]{:S(2)}, u32[]{:S(2)}) collective-permute-start(s16[13,264,128]{2,1,0:T(8,128)(2,1)} %get-tuple-element.24), channel_id=1, source_target_pairs={{0,1},{1,2},{2,3},{4,5},{5,6},{6,7},{8,9},{9,10},{10,11},{12,13},{... | collective-permute-start | bytes 2635784 | tf_op jit(solution)/shard_map/ppermute | solution.py:690
  120.4 61.5 %collective-permute-start.4 = (s16[13,264,128]{2,1,0:T(8,128)(2,1)}, s16[13,264,128]{2,1,0:T(8,128)(2,1)}, u32[]{:S(2)}, u32[]{:S(2)}) collective-permute-start(s16[13,264,128]{2,1,0:T(8,128)(2,1)} %get-tuple-element.25), channel_id=1, source_target_pairs={{1,0},{2,1},{3,2},{5,4},{6,5},{7,6},{9,8},{10,9},{11,10},{13,12},{... | collective-permute-start | bytes 2635784 | tf_op jit(solution)/shard_map/ppermute | solution.py:691
  199.1 7.6 %collective-permute-start.12 = (bf16[8,64,128]{2,1,0:T(8,128)(2,1)}, bf16[8,64,128]{2,1,0:T(8,128)(2,1)S(1)}, u32[]{:S(2)}, u32[]{:S(2)}) collective-permute-start(bf16[8,64,128]{2,1,0:T(8,128)(2,1)} %get-tuple-element.34), channel_id=1, source_target_pairs={{0,12},{4,0},{8,4},{12,8},{16,28},{20,16},{24,20},{28,24},{1,13},{... | collective-permute-start | bytes 393224 | tf_op jit(solution)/shard_map/ppermute | solution.py:714
  200.9 9.8 %collective-permute-start.11 = (bf16[8,64,128]{2,1,0:T(8,128)(2,1)}, bf16[8,64,128]{2,1,0:T(8,128)(2,1)S(1)}, u32[]{:S(2)}, u32[]{:S(2)}) collective-permute-start(bf16[8,64,128]{2,1,0:T(8,128)(2,1)} %get-tuple-element.33), channel_id=1, source_target_pairs={{0,8},{4,12},{8,0},{12,4},{16,24},{20,28},{24,16},{28,20},{1,9},{5... | collective-permute-start | bytes 393224 | tf_op jit(solution)/shard_map/ppermute | solution.py:714
  203.7 7.2 %collective-permute-start.10 = (bf16[8,64,128]{2,1,0:T(8,128)(2,1)}, bf16[8,64,128]{2,1,0:T(8,128)(2,1)S(1)}, u32[]{:S(2)}, u32[]{:S(2)}) collective-permute-start(bf16[8,64,128]{2,1,0:T(8,128)(2,1)} %get-tuple-element.32), channel_id=1, source_target_pairs={{0,4},{4,8},{8,12},{12,0},{16,20},{20,24},{24,28},{28,16},{1,5},{5... | collective-permute-start | bytes 393224 | tf_op jit(solution)/shard_map/ppermute | solution.py:714
